TPU v7x, 32 devices: a whole 2x2x4 slice. The times are simulated.
32 devices in a mesh: dp: 8 (over z, y), tensor: 4 (over x, core).
Axes of the slice: x: 2, y: 2, z: 4, core: 2. Of those that a mesh axis runs over, the one named last changes fastest.
Arguments:
- block_input: bfloat16 [2048, 8, 768], P('tensor', 'dp'), may hold values from -6 to 6
- condition: bfloat16 [8, 128], P('dp'), may hold values from -6 to 6
- modulation_weight: bfloat16 [128, 4608], P(None, 'dp'), may hold values from -0.25 to 0.25
- modulation_bias: bfloat16 [4608], P('dp'), may hold values from -3 to 3
- first_gain: bfloat16 [768], P('dp'), may hold values from 0.5 to 1.5
- qkv_weight: bfloat16 [3, 768, 768], P(None, 'dp', 'tensor'), may hold values from -0.3125 to 0.3125
- out_weight: bfloat16 [768, 768], P('tensor', 'dp'), may hold values from -0.875 to 0.875
- second_gain: bfloat16 [768], P('dp'), may hold values from 0.5 to 1.5
- up_weight: bfloat16 [768, 3072], P('dp', 'tensor'), may hold values from -0.21875 to 0.21875
- up_bias: bfloat16 [3072], P('dp'), may hold values from -3 to 3
- down_weight: bfloat16 [3072, 768], P('tensor', 'dp'), may hold values from -0.109375 to 0.109375
- down_bias: bfloat16 [768], P('dp'), may hold values from -2 to 2
- grad_output: bfloat16 [2048, 8, 768], P('tensor', 'dp'), may hold values from -6 to 6
Outputs:
- block_output: bfloat16 [2048, 8, 768], P('tensor', 'dp')
- grad_input: float32 [2048, 8, 768], P('tensor', 'dp')
- grad_condition: float32 [8, 128], P('dp')
- grad_modulation_weight: float32 [128, 4608], replicated
- grad_modulation_bias: float32 [4608], replicated
- grad_first_gain: float32 [768], replicated
- grad_qkv_weight: float32 [3, 768, 768], P(None, 'dp', 'tensor')
- grad_out_weight: float32 [768, 768], P('tensor', 'dp')
- grad_second_gain: float32 [768], replicated
- grad_up_weight: float32 [768, 3072], P('dp', 'tensor')
- grad_up_bias: float32 [3072], replicated
- grad_down_weight: float32 [3072, 768], P('tensor', 'dp')
- grad_down_bias: float32 [768], replicated
- root_means: float32 [3], replicated
All inputs are finite; a program needn't handle non-finite values.
Results may differ from a plain program's by a relative error of at most 0.014.
The roundings to bfloat16 on the way count: a program that leaves them out, or rounds other values in their place, can miss the bound.
Values may be sent and summed in bfloat16 or wider, within the bound.
A program may use at most 128 MiB of HBM per device.

v0:
```python
from functools import partial

import jax
import jax.numpy as jnp
from jax import lax
from jax.sharding import PartitionSpec as P

HEAD_DIM = 64


PRECISE = lax.Precision.HIGHEST
EPSILON = 1e-05


def norm_mod(stream, gain_vec, shift_vec, scale_vec):
    row_mean = jnp.mean(stream, axis=-1, keepdims=True)
    centred = stream - row_mean
    variance = jnp.mean(centred * centred, axis=-1, keepdims=True)
    normed = centred * lax.rsqrt(variance + EPSILON) * gain_vec
    return normed * (1.0 + scale_vec) + shift_vec


def rotary_tables(length, head_width):
    half_dim = head_width // 2
    inverse = 1.0 / 10000.0 ** (jnp.arange(half_dim, dtype=jnp.float32) * 2.0 / head_width)
    angles = jnp.arange(length, dtype=jnp.float32)[:, None] * inverse[None, :]
    angles = jnp.concatenate([angles, angles], axis=-1)
    return (jnp.cos(angles), jnp.sin(angles))


def rotate(vector, cos_table, sine_table):
    half_dim = vector.shape[-1] // 2
    turned = jnp.concatenate([-vector[..., half_dim:], vector[..., :half_dim]], axis=-1)
    return vector * cos_table[:, None, None, :] + turned * sine_table[:, None, None, :]


def gelu_tanh(values):
    return jax.nn.gelu(values, approximate=True)


def seq_block(heads_all, sequence, offset, block_rows):
    whole_seq = lax.dynamic_index_in_dim(heads_all, sequence, 0, keepdims=False)
    return lax.dynamic_slice_in_dim(whole_seq, offset, block_rows, 1)


def blocks_to_rows(blocks, sequences, per_seq, length):
    heads_here, block_rows, head_width = (blocks.shape[1], blocks.shape[2], blocks.shape[3])
    arranged = blocks.reshape(sequences, per_seq, heads_here, block_rows, head_width).transpose(
        1, 3, 0, 2, 4
    )
    return arranged.reshape(length, sequences, heads_here, head_width)


def shards(
    block_input,
    condition,
    modulation_weight,
    modulation_bias,
    first_gain,
    qkv_weight,
    out_weight,
    second_gain,
    up_weight,
    up_bias,
    down_weight,
    down_bias,
    grad_output,
):
    n_tensor = lax.axis_size("tensor")
    n_data = lax.axis_size("dp")
    t_index = lax.axis_index("tensor")
    d_index = lax.axis_index("dp")
    local_rows, sequences, features = block_input.shape
    length = local_rows * n_tensor
    ada_full, ada_b_full, gain_one, qkv_w, out_w, gain_two, up_w, b_up_full, down_w, b_down_full = (
        lax.all_gather(modulation_weight, "dp", axis=1, tiled=True),
        lax.all_gather(modulation_bias, "dp", axis=0, tiled=True),
        lax.all_gather(first_gain, "dp", axis=0, tiled=True),
        lax.all_gather(qkv_weight, "dp", axis=1, tiled=True),
        lax.all_gather(out_weight, "dp", axis=1, tiled=True),
        lax.all_gather(second_gain, "dp", axis=0, tiled=True),
        lax.all_gather(up_weight, "dp", axis=0, tiled=True),
        lax.all_gather(up_bias, "dp", axis=0, tiled=True),
        lax.all_gather(down_weight, "dp", axis=1, tiled=True),
        lax.all_gather(down_bias, "dp", axis=0, tiled=True),
    )
    ada_float = ada_full.astype(jnp.float32)
    gain_one_f = gain_one.astype(jnp.float32)
    gain_two_f = gain_two.astype(jnp.float32)
    b_up_f = b_up_full.astype(jnp.float32)
    b_down_f = b_down_full.astype(jnp.float32)
    cond_float = condition.astype(jnp.float32)
    modulation = jnp.dot(cond_float, ada_float, precision=PRECISE) + ada_b_full.astype(jnp.float32)
    shift_attn, scale_attn, gate_attn, shift_mlp, scale_mlp, gate_mlp = jnp.split(
        modulation, 6, axis=-1
    )
    stream = block_input.astype(jnp.float32)
    attn_in = norm_mod(stream, gain_one_f, shift_attn, scale_attn).astype(jnp.bfloat16)
    full_attn_in = lax.all_gather(attn_in, "tensor", axis=0, tiled=True)
    projected = jnp.einsum("lbd,jde->lbje", full_attn_in, qkv_w, preferred_element_type=jnp.float32)
    heads_here = qkv_w.shape[2] // HEAD_DIM
    head_shape = (length, sequences, heads_here, HEAD_DIM)
    cos_table, sine_table = rotary_tables(length, HEAD_DIM)
    query_scale = HEAD_DIM ** (-0.5)
    query_pre = projected[:, :, 0].reshape(head_shape)
    key_pre = projected[:, :, 1].reshape(head_shape)
    query_rot = (rotate(query_pre, cos_table, sine_table) * query_scale).astype(jnp.bfloat16)
    key_rot = rotate(key_pre, cos_table, sine_table).astype(jnp.bfloat16)
    value_low = projected[:, :, 2].reshape(head_shape).astype(jnp.bfloat16)
    query_heads = query_rot.transpose(1, 2, 0, 3)
    key_heads = key_rot.transpose(1, 2, 0, 3)
    value_heads = value_low.transpose(1, 2, 0, 3)
    block_rows = min(512, length)
    per_seq = length // block_rows
    block_count = sequences * per_seq

    def forward_block(position):
        sequence = position // per_seq
        offset = position % per_seq * block_rows
        query_blk = seq_block(query_heads, sequence, offset, block_rows)
        key_seq = lax.dynamic_index_in_dim(key_heads, sequence, 0, keepdims=False)
        value_seq = lax.dynamic_index_in_dim(value_heads, sequence, 0, keepdims=False)
        scores = jnp.einsum("hqe,hke->hqk", query_blk, key_seq, preferred_element_type=jnp.float32)
        row_max = jnp.max(scores, axis=-1, keepdims=True)
        shifted = jnp.exp(scores - row_max)
        row_total = jnp.sum(shifted, axis=-1, keepdims=True)
        probs = (shifted / row_total).astype(jnp.bfloat16)
        mixed_blk = jnp.einsum("hqk,hke->hqe", probs, value_seq, preferred_element_type=jnp.float32)
        return (mixed_blk.astype(jnp.bfloat16), (row_max + jnp.log(row_total))[..., 0])

    mixed_blocks, log_total = lax.map(forward_block, jnp.arange(block_count))
    mixed_all = blocks_to_rows(mixed_blocks, sequences, per_seq, length).reshape(
        length, sequences, heads_here * HEAD_DIM
    )
    portion = mixed_all
    attn_out = lax.psum_scatter(
        jnp.einsum("lbe,ed->lbd", portion, out_w, preferred_element_type=jnp.float32),
        "tensor",
        scatter_dimension=0,
        tiled=True,
    )
    attn_branch = gate_attn * attn_out
    middle = stream + attn_branch
    mlp_in = norm_mod(middle, gain_two_f, shift_mlp, scale_mlp).astype(jnp.bfloat16)
    unit_count = up_w.shape[1]
    b_up_own = lax.dynamic_slice_in_dim(b_up_f, t_index * unit_count, unit_count, 0)
    full_mlp_in = lax.all_gather(mlp_in, "tensor", axis=0, tiled=True)
    hidden = (
        jnp.einsum("lbd,df->lbf", full_mlp_in, up_w, preferred_element_type=jnp.float32) + b_up_own
    )
    active = gelu_tanh(hidden).astype(jnp.bfloat16)
    portion = active
    mlp_out = (
        lax.psum_scatter(
            jnp.einsum("lbf,fd->lbd", portion, down_w, preferred_element_type=jnp.float32).astype(
                jnp.bfloat16
            ),
            "tensor",
            scatter_dimension=0,
            tiled=True,
        ).astype(jnp.float32)
        + b_down_f
    )
    mlp_branch = gate_mlp * mlp_out
    result = middle + mlp_branch
    local_squares = jnp.stack(
        [
            jnp.sum(attn_branch * attn_branch),
            jnp.sum(mlp_branch * mlp_branch),
            jnp.sum(result * result),
        ]
    )
    out_grad = grad_output.astype(jnp.float32)
    d_gate_mlp = jnp.sum(out_grad * mlp_out, axis=0)
    d_mlp = (gate_mlp * out_grad).astype(jnp.bfloat16)
    d_b_down = jnp.sum(d_mlp.astype(jnp.float32), axis=(0, 1))
    full_d_mlp = lax.all_gather(d_mlp, "tensor", axis=0, tiled=True)
    d_active = jnp.einsum("lbd,fd->lbf", full_d_mlp, down_w, preferred_element_type=jnp.float32)
    grad_down = jnp.einsum("lbf,lbd->fd", active, full_d_mlp, preferred_element_type=jnp.float32)
    d_hidden = jax.vjp(gelu_tanh, hidden)[1](d_active)[0].astype(jnp.bfloat16)
    grad_up = jnp.einsum("lbd,lbf->df", full_mlp_in, d_hidden, preferred_element_type=jnp.float32)
    own_b_up = jnp.sum(d_hidden.astype(jnp.float32), axis=(0, 1))
    d_b_up = lax.dynamic_update_slice_in_dim(
        jnp.zeros(b_up_f.shape, jnp.float32), own_b_up, t_index * unit_count, 0
    )
    portion = d_hidden
    d_mlp_in = lax.psum_scatter(
        jnp.einsum("lbf,df->lbd", portion, up_w, preferred_element_type=jnp.float32),
        "tensor",
        scatter_dimension=0,
        tiled=True,
    )
    pull_two = jax.vjp(norm_mod, middle, gain_two_f, shift_mlp, scale_mlp)[1]
    middle_part, d_gain_two, d_shift_mlp, d_scale_mlp = pull_two(d_mlp_in)
    d_middle = out_grad + middle_part
    d_gate_attn = jnp.sum(d_middle * attn_out, axis=0)
    d_attn = (gate_attn * d_middle).astype(jnp.bfloat16)
    full_d_attn = lax.all_gather(d_attn, "tensor", axis=0, tiled=True)
    grad_out = jnp.einsum("lbe,lbd->ed", mixed_all, full_d_attn, preferred_element_type=jnp.float32)
    d_mixed = jnp.einsum(
        "lbd,ed->lbe", full_d_attn, out_w, preferred_element_type=jnp.float32
    ).astype(jnp.bfloat16)
    d_mixed_heads = d_mixed.reshape(head_shape).transpose(1, 2, 0, 3)

    def backward_block(accums, inputs):
        key_acc, value_acc = accums
        position, log_blk = inputs
        sequence = position // per_seq
        offset = position % per_seq * block_rows
        query_blk = seq_block(query_heads, sequence, offset, block_rows)
        d_mixed_blk = seq_block(d_mixed_heads, sequence, offset, block_rows)
        key_seq = lax.dynamic_index_in_dim(key_heads, sequence, 0, keepdims=False)
        value_seq = lax.dynamic_index_in_dim(value_heads, sequence, 0, keepdims=False)
        scores = jnp.einsum("hqe,hke->hqk", query_blk, key_seq, preferred_element_type=jnp.float32)
        probs = jnp.exp(scores - log_blk[..., None])
        d_probs = jnp.einsum(
            "hqe,hke->hqk", d_mixed_blk, value_seq, preferred_element_type=jnp.float32
        )
        row_inner = jnp.sum(probs * d_probs, axis=-1, keepdims=True)
        d_scores = (probs * (d_probs - row_inner)).astype(jnp.bfloat16)
        d_query_blk = jnp.einsum(
            "hqk,hke->hqe", d_scores, key_seq, preferred_element_type=jnp.float32
        )
        d_key_blk = jnp.einsum(
            "hqk,hqe->hke", d_scores, query_blk, preferred_element_type=jnp.float32
        )
        d_value_blk = jnp.einsum(
            "hqk,hqe->hke",
            probs.astype(jnp.bfloat16),
            d_mixed_blk,
            preferred_element_type=jnp.float32,
        )
        key_now = lax.dynamic_index_in_dim(key_acc, sequence, 0, keepdims=False) + d_key_blk
        value_now = lax.dynamic_index_in_dim(value_acc, sequence, 0, keepdims=False) + d_value_blk
        key_acc = lax.dynamic_update_index_in_dim(key_acc, key_now, sequence, 0)
        value_acc = lax.dynamic_update_index_in_dim(value_acc, value_now, sequence, 0)
        return ((key_acc, value_acc), d_query_blk)

    zero_heads = jnp.zeros((sequences, heads_here, length, HEAD_DIM), jnp.float32)
    (d_key_heads, d_value_heads), d_query_blocks = lax.scan(
        backward_block, (zero_heads, zero_heads), (jnp.arange(block_count), log_total)
    )
    d_query_rot = blocks_to_rows(d_query_blocks, sequences, per_seq, length) * query_scale
    pull_rotate = jax.vjp(partial(rotate, cos_table=cos_table, sine_table=sine_table), query_pre)[1]
    d_query_pre = pull_rotate(d_query_rot)[0]
    d_key_pre = pull_rotate(d_key_heads.transpose(2, 0, 1, 3))[0]
    d_value_all = d_value_heads.transpose(2, 0, 1, 3)
    flat_shape = (length, sequences, heads_here * HEAD_DIM)
    d_projected = jnp.stack(
        [
            d_query_pre.reshape(flat_shape),
            d_key_pre.reshape(flat_shape),
            d_value_all.reshape(flat_shape),
        ],
        axis=2,
    ).astype(jnp.bfloat16)
    grad_qkv = jnp.einsum(
        "lbd,lbje->jde", full_attn_in, d_projected, preferred_element_type=jnp.float32
    )
    portion = d_projected
    d_attn_in = lax.psum_scatter(
        jnp.einsum("lbje,jde->lbd", portion, qkv_w, preferred_element_type=jnp.float32),
        "tensor",
        scatter_dimension=0,
        tiled=True,
    )
    pull_one = jax.vjp(norm_mod, stream, gain_one_f, shift_attn, scale_attn)[1]
    stream_part, d_gain_one, d_shift_attn, d_scale_attn = pull_one(d_attn_in)
    d_stream = d_middle + stream_part
    grad_qkv_own, grad_out_own, grad_up_own, grad_down_own = (
        lax.psum_scatter(grad_qkv, "dp", scatter_dimension=1, tiled=True),
        lax.psum_scatter(grad_out, "dp", scatter_dimension=1, tiled=True),
        lax.psum_scatter(grad_up, "dp", scatter_dimension=0, tiled=True),
        lax.psum_scatter(grad_down, "dp", scatter_dimension=1, tiled=True),
    )
    d_modulation = jnp.concatenate(
        [d_shift_attn, d_scale_attn, d_gate_attn, d_shift_mlp, d_scale_mlp, d_gate_mlp], axis=-1
    )
    d_ada_b = jnp.sum(d_modulation, axis=0)
    d_ada_w = jnp.dot(cond_float.T, d_modulation, precision=PRECISE)
    d_cond_here = jnp.dot(d_modulation, ada_float.T, precision=PRECISE)
    cond_table = jnp.zeros((sequences * n_data, condition.shape[1]), jnp.float32)
    cond_table = lax.dynamic_update_slice_in_dim(cond_table, d_cond_here, d_index * sequences, 0)
    totals = lax.psum(
        (local_squares, cond_table, d_ada_w, d_ada_b, d_gain_one, d_gain_two, d_b_up, d_b_down),
        ("dp", "tensor"),
    )
    root_means = jnp.sqrt(totals[0] / (local_rows * sequences * features * n_tensor * n_data))
    grad_condition = lax.dynamic_slice_in_dim(totals[1], d_index * sequences, sequences, 0)
    return (
        result.astype(jnp.bfloat16),
        d_stream,
        grad_condition,
        totals[2],
        totals[3],
        totals[4],
        grad_qkv_own,
        grad_out_own,
        totals[5],
        grad_up_own,
        totals[6],
        grad_down_own,
        totals[7],
        root_means,
    )


def solution(mesh):
    in_specs = (
        P("tensor", "dp", None),
        P("dp", None),
        P(None, "dp"),
        P("dp"),
        P("dp"),
        P(None, "dp", "tensor"),
        P("tensor", "dp"),
        P("dp"),
        P("dp", "tensor"),
        P("dp"),
        P("tensor", "dp"),
        P("dp"),
        P("tensor", "dp", None),
    )
    out_specs = (
        P("tensor", "dp", None),
        P("tensor", "dp", None),
        P("dp", None),
        P(),
        P(),
        P(),
        P(None, "dp", "tensor"),
        P("tensor", "dp"),
        P(),
        P("dp", "tensor"),
        P(),
        P("tensor", "dp"),
        P(),
        P(),
    )
    return jax.shard_map(shards, mesh=mesh, in_specs=in_specs, out_specs=out_specs, check_vma=False)
```

profile of v0, /device:TPU:0, one launch (start us, length us, event | category | flops | bytes accessed | tf_op | source)
XLA Modules:
  0.0 1209.0 jit_solution(3161789117916995180)
XLA Ops:
  13.9 39.8 %all-reduce.9 = (bf16[4608]{0:T(1024)(128)(2,1)S(1)}, bf16[768]{0:T(1024)(128)(2,1)S(1)}, bf16[768]{0:T(1024)(128)(2,1)}, bf16[768]{0:T(1024)(128)(2,1)}) all-reduce(bf16[4608]{0:T(1024)(128)(2,1)S(1)} %dynamic-update-slice, bf16[768]{0:T(1024)(128)(2,1)S(1)} %dynamic-update-slice.1, ...), channel_id=1, replica_groups=mesh['dp'=8,'tensor'=4] {'dp'}, use_global_device_ids=true, to_apply=%add.4 | all-reduce | flops 6912 | bytes 27648
  60.7 34.8 %all_gather.46 = bf16[3,768,192]{2,0,1:T(4,128)(2,1)S(1)} all-gather(bf16[3,96,192]{2,0,1:T(4,128)(2,1)S(1)} %copy.49), channel_id=1, replica_groups=mesh['dp'=8,'tensor'=4] {'dp'}, dimensions={1}, use_global_device_ids=true | all-gather | bytes 995328 | tf_op jit(solution)/shard_map/all_gather | solution.py:79
  97.6 33.3 %all_gather.47 = bf16[192,768]{0,1:T(8,128)(2,1)} all-gather(bf16[192,96]{0,1:T(8,128)(2,1)S(1)} %copy.55), channel_id=1, replica_groups=mesh['dp'=8,'tensor'=4] {'dp'}, dimensions={1}, use_global_device_ids=true | all-gather | bytes 331776 | tf_op jit(solution)/shard_map/all_gather | solution.py:80
  131.0 3.0 broadcast_multiply_fusion.2
  133.9 3.9 fusion.53
  146.7 101.9 %while.30 = (s32[]{:T(128)}, bf16[4,3,512,64]{3,2,1,0:T(8,128)(2,1)}, f32[4,3,512]{2,1,0:T(4,128)}, s32[4]{0:T(128)S(1)}, bf16[1,3,2048,64]{2,3,1,0:T(8,128)(2,1...) while((s32[]{:T(128)}, ...), condition=%wide.region_5.6_spmd, body=%wide.region_2.5_spmd.sunk | while | flops 1217493504 | bytes 29923640 | solution.py:131
  151.1 14.6 %dot_general.129 = f32[3,512,64]{2,1,0:T(8,128)} custom-call(bf16[3,512,64]{2,1,0:T(8,128)(2,1)} %bitcast.231, bf16[3,2048,64]{2,1,0:T(8,128)(2,1)S(1)} %bitcast.227, bf16[3,2048,64]{2,1,0:T(8,128)(2,1)} %bitcast.230), custom_call_target="tpu_custom_call" | custom-call | flops 805306368 | bytes 1769472 | tf_op jit(solution)/shard_map/while/body/eval_jaxpr/hqk,hke->hqe/dot_general | solution.py:128
  176.6 14.7 %dot_general.129 = f32[3,512,64]{2,1,0:T(8,128)} custom-call(bf16[3,512,64]{2,1,0:T(8,128)(2,1)} %bitcast.231, bf16[3,2048,64]{2,1,0:T(8,128)(2,1)S(1)} %bitcast.227, bf16[3,2048,64]{2,1,0:T(8,128)(2,1)} %bitcast.230), custom_call_target="tpu_custom_call" | custom-call | flops 805306368 | bytes 1769472 | tf_op jit(solution)/shard_map/while/body/eval_jaxpr/hqk,hke->hqe/dot_general | solution.py:128
  202.1 14.7 %dot_general.129 = f32[3,512,64]{2,1,0:T(8,128)} custom-call(bf16[3,512,64]{2,1,0:T(8,128)(2,1)} %bitcast.231, bf16[3,2048,64]{2,1,0:T(8,128)(2,1)S(1)} %bitcast.227, bf16[3,2048,64]{2,1,0:T(8,128)(2,1)} %bitcast.230), custom_call_target="tpu_custom_call" | custom-call | flops 805306368 | bytes 1769472 | tf_op jit(solution)/shard_map/while/body/eval_jaxpr/hqk,hke->hqe/dot_general | solution.py:128
  227.5 14.7 %dot_general.129 = f32[3,512,64]{2,1,0:T(8,128)} custom-call(bf16[3,512,64]{2,1,0:T(8,128)(2,1)} %bitcast.231, bf16[3,2048,64]{2,1,0:T(8,128)(2,1)S(1)} %bitcast.227, bf16[3,2048,64]{2,1,0:T(8,128)(2,1)} %bitcast.230), custom_call_target="tpu_custom_call" | custom-call | flops 805306368 | bytes 1769472 | tf_op jit(solution)/shard_map/while/body/eval_jaxpr/hqk,hke->hqe/dot_general | solution.py:128
  251.6 3.7 convolution_bitcast_fusion.2
  256.4 56.3 %reduce-scatter.13.cloned.1.call-done = f32[512,1,768]{2,0,1:T(8,128)} async-done(((f32[2048,1,768]{2,0,1:T(8,128)}), f32[512,1,768]{2,0,1:T(8,128)}) %reduce-scatter.13.cloned.1.call-update) | async-done | bytes 1572880 | tf_op jit(solution)/shard_map/reduce_scatter | solution.py:136
  319.7 26.1 %all-gather = bf16[8,1,384]{2,1,0:T(2,128)(2,1)S(1)} all-gather(bf16[1,1,384]{2,1,0:T(2,128)(2,1)S(1)} %reshape.555), channel_id=1, replica_groups=mesh['dp'=8,'tensor'=4] {'dp'}, dimensions={0}, use_global_device_ids=true | all-gather | bytes 6912 | tf_op jit(solution)/shard_map/all_gather | solution.py:83
  347.7 8.4 all-gather.15.cloned.1.call-done
  356.1 29.4 %all-gather.13.cloned.1.call-done = bf16[2048,1,768]{2,0,1:T(8,128)(2,1)} async-done(((bf16[512,1,768]{2,0,1:T(8,128)(2,1)}), bf16[2048,1,768]{2,0,1:T(8,128)(2,1)}) %all-gather.13.cloned.1.call-update) | async-done | bytes 3145744 | tf_op jit(solution)/shard_map/all_gather | solution.py:147
  385.5 7.5 fusion.51
  393.0 35.9 %all-gather.17.cloned.1.call-done = bf16[768,768]{0,1:T(8,128)(2,1)} async-done(((bf16[768,96]{0,1:T(8,128)(2,1)}), bf16[768,768]{0,1:T(8,128)(2,1)}) %all-gather.17.cloned.1.call-update) | async-done | bytes 1179664 | tf_op jit(solution)/shard_map/all_gather | solution.py:84
  428.9 8.9 fusion.55
  437.9 20.6 %all-gather.19.cloned.1.call-done = bf16[2048,1,768]{2,0,1:T(8,128)(2,1)} async-done(((bf16[512,1,768]{2,0,1:T(8,128)(2,1)}), bf16[2048,1,768]{2,0,1:T(8,128)(2,1)}) %all-gather.19.cloned.1.call-update) | async-done | bytes 3145744 | tf_op jit(solution)/shard_map/all_gather | solution.py:177
  458.4 9.4 convert_reduce_fusion
  469.6 4.5 convolution_bitcast_fusion.3
  475.6 23.6 %reduce-scatter.15.cloned.1.call-done = bf16[512,1,768]{2,0,1:T(8,128)(2,1)} async-done(((bf16[2048,1,768]{2,0,1:T(8,128)(2,1)}), bf16[512,1,768]{2,0,1:T(8,128)(2,1)}) %reduce-scatter.15.cloned.1.call-update) | async-done | bytes 786448 | tf_op jit(solution)/shard_map/reduce_scatter | solution.py:154
  499.1 60.9 %reduce-scatter.17.cloned.1.call-done = f32[512,1,768]{2,0,1:T(8,128)} async-done(((f32[2048,1,768]{2,0,1:T(8,128)}), f32[512,1,768]{2,0,1:T(8,128)}) %reduce-scatter.17.cloned.1.call-update) | async-done | bytes 1572880 | tf_op jit(solution)/shard_map/reduce_scatter | solution.py:187
  560.1 4.8 multiply_reduce_fusion.2
  569.5 28.6 %all-gather.21.cloned.1.call-done = bf16[2048,1,768]{2,0,1:T(8,128)(2,1)} async-done(((bf16[512,1,768]{2,0,1:T(8,128)(2,1)}), bf16[2048,1,768]{2,0,1:T(8,128)(2,1)}) %all-gather.21.cloned.1.call-update) | async-done | bytes 3145744 | tf_op jit(solution)/shard_map/all_gather | solution.py:198
  598.2 4.0 fusion.56
  603.6 110.1 %while.31 = (s32[]{:T(128)}, f32[1,3,2048,64]{2,3,1,0:T(8,128)S(1)}, f32[1,3,2048,64]{2,3,1,0:T(8,128)}, f32[4,3,512,64]{2,3,1,0:T(8,128)}, s32[4]{0:T(128)S(1)}...) while((s32[]{:T(128)}, ...), condition=%wide.region_15.16_spmd, body=%wide.region_13.15_spmd.sunk | while | flops 2042362368 | bytes 129411448 | solution.py:240
  606.9 2.7 fusion.152
  609.7 4.9 fusion.154
  614.5 4.0 multiply_reduce_fusion.10
  618.5 4.5 multiply_convert_fusion.6
  623.1 5.7 fusion.155
  634.4 2.7 fusion.152
  637.2 4.9 fusion.154
  642.1 4.0 multiply_reduce_fusion.10
  646.1 4.5 multiply_convert_fusion.6
  650.6 5.7 fusion.155
  662.0 2.7 fusion.152
  664.7 4.9 fusion.154
  669.6 4.0 multiply_reduce_fusion.10
  673.6 4.5 multiply_convert_fusion.6
  678.1 5.7 fusion.155
  689.5 2.7 fusion.152
  692.2 4.9 fusion.154
  697.1 4.0 multiply_reduce_fusion.10
  701.1 4.5 multiply_convert_fusion.6
  705.7 5.7 fusion.155
  713.8 2.8 copy.68
  716.6 4.2 fusion.89
  728.2 3.2 fusion.86
  731.4 3.0 copy.62
  734.3 2.8 reshape.575
  738.5 6.7 convolution_bitcast_fusion.1
  745.9 8.7 fusion.45
  755.0 6.0 fusion.49
  764.0 19.5 %reduce-scatter.27.cloned.1.call-done = f32[96,192]{1,0:T(8,128)} async-done(((f32[768,192]{1,0:T(8,128)}), f32[96,192]{1,0:T(8,128)}) %reduce-scatter.27.cloned.1.call-update) | async-done | bytes 73744
  785.1 68.1 %reduce-scatter.25.cloned.1.call-done = f32[96,576]{1,0:T(8,128)} async-done(((f32[768,576]{1,0:T(8,128)}), f32[96,576]{1,0:T(8,128)}) %reduce-scatter.25.cloned.1.call-update) | async-done | bytes 221200
  855.2 58.1 %reduce-scatter.19.cloned.1.call-done = f32[512,1,768]{2,0,1:T(8,128)} async-done(((f32[2048,1,768]{2,0,1:T(8,128)}), f32[512,1,768]{2,0,1:T(8,128)}) %reduce-scatter.19.cloned.1.call-update) | async-done | bytes 1572880 | tf_op jit(solution)/shard_map/reduce_scatter | solution.py:261
  921.6 2.8 copy.58
  925.0 41.4 %all-reduce.8 = (f32[8,128]{1,0:T(8,128)S(1)}, f32[4608]{0:T(1024)}, f32[768]{0:T(1024)}, f32[768]{0:T(1024)}, f32[3072]{0:T(1024)}, /*index=5*/f32[768]{0:T(1024)}, f32[3]{0:T(128)S(1)}) all-reduce(f32[8,128]{1,0:T(8,128)S(1)} %dynamic_update_slice.30, f32[4608]{0:T(1024)S(1)} %reduce.25, ...), channel_id=1, replica_groups=mesh['dp'=8,'tensor'=4] {'dp','tensor'}, use_global_device_ids=true, to_apply=%region_25.26 | all-reduce | flops 11011 | bytes 88088 | tf_op jit(solution)/shard_map/psum | solution.py:284
  967.4 19.2 %reduce-scatter.23.cloned.1.call-done = f32[768,96]{0,1:T(8,128)} async-done(((f32[768,768]{0,1:T(8,128)}), f32[768,96]{0,1:T(8,128)}) %reduce-scatter.23.cloned.1.call-update) | async-done | bytes 294928 | tf_op jit(solution)/shard_map/reduce_scatter | solution.py:274
  986.7 72.0 %reduce-scatter.21.cloned.1.call-done = f32[96,768]{1,0:T(8,128)} async-done(((f32[768,768]{1,0:T(8,128)}), f32[96,768]{1,0:T(8,128)}) %reduce-scatter.21.cloned.1.call-update) | async-done | bytes 294928 | tf_op jit(solution)/shard_map/reduce_scatter | solution.py:273
  1058.7 140.1 %all-reduce.12.cloned.1.call-done = f32[128,4608]{1,0:T(8,128)} async-done(((f32[128,4608]{1,0:T(8,128)}), f32[128,4608]{1,0:T(8,128)}) %all-reduce.12.cloned.1.call-update) | async-done | bytes 2359312 | tf_op jit(solution)/shard_map/psum | solution.py:284
  1198.8 3.2 copy.108
  (292 shorter events, 121.2 us)
Async XLA Ops:
  7.2 49.4 %copy-start.57 = (bf16[1,128]{1,0:T(2,128)(2,1)S(1)}, bf16[1,128]{1,0:T(2,128)(2,1)}, u32[]{:S(2)}) copy-start(bf16[1,128]{1,0:T(2,128)(2,1)} %param.18) | copy-start | bytes 772
  7.2 51.8 %copy-start.3 = (bf16[512,1,768]{2,0,1:T(8,128)(2,1)S(1)}, bf16[512,1,768]{2,0,1:T(8,128)(2,1)}, u32[]{:S(2)}) copy-start(bf16[512,1,768]{2,0,1:T(8,128)(2,1)} %param.17) | copy-start | bytes 2359300
  7.2 49.4 %all-gather.9.cloned.1.call-start = ((), (), s32[]{:S(2)}) async-start(), calls=%async_computation.8 | async-start | bytes 1327104 | tf_op jit(solution)/shard_map/all_gather | solution.py:76
  7.9 126.0 %all-gather.11.cloned.1.call-start = ((), (), s32[]{:S(2)}) async-start(), calls=%async_computation.9 | async-start | bytes 3932160 | tf_op jit(solution)/shard_map/all_gather | solution.py:99
  53.7 6.6 copy-start.30
  55.0 5.3 copy-start.34
  56.5 1.8 copy-start.44
  56.6 3.8 copy-start.40
  56.6 3.9 copy-start.36
  58.3 2.2 copy-start.29
  59.0 1.4 copy-start.32
  59.0 253.7 %copy-start.37 = (f32[768]{0:T(1024)}, f32[768]{0:T(1024)S(1)}, u32[]{:S(2)}) copy-start(f32[768]{0:T(1024)S(1)} %get-tuple-element.319) | copy-start | bytes 9220
  60.3 252.4 %reduce-scatter.13.cloned.1.call-start = ((), (), s32[]{:S(2)}) async-start(), calls=%async_computation.10 | async-start | bytes 7864320 | tf_op jit(solution)/shard_map/reduce_scatter | solution.py:136
  97.6 36.4 %copy-start.23 = (bf16[3,768,192]{1,2,0:T(8,128)(2,1)S(1)}, bf16[3,768,192]{1,2,0:T(8,128)(2,1)}, u32[]{:S(2)}) copy-start(bf16[3,768,192]{1,2,0:T(8,128)(2,1)} %copy.50) | copy-start | bytes 2654212
  138.0 1.4 copy-start.1
  142.4 1.4 copy-start.8
  142.4 1.5 copy-start.15
  142.4 1.7 copy-start.17
  248.6 3.0 copy-start.20
  255.3 100.8 %all-gather.15.cloned.1.call-start = ((), (), s32[]{:S(2)}) async-start(), calls=%async_computation.12 | async-start | bytes 1327104 | tf_op jit(solution)/shard_map/all_gather | solution.py:82
  255.9 129.6 %all-gather.13.cloned.1.call-start = ((), (), s32[]{:S(2)}) async-start(), calls=%async_computation.11 | async-start | bytes 3932160 | tf_op jit(solution)/shard_map/all_gather | solution.py:147
  315.4 1.9 copy-start.9
  316.6 112.3 %all-gather.17.cloned.1.call-start = ((), (), s32[]{:S(2)}) async-start(), calls=%async_computation.13 | async-start | bytes 1327104 | tf_op jit(solution)/shard_map/all_gather | solution.py:84
  317.2 141.2 %all-gather.19.cloned.1.call-start = ((), (), s32[]{:S(2)}) async-start(), calls=%async_computation.15 | async-start | bytes 3932160 | tf_op jit(solution)/shard_map/all_gather | solution.py:177
  318.9 180.2 %reduce-scatter.15.cloned.1.call-start = ((), (), s32[]{:S(2)}) async-start(), calls=%async_computation.14 | async-start | bytes 3932160 | tf_op jit(solution)/shard_map/reduce_scatter | solution.py:154
  437.8 122.3 %reduce-scatter.17.cloned.1.call-start = ((), (), s32[]{:S(2)}) async-start(), calls=%async_computation.16 | async-start | bytes 7864320 | tf_op jit(solution)/shard_map/reduce_scatter | solution.py:187
  458.4 11.1 copy-start.61
  467.8 1.8 copy-start.62
  474.1 124.1 %all-gather.21.cloned.1.call-start = ((), (), s32[]{:S(2)}) async-start(), calls=%async_computation.17 | async-start | bytes 3932160 | tf_op jit(solution)/shard_map/all_gather | solution.py:198
  560.1 5.5 copy-start.12
  565.6 1.5 copy-start.11
  565.6 1.5 copy-start.38
  567.1 2.3 copy-start.7
  567.1 2.3 copy-start.42
  569.5 214.0 %reduce-scatter.27.cloned.1.call-start = ((), (), s32[]{:S(2)}) async-start(), calls=%async_computation.23 | async-start | bytes 884736
  602.2 1.5 copy-start.2
  623.1 5.7 copy-start
  650.6 5.7 copy-start
  678.1 5.7 copy-start
  705.7 5.7 copy-start
  713.8 2.8 copy-start.14
  716.6 4.5 copy-start.22
  720.8 132.4 %reduce-scatter.25.cloned.1.call-start = ((), (), s32[]{:S(2)}) async-start(), calls=%async_computation.22 | async-start | bytes 2211840
  723.8 1.8 copy-start.21
  724.0 2.0 copy-start.6
  724.0 2.0 copy-start.16
  725.6 1.2 copy-start.28
  726.0 2.2 copy-start.59
  737.1 1.4 copy-start.26
  737.2 176.1 %reduce-scatter.19.cloned.1.call-start = ((), (), s32[]{:S(2)}) async-start(), calls=%async_computation.18 | async-start | bytes 7864320 | tf_op jit(solution)/shard_map/reduce_scatter | solution.py:261
  745.3 241.4 %reduce-scatter.23.cloned.1.call-start = ((), (), s32[]{:S(2)}) async-start(), calls=%async_computation.21 | async-start | bytes 2654208 | tf_op jit(solution)/shard_map/reduce_scatter | solution.py:274
  745.9 9.0 copy-start.60
  754.7 304.0 %reduce-scatter.21.cloned.1.call-start = ((), (), s32[]{:S(2)}) async-start(), calls=%async_computation.20 | async-start | bytes 2654208 | tf_op jit(solution)/shard_map/reduce_scatter | solution.py:273
  761.0 152.3 %copy-start.4 = (bf16[512,1,768]{2,0,1:T(8,128)(2,1)S(1)}, bf16[512,1,768]{2,0,1:T(8,128)(2,1)}, u32[]{:S(2)}) copy-start(bf16[512,1,768]{2,0,1:T(8,128)(2,1)} %param.17) | copy-start | bytes 2359300
  761.0 152.3 %copy-start.31 = (f32[768]{0:T(1024)S(1)}, f32[768]{0:T(1024)}, u32[]{:S(2)}) copy-start(f32[768]{0:T(1024)} %copy-done.30) | copy-start | bytes 9220
  761.0 152.3 %copy-start.33 = (f32[768]{0:T(1024)S(1)}, f32[768]{0:T(1024)}, u32[]{:S(2)}) copy-start(f32[768]{0:T(1024)} %copy-done.32) | copy-start | bytes 9220
  761.0 152.3 %copy-start.35 = (f32[512]{0:T(512)S(1)}, f32[512]{0:T(512)}, u32[]{:S(2)}) copy-start(f32[512]{0:T(512)} %copy-done.34) | copy-start | bytes 6148
  761.1 437.7 %all-reduce.12.cloned.1.call-start = ((), (), s32[]{:S(2)}) async-start(), calls=%async_computation.19 | async-start | bytes 4718592 | tf_op jit(solution)/shard_map/psum | solution.py:284
  854.4 60.9 %copy-start.45 = (f32[512]{0:T(512)S(1)}, f32[512]{0:T(512)}, u32[]{:S(2)}) copy-start(f32[512]{0:T(512)} %copy-done.44) | copy-start | bytes 6148
  854.4 60.9 %copy-start.41 = (f32[512]{0:T(512)S(1)}, f32[512]{0:T(512)}, u32[]{:S(2)}) copy-start(f32[512]{0:T(512)} %copy-done.40) | copy-start | bytes 6148
  913.3 2.1 copy-start.5
  921.5 2.8 copy-start.19
  921.5 3.4 copy-start.47
  921.6 3.4 copy-start.48
  (18 other events, 17.4 us)
Sparse Core Ops, SparseCore 0:
  10.2 44.0 all-gather.8
  60.4 25.7 all-gather.10
  255.4 57.2 reduce-scatter.12
  315.0 41.0 all-gather.14
  358.2 27.2 all-gather.12
  387.8 41.0 all-gather.16
  431.1 27.2 all-gather.18
  461.1 37.9 reduce-scatter.14
  501.7 58.3 reduce-scatter.16
  569.6 28.5 all-gather.20
  720.9 62.4 reduce-scatter.26
  787.4 65.8 reduce-scatter.24
  855.9 57.2 reduce-scatter.18
  917.2 69.4 reduce-scatter.22
  990.6 68.0 reduce-scatter.20
  1064.7 134.0 all-reduce.11
where the time goes:
time: 1210 us
  waiting for transfers between devices  643 us (53%)
  blocking collectives  175 us (14%)
  matrix products  160 us (13%)
  other arithmetic  77 us (6%)
  local copies, waits for them, and re-layouts  61.4 us (5%)
  Pallas kernels  58.6 us (5%)
  between operations  16.6 us (1%)
  loops' own time  15.9 us (1%)
    psum x1, waiting for transfers between devices, shards(): lax.psum((local_squares, cond_table, d_ada_w, d_ada_b, d_gain_one, d_gain...  140 us
    unnamed x18, waiting for transfers between devices  89.6 us
    reduce_scatter x1, waiting for transfers between devices, shards(): lax.psum_scatter(grad_up, 'dp', scatter_dimension=0, tiled=True)  72 us
    reduce_scatter x1, waiting for transfers between devices, shards(): lax.psum_scatter(jnp.einsum('lbf,df->lbd', portion, up_w, preferred_eleme...  60.9 us
    dot_general x4, Pallas kernels, forward_block(): jnp.einsum('hqk,hke->hqe', probs, value_seq, preferred_element_type=jnp.f...  58.6 us
    reduce_scatter x1, waiting for transfers between devices, shards(): lax.psum_scatter(jnp.einsum('lbje,jde->lbd', portion, qkv_w, preferred_el...  58.1 us
    reduce_scatter x1, waiting for transfers between devices, shards(): lax.psum_scatter(jnp.einsum('lbe,ed->lbd', portion, out_w, preferred_elem...  56.3 us
    psum x1, blocking collectives, shards(): lax.psum((local_squares, cond_table, d_ada_w, d_ada_b, d_gain_one, d_gain...  41.4 us
  transfers between devices with their start and end apart: 16, of which 14 were waited for; matrix products, arithmetic and copies ran while one was open for 9% of the time, Pallas kernels for 0%

commit v1 on v0

v1 whole, which is shorter than its diff:
```python
from functools import partial

import jax
import jax.numpy as jnp
import numpy as np
from jax import lax
from jax.experimental import pallas as pl
from jax.experimental.pallas import tpu as pltpu
from jax.sharding import PartitionSpec as P

HEAD_DIM = 64
EPSILON = 1e-05
CORES = 2
INNER = 2
MESH = pl.DeviceIdType.MESH
VMEM_LIMIT = 58 << 20
GELU_C = float(np.sqrt(2.0 / np.pi))
GELU_A = 0.044715
F32 = jnp.float32
BF16 = jnp.bfloat16
ANY = pl.BlockSpec(memory_space=pl.ANY)
VMEM = pl.BlockSpec(memory_space=pltpu.VMEM)
DMA = pltpu.SemaphoreType.DMA


def dot(lhs, rhs, lhs_dim, rhs_dim):
    return lax.dot_general(
        lhs, rhs, (((lhs_dim,), (rhs_dim,)), ((), ())), preferred_element_type=F32
    )


def params(collective_id=None, **more):
    if collective_id is not None:
        more.update(collective_id=collective_id, has_side_effects=True)
    return pltpu.CompilerParams(vmem_limit_bytes=VMEM_LIMIT, **more)


def cost(flops, moved, special=0):
    return pl.CostEstimate(flops=int(flops), bytes_accessed=int(moved), transcendentals=int(special))


def struct(shape, dtype):
    return jax.ShapeDtypeStruct(shape, dtype)


def mean_rows(values):
    return jnp.mean(values, axis=-1, keepdims=True)


def sum_tokens(values):
    return jnp.sum(values, axis=0, keepdims=True)


def greet(n_d, n_t):
    d, t = lax.axis_index("dp"), lax.axis_index("tensor")
    barrier = pltpu.get_barrier_semaphore()
    for r in range(1, n_t):
        pl.semaphore_signal(
            barrier, 1, device_id=(d, lax.rem(t + r, n_t)), device_id_type=MESH
        )
    for r in range(1, n_d):
        pl.semaphore_signal(
            barrier, 1, device_id=(lax.rem(d + r, n_d), t), device_id_type=MESH
        )
    pl.semaphore_wait(barrier, n_t - 1 + n_d - 1)


def remote(src, dst, send, recv, d, t):
    return pltpu.make_async_remote_copy(
        src_ref=src, dst_ref=dst, send_sem=send, recv_sem=recv, device_id=(d, t), device_id_type=MESH
    )


def gather_kernel(
    n_d, n_t, parts, cond_at,
    x_ref, w_ref, small_ref, ada_ref, ada_b_ref,
    x_all, w_all, small_all, mod_all, mod_rows,
    s_x, r_x, s_c, r_c, s_f, r_f, s_z, r_z, s_y, r_y, s_s, r_s, s_m, r_m, s_l,
):
    d, t = lax.axis_index("dp"), lax.axis_index("tensor")
    nx, no = n_t // CORES, n_d // INNER
    xi, ci = t // CORES, lax.rem(t, CORES)
    oi, ii = d // INNER, lax.rem(d, INNER)
    other = xi * CORES + (1 - ci)
    rows = x_ref.shape[0] // parts
    greet(n_d, n_t)
    local = [
        pltpu.make_async_copy(x_ref, x_all.at[t], s_l.at[0]),
        pltpu.make_async_copy(w_ref, w_all.at[d], s_l.at[1]),
        pltpu.make_async_copy(small_ref, small_all.at[d], s_l.at[2]),
    ]
    for copy in local:
        copy.start()
    sends = []
    for r in range(1, n_d):
        copy = remote(
            small_ref, small_all.at[d], s_s.at[r - 1], r_s.at[r - 1], lax.rem(d + r, n_d), t
        )
        copy.start()
        sends.append(copy)
    x_copies = []
    for r in range(1, nx):
        peer = lax.rem(xi + r, nx) * CORES + ci
        for p in range(parts):
            part = pl.ds(p * rows, rows)
            copy = remote(
                x_ref.at[part], x_all.at[t, part], s_x.at[r - 1, p], r_x.at[r - 1, p], d, peer
            )
            copy.start()
            x_copies.append((r, p, copy))
    z_copies = []
    for r in range(1, no):
        copy = remote(
            w_ref, w_all.at[d], s_z.at[r - 1], r_z.at[r - 1], lax.rem(oi + r, no) * INNER + ii, t
        )
        copy.start()
        z_copies.append(copy)
    y_copies = []
    for q in range(1, INNER):
        copy = remote(
            w_ref, w_all.at[d], s_y.at[q - 1, 0], r_y.at[q - 1, 0],
            oi * INNER + lax.rem(ii + q, INNER), t,
        )
        copy.start()
        y_copies.append(copy)
    core_copy = remote(x_ref, x_all.at[t], s_c, r_c, d, other)
    core_copy.start()
    local[2].wait()
    for copy in sends:
        copy.wait()
    cond = small_all[:, 0, cond_at:].astype(BF16)
    mod_rows[:, 0, :] = dot(cond, ada_ref[...], 1, 0) + ada_b_ref[...].astype(F32)
    own_mod = pltpu.make_async_copy(mod_rows.at[d], mod_all.at[d], s_l.at[3])
    own_mod.start()
    m_copies = []
    for r in range(1, n_d):
        peer = lax.rem(d + r, n_d)
        copy = remote(mod_rows.at[peer], mod_all.at[d], s_m.at[r - 1], r_m.at[r - 1], peer, t)
        copy.start()
        m_copies.append(copy)
    for r in range(1, no):
        z_copies[r - 1].wait()
        origin = lax.rem(oi + no - r, no) * INNER + ii
        for q in range(1, INNER):
            copy = remote(
                w_all.at[origin], w_all.at[origin], s_y.at[q - 1, r], r_y.at[q - 1, r],
                oi * INNER + lax.rem(ii + q, INNER), t,
            )
            copy.start()
            y_copies.append(copy)
    f_copies = []
    for r, p, copy in x_copies:
        copy.wait()
        origin = lax.rem(xi + nx - r, nx) * CORES + ci
        part = pl.ds(p * rows, rows)
        copy = remote(
            x_all.at[origin, part], x_all.at[origin, part],
            s_f.at[r - 1, p], r_f.at[r - 1, p], d, other,
        )
        copy.start()
        f_copies.append(copy)
    core_copy.wait()
    for copy in m_copies + y_copies + f_copies + [local[0], local[1], own_mod]:
        copy.wait()


def gather_call(x, w, small, ada, ada_b, cond_at, n_d, n_t):
    parts = 4
    nx, no = n_t // CORES, n_d // INNER
    cols = ada.shape[1]
    return pl.pallas_call(
        partial(gather_kernel, n_d, n_t, parts, cond_at),
        name="gather_tokens",
        out_shape=[
            struct((n_t,) + x.shape, BF16),
            struct((n_d,) + w.shape, BF16),
            struct((n_d,) + small.shape, F32),
            struct((n_d, 1, cols), F32),
        ],
        in_specs=[ANY, ANY, VMEM, VMEM, VMEM],
        out_specs=[ANY, ANY, VMEM, VMEM],
        scratch_shapes=[
            pltpu.VMEM((n_d, 1, cols), F32),
            DMA((nx - 1, parts)), DMA((nx - 1, parts)), DMA, DMA,
            DMA((nx - 1, parts)), DMA((nx - 1, parts)),
            DMA((no - 1,)), DMA((no - 1,)),
            DMA((INNER - 1, no)), DMA((INNER - 1, no)),
            DMA((n_d - 1,)), DMA((n_d - 1,)), DMA((n_d - 1,)), DMA((n_d - 1,)),
            DMA((4,)),
        ],
        compiler_params=params(0),
        cost_estimate=cost(1e6, 60e6),
    )(x, w, small, ada, ada_b)


def project_kernel(x_ref, w_ref, vec_ref, cos_ref, sin_ref, in_ref, out_ref):
    x = x_ref[0].astype(F32)
    gain, shift, scale = vec_ref[0:1], vec_ref[1:2], vec_ref[2:3]
    centred = x - mean_rows(x)
    normed = centred * lax.rsqrt(mean_rows(centred * centred) + EPSILON) * gain
    low = (normed * (1.0 + scale) + shift).astype(BF16)
    in_ref[0] = low
    proj = dot(w_ref[...], low, 0, 1)
    width = proj.shape[0] // 3
    half = HEAD_DIM // 2
    cos, sin = cos_ref[...], sin_ref[...]
    for j in range(2):
        factor = HEAD_DIM**-0.5 if j == 0 else 1.0
        for h in range(width // HEAD_DIM):
            at = j * width + h * HEAD_DIM
            a, b = proj[at : at + half], proj[at + half : at + HEAD_DIM]
            out_ref[0, at : at + half] = ((a * cos - b * sin) * factor).astype(BF16)
            out_ref[0, at + half : at + HEAD_DIM] = ((b * cos + a * sin) * factor).astype(BF16)
    out_ref[0, 2 * width :] = proj[2 * width :].astype(BF16)


def project_call(x_all, w, vecs, cos, sin):
    n_t, rows, features = x_all.shape
    width = w.shape[1]
    return pl.pallas_call(
        project_kernel,
        name="project",
        grid=(n_t,),
        in_specs=[
            pl.BlockSpec((1, rows, features), lambda i: (i, 0, 0)),
            pl.BlockSpec((features, width), lambda i: (0, 0)),
            pl.BlockSpec(vecs.shape, lambda i: (0, 0)),
            pl.BlockSpec((HEAD_DIM // 2, rows), lambda i: (0, i)),
            pl.BlockSpec((HEAD_DIM // 2, rows), lambda i: (0, i)),
        ],
        out_specs=[
            pl.BlockSpec((1, rows, features), lambda i: (i, 0, 0)),
            pl.BlockSpec((1, width, rows), lambda i: (i, 0, 0)),
        ],
        out_shape=[
            struct((n_t, rows, features), BF16),
            struct((n_t, width, rows), BF16),
        ],
        compiler_params=params(),
        cost_estimate=cost(2 * n_t * rows * features * width, 12e6),
    )(x_all, w, vecs, cos, sin)


def attend_kernel(heads, proj_ref, mix_ref, lse_ref, key_ref, val_ref):
    i = pl.program_id(0)
    blocks, total, rows = proj_ref.shape
    width = total // 3

    @pl.when(i == 0)
    def _():
        for b in range(blocks):
            for h in range(heads):
                at = width + h * HEAD_DIM
                key_ref[h, b * rows : (b + 1) * rows] = proj_ref[b, at : at + HEAD_DIM].T
            val_ref[:, b * rows : (b + 1) * rows] = proj_ref[b, 2 * width :]

    for h in range(heads):
        at = h * HEAD_DIM
        scores = dot(key_ref[h], proj_ref[i, at : at + HEAD_DIM], 1, 0)
        top = jnp.max(scores, axis=0, keepdims=True)
        grown = jnp.exp(scores - top)
        total_row = jnp.sum(grown, axis=0, keepdims=True)
        mixed = dot(val_ref[at : at + HEAD_DIM], grown.astype(BF16), 1, 0)
        mix_ref[0, at : at + HEAD_DIM] = (mixed / total_row).astype(BF16)
        lse_ref[0, h : h + 1] = top + jnp.log(total_row)


def attend_call(proj):
    blocks, total, rows = proj.shape
    width = total // 3
    heads = width // HEAD_DIM
    length = blocks * rows
    return pl.pallas_call(
        partial(attend_kernel, heads),
        name="attend",
        grid=(blocks,),
        in_specs=[pl.BlockSpec(proj.shape, lambda i: (0, 0, 0))],
        out_specs=[
            pl.BlockSpec((1, width, rows), lambda i: (i, 0, 0)),
            pl.BlockSpec((1, heads, rows), lambda i: (i, 0, 0)),
        ],
        out_shape=[struct((blocks, width, rows), BF16), struct((blocks, heads, rows), F32)],
        scratch_shapes=[
            pltpu.VMEM((heads, length, HEAD_DIM), BF16),
            pltpu.VMEM((width, length), BF16),
        ],
        compiler_params=params(),
        cost_estimate=cost(16 * heads * length * length * HEAD_DIM, 4e6, heads * length * length),
    )(proj)


def swap_kernel(n_t, src_ref, dst_ref, send, recv, own):
    d, t = lax.axis_index("dp"), lax.axis_index("tensor")
    barrier = pltpu.get_barrier_semaphore()
    for r in range(1, n_t):
        pl.semaphore_signal(barrier, 1, device_id=(d, lax.rem(t + r, n_t)), device_id_type=MESH)
    pl.semaphore_wait(barrier, n_t - 1)
    copies = [pltpu.make_async_copy(src_ref.at[t], dst_ref.at[t], own)]
    copies[0].start()
    for r in range(1, n_t):
        peer = lax.rem(t + r, n_t)
        copy = remote(src_ref.at[peer], dst_ref.at[t], send.at[r - 1], recv.at[r - 1], d, peer)
        copy.start()
        copies.append(copy)
    for copy in copies:
        copy.wait()


def swap_call(blocks, n_t, collective_id):
    return pl.pallas_call(
        partial(swap_kernel, n_t),
        name="swap_blocks",
        out_shape=struct(blocks.shape, blocks.dtype),
        in_specs=[ANY],
        out_specs=ANY,
        scratch_shapes=[DMA((n_t - 1,)), DMA((n_t - 1,)), DMA],
        compiler_params=params(collective_id),
        cost_estimate=cost(0, 30e6),
    )(blocks)


GAIN1, SHIFT_A, SCALE_A, GATE_A, GAIN2, SHIFT_M, SCALE_M, GATE_M, B_DOWN, B_UP = range(10)
S_SHIFT_A, S_SCALE_A, S_GATE_A, S_SHIFT_M, S_SCALE_M, S_GATE_M = range(6)
S_GAIN2, S_B_DOWN, S_SQ_A, S_SQ_M, S_SQ_R, S_GAIN1, S_B_UP = range(6, 13)


def middle_kernel(
    n_d, n_t,
    mix_ref, x_ref, g_ref, vec_ref, w_ref,
    out_ref, dmid_ref, dmix_ref, stat_ref, grad_ref,
    w_buf, o_buf, g_buf, go_buf, mid_ref, low_ref, lowt_ref, dlt_ref, dl_ref, acc_out, acc_in, s_w, s_o, s_g,
):
    rows, features = x_ref.shape
    width = mix_ref.shape[1]
    units = w_buf.shape[3] // 2
    loads = [
        pltpu.make_async_copy(w_ref.at[:, :, :, pl.ds(2 * units, o_buf.shape[3])], o_buf, s_o)
    ]
    for b in range(n_t):
        loads.append(
            pltpu.make_async_copy(
                w_ref.at[:, b, :, pl.ds(0, 2 * units)], w_buf.at[b], s_w.at[b]
            )
        )
    for copy in loads:
        copy.start()
    vec = lambda row: vec_ref[row : row + 1]
    x = x_ref[...].astype(F32)
    cot = g_ref[...].astype(F32)
    d_mlp = (vec(GATE_M) * cot).astype(BF16)
    dl_ref[...] = d_mlp
    dlt_ref[...] = d_mlp.T
    stat_ref[S_B_DOWN : S_B_DOWN + 1] = sum_tokens(d_mlp.astype(F32))
    loads[0].wait()
    attn_out = jnp.zeros((rows, features), F32)
    for b in range(n_t):
        w_out = o_buf[:, b].reshape(features, o_buf.shape[3])[:, :width]
        attn_out += dot(mix_ref[b].T, w_out, 1, 1)
    branch = vec(GATE_A) * attn_out
    stat_ref[S_SQ_A : S_SQ_A + 1] = sum_tokens(branch * branch)
    middle = x + branch
    mid_ref[...] = middle
    centred = middle - mean_rows(middle)
    inv = lax.rsqrt(mean_rows(centred * centred) + EPSILON)
    low = (centred * inv * vec(GAIN2) * (1.0 + vec(SCALE_M)) + vec(SHIFT_M)).astype(BF16)
    low_ref[...] = low
    lowt_ref[...] = low.T
    acc_out[...] = jnp.zeros_like(acc_out)
    acc_in[...] = jnp.zeros_like(acc_in)
    stores = []
    for b in range(n_t):
        loads[1 + b].wait()
        up = w_buf[b, :, :, :units].reshape(features, units)
        down = w_buf[b, :, :, units:].reshape(features, units)
        hidden = dot(low_ref[...], up, 1, 0) + vec(B_UP + b)
        square = hidden * hidden
        bent = jnp.tanh(GELU_C * hidden * (1.0 + GELU_A * square))
        half = 0.5 * (1.0 + bent)
        active = (hidden * half).astype(BF16)
        slope = half + (0.5 * GELU_C) * hidden * (1.0 - bent * bent) * (
            1.0 + (3.0 * GELU_A) * square
        )
        acc_out[...] += dot(active, down, 1, 1)
        g_buf[b, :, :, units:] = (
            dot(dlt_ref[...], active, 1, 0).astype(BF16).reshape(n_d, -1, units)
        )
        d_hidden = (dot(dl_ref[...], down, 1, 0) * slope).astype(BF16)
        stat_ref[S_B_UP + b : S_B_UP + b + 1] = sum_tokens(d_hidden.astype(F32))
        g_buf[b, :, :, :units] = (
            dot(lowt_ref[...], d_hidden, 1, 0).astype(BF16).reshape(n_d, -1, units)
        )
        copy = pltpu.make_async_copy(
            g_buf.at[b], grad_ref.at[:, b, :, pl.ds(0, 2 * units)], s_g.at[b]
        )
        copy.start()
        stores.append(copy)
        acc_in[...] += dot(d_hidden, up, 1, 1)
    middle = mid_ref[...]
    cot = g_ref[...].astype(F32)
    mlp_out = acc_out[...] + vec(B_DOWN)
    mlp_branch = vec(GATE_M) * mlp_out
    result = middle + mlp_branch
    out_ref[...] = result.astype(BF16)
    stat_ref[S_SQ_M : S_SQ_M + 1] = sum_tokens(mlp_branch * mlp_branch)
    stat_ref[S_SQ_R : S_SQ_R + 1] = sum_tokens(result * result)
    stat_ref[S_GATE_M : S_GATE_M + 1] = sum_tokens(cot * mlp_out)
    e = acc_in[...]
    centred = middle - mean_rows(middle)
    inv = lax.rsqrt(mean_rows(centred * centred) + EPSILON)
    nhat = centred * inv
    gain, scale = vec(GAIN2), 1.0 + vec(SCALE_M)
    by_nhat = sum_tokens(e * nhat)
    stat_ref[S_SHIFT_M : S_SHIFT_M + 1] = sum_tokens(e)
    stat_ref[S_SCALE_M : S_SCALE_M + 1] = by_nhat * gain
    stat_ref[S_GAIN2 : S_GAIN2 + 1] = by_nhat * scale
    dn = e * (scale * gain)
    d_middle = cot + inv * (dn - mean_rows(dn) - nhat * mean_rows(dn * nhat))
    dmid_ref[...] = d_middle
    attn_out = jnp.zeros((rows, features), F32)
    for b in range(n_t):
        w_out = o_buf[:, b].reshape(features, o_buf.shape[3])[:, :width]
        attn_out += dot(mix_ref[b].T, w_out, 1, 1)
    stat_ref[S_GATE_A : S_GATE_A + 1] = sum_tokens(d_middle * attn_out)
    d_attn = (vec(GATE_A) * d_middle).astype(BF16)
    d_attn_t = d_attn.T
    go_buf[...] = jnp.zeros_like(go_buf)
    for b in range(n_t):
        w_out = o_buf[:, b].reshape(features, o_buf.shape[3])[:, :width]
        dmix_ref[b] = dot(d_attn, w_out, 1, 0).astype(BF16).T
        go_buf[:, b, :, :width] = dot(d_attn_t, mix_ref[b], 1, 1).astype(BF16).reshape(n_d, -1, width)
    stat_ref[S_GAIN1 : S_GAIN1 + 1] = jnp.zeros((1, features), F32)
    stat_ref[S_SHIFT_A : S_SCALE_A + 1] = jnp.zeros((2, features), F32)
    if stat_ref.shape[0] > S_B_UP + n_t:
        stat_ref[S_B_UP + n_t :] = jnp.zeros((stat_ref.shape[0] - S_B_UP - n_t, features), F32)
    copy = pltpu.make_async_copy(
        go_buf, grad_ref.at[:, :, :, pl.ds(2 * units, o_buf.shape[3])], s_o
    )
    copy.start()
    for copy in stores + [copy]:
        copy.wait()


def middle_call(mix, x, g, vecs, w, n_d, n_t, stat_rows):
    rows, features = x.shape
    part, columns = w.shape[2], w.shape[3]
    width = mix.shape[1]
    units = features
    extra = columns - 2 * units
    return pl.pallas_call(
        partial(middle_kernel, n_d, n_t),
        name="middle",
        out_shape=[
            struct((rows, features), BF16),
            struct((rows, features), F32),
            struct((n_t, width, rows), BF16),
            struct((stat_rows, features), F32),
            struct(w.shape, BF16),
        ],
        in_specs=[VMEM, VMEM, VMEM, VMEM, ANY],
        out_specs=[VMEM, VMEM, VMEM, VMEM, ANY],
        scratch_shapes=[
            pltpu.VMEM((n_t, n_d, part, 2 * units), BF16),
            pltpu.VMEM((n_d, n_t, part, extra), BF16),
            pltpu.VMEM((n_t, n_d, part, 2 * units), BF16),
            pltpu.VMEM((n_d, n_t, part, extra), BF16),
            pltpu.VMEM((rows, features), F32),
            pltpu.VMEM((rows, features), BF16),
            pltpu.VMEM((features, rows), BF16),
            pltpu.VMEM((features, rows), BF16),
            pltpu.VMEM((rows, features), BF16),
            pltpu.VMEM((rows, features), F32),
            pltpu.VMEM((rows, features), F32),
            DMA((n_t,)), DMA, DMA((n_t,)),
        ],
        compiler_params=params(),
        cost_estimate=cost(2 * rows * features * features * (6 * n_t + 4), 30e6),
    )(mix, x, g, vecs, w)


def attend_back_kernel(
    heads, proj_ref, dmix_ref, mix_ref, lse_ref, cos_ref, sin_ref, out_ref,
    key_ref, keyt_ref, val_ref, dkey_ref, dval_ref,
):
    i = pl.program_id(0)
    blocks, total, rows = proj_ref.shape
    width = total // 3
    half = HEAD_DIM // 2

    @pl.when(i == 0)
    def _():
        dkey_ref[...] = jnp.zeros_like(dkey_ref)
        dval_ref[...] = jnp.zeros_like(dval_ref)
        for b in range(blocks):
            part = slice(b * rows, (b + 1) * rows)
            keyt_ref[:, part] = proj_ref[b, width : 2 * width]
            for h in range(heads):
                at = h * HEAD_DIM
                key_ref[h, part] = proj_ref[b, width + at : width + at + HEAD_DIM].T
                val_ref[h, part] = proj_ref[b, 2 * width + at : 2 * width + at + HEAD_DIM].T

    def unrotate(block, at, rows_at, factor, a, b):
        cos, sin = cos_ref[:, rows_at], sin_ref[:, rows_at]
        out_ref[block, at : at + half] = ((a * cos + b * sin) * factor).astype(BF16)
        out_ref[block, at + half : at + HEAD_DIM] = ((b * cos - a * sin) * factor).astype(BF16)

    for h in range(heads):
        at = h * HEAD_DIM
        query_t = proj_ref[i, at : at + HEAD_DIM]
        dmix_t = dmix_ref[i, at : at + HEAD_DIM]
        mix_t = mix_ref[i, at : at + HEAD_DIM]
        inner = jnp.sum(dmix_t.astype(F32) * mix_t.astype(F32), axis=0, keepdims=True)
        probs = jnp.exp(dot(key_ref[h], query_t, 1, 0) - lse_ref[i, h : h + 1])
        d_probs = dot(val_ref[h], dmix_t, 1, 0)
        d_scores = (probs * (d_probs - inner)).astype(BF16)
        dval_ref[h] += dot(probs.astype(BF16), dmix_t.T, 1, 0)
        dkey_ref[h] += dot(d_scores, query_t.T, 1, 0)
        d_query = dot(keyt_ref[at : at + HEAD_DIM], d_scores, 1, 0)
        unrotate(
            i, at, pl.ds(pl.multiple_of(i * rows, rows), rows), HEAD_DIM**-0.5,
            d_query[:half], d_query[half:],
        )

    @pl.when(i == blocks - 1)
    def _():
        for b in range(blocks):
            part = slice(b * rows, (b + 1) * rows)
            for h in range(heads):
                at = h * HEAD_DIM
                d_key = dkey_ref[h, part].T
                unrotate(b, width + at, part, 1.0, d_key[:half], d_key[half:])
                out_ref[b, 2 * width + at : 2 * width + at + HEAD_DIM] = (
                    dval_ref[h, part].T.astype(BF16)
                )


def attend_back_call(proj, dmix, mix, lse, cos, sin):
    blocks, total, rows = proj.shape
    width = total // 3
    heads = width // HEAD_DIM
    length = blocks * rows
    whole = lambda a: pl.BlockSpec(a.shape, lambda i: (0,) * a.ndim)
    return pl.pallas_call(
        partial(attend_back_kernel, heads),
        name="attend_back",
        grid=(blocks,),
        in_specs=[whole(a) for a in (proj, dmix, mix, lse, cos, sin)],
        out_specs=whole(proj),
        out_shape=struct(proj.shape, BF16),
        scratch_shapes=[
            pltpu.VMEM((heads, length, HEAD_DIM), BF16),
            pltpu.VMEM((width, length), BF16),
            pltpu.VMEM((heads, length, HEAD_DIM), BF16),
            pltpu.VMEM((heads, length, HEAD_DIM), F32),
            pltpu.VMEM((heads, length, HEAD_DIM), F32),
        ],
        compiler_params=params(),
        cost_estimate=cost(40 * heads * length * length * HEAD_DIM, 6e6, heads * length * length),
    )(proj, dmix, mix, lse, cos, sin)


def project_back_kernel(n_d, dproj_ref, in_ref, w_ref, part_ref, grad_ref, acc_ref):
    i = pl.program_id(0)

    @pl.when(i == 0)
    def _():
        acc_ref[...] = jnp.zeros_like(acc_ref)

    d_proj = dproj_ref[0]
    part_ref[0] = dot(d_proj.T, w_ref[...], 1, 1).astype(BF16)
    acc_ref[...] += dot(d_proj, in_ref[0], 1, 0)

    @pl.when(i == pl.num_programs(0) - 1)
    def _():
        grad_ref[...] = acc_ref[...].T.astype(BF16).reshape(grad_ref.shape)


def project_back_call(dproj, attn_in, w, n_d):
    n_t, rows, features = attn_in.shape
    width = w.shape[1]
    return pl.pallas_call(
        partial(project_back_kernel, n_d),
        name="project_back",
        grid=(n_t,),
        in_specs=[
            pl.BlockSpec((1, width, rows), lambda i: (i, 0, 0)),
            pl.BlockSpec((1, rows, features), lambda i: (i, 0, 0)),
            pl.BlockSpec(w.shape, lambda i: (0, 0)),
        ],
        out_specs=[
            pl.BlockSpec((1, rows, features), lambda i: (i, 0, 0)),
            pl.BlockSpec((n_d, features // n_d, width), lambda i: (0, 0, 0)),
        ],
        out_shape=[
            struct((n_t, rows, features), BF16),
            struct((n_d, features // n_d, width), BF16),
        ],
        scratch_shapes=[pltpu.VMEM((width, features), F32)],
        compiler_params=params(),
        cost_estimate=cost(4 * n_t * rows * features * width, 12e6),
    )(dproj, attn_in, w)


def reduce_kernel(
    n_d, n_t, parts,
    part_ref, grad_ref, sum_ref, gsum_ref,
    rc, sx, rx, ry, sz, rz,
    s_c, r_c, s_x, r_x, s_y, r_y, s_z, r_z,
):
    d, t = lax.axis_index("dp"), lax.axis_index("tensor")
    nx, no = n_t // CORES, n_d // INNER
    xi, ci = t // CORES, lax.rem(t, CORES)
    oi, ii = d // INNER, lax.rem(d, INNER)
    other = xi * CORES + (1 - ci)
    rows = sum_ref.shape[0] // parts
    greet(n_d, n_t)
    y_copies = []
    for q in range(1, INNER):
        to = lax.rem(ii + q, INNER)
        copy = remote(
            grad_ref.at[:, to], ry.at[q - 1], s_y.at[q - 1], r_y.at[q - 1], oi * INNER + to, t
        )
        copy.start()
        y_copies.append(copy)
    c_copies = []
    for r in list(range(1, nx)) + [0]:
        block = lax.rem(xi + r, nx) * CORES + (1 - ci)
        for p in range(parts):
            at = pl.ds(p * rows, rows)
            copy = remote(
                part_ref.at[block, at], rc.at[r, at], s_c.at[r, p], r_c.at[r, p], d, other
            )
            copy.start()
            c_copies.append((r, p, copy))
    x_copies = []
    for r, p, copy in c_copies:
        copy.wait()
        if r > 0:
            to = lax.rem(xi + r, nx) * CORES + ci
            at = pl.ds(p * rows, rows)
            sx[r - 1, at] = (part_ref[to, at].astype(F32) + rc[r, at].astype(F32)).astype(BF16)
            copy = remote(
                sx.at[r - 1, at], rx.at[r - 1, at], s_x.at[r - 1, p], r_x.at[r - 1, p], d, to
            )
            copy.start()
            x_copies.append((r, p, copy))
    for copy in y_copies:
        copy.wait()
    z_copies = []
    for r in range(1, no):
        to = lax.rem(oi + r, no)
        total = grad_ref[to, ii].astype(F32)
        for q in range(1, INNER):
            total += ry[q - 1, to].astype(F32)
        sz[r - 1] = total.astype(BF16)
        copy = remote(sz.at[r - 1], rz.at[r - 1], s_z.at[r - 1], r_z.at[r - 1], to * INNER + ii, t)
        copy.start()
        z_copies.append(copy)
    total = grad_ref[oi, ii].astype(F32)
    for q in range(1, INNER):
        total += ry[q - 1, oi].astype(F32)
    for copy in z_copies:
        copy.wait()
    for r in range(1, no):
        total += rz[r - 1].astype(F32)
    gsum_ref[...] = total
    for r, p, copy in x_copies:
        copy.wait()
    for p in range(parts):
        at = pl.ds(p * rows, rows)
        total = part_ref[t, at].astype(F32) + rc[0, at].astype(F32)
        for r in range(1, nx):
            total += rx[r - 1, at].astype(F32)
        sum_ref[at] = total


def reduce_call(part, grad, n_d, n_t):
    parts = 4
    nx, no = n_t // CORES, n_d // INNER
    block = part.shape[1:]
    piece = grad.shape[1:]
    grad = grad.reshape((no, INNER) + piece)
    return pl.pallas_call(
        partial(reduce_kernel, n_d, n_t, parts),
        name="reduce_parts",
        out_shape=[struct(block, F32), struct(piece, F32)],
        in_specs=[VMEM, VMEM],
        out_specs=[VMEM, VMEM],
        scratch_shapes=[
            pltpu.VMEM((nx,) + block, BF16),
            pltpu.VMEM((nx - 1,) + block, BF16),
            pltpu.VMEM((nx - 1,) + block, BF16),
            pltpu.VMEM((INNER - 1, no) + piece, BF16),
            pltpu.VMEM((no - 1,) + piece, BF16),
            pltpu.VMEM((no - 1,) + piece, BF16),
            DMA((nx, parts)), DMA((nx, parts)),
            DMA((nx - 1, parts)), DMA((nx - 1, parts)),
            DMA((INNER - 1,)), DMA((INNER - 1,)),
            DMA((no - 1,)), DMA((no - 1,)),
        ],
        compiler_params=params(3),
        cost_estimate=cost(1e6, 60e6),
    )(part, grad)


def norm_back_kernel(x_ref, e_ref, dmid_ref, vec_ref, stat_in_ref, out_ref, stat_ref):
    x = x_ref[...].astype(F32)
    e = e_ref[...]
    gain, scale = vec_ref[GAIN1 : GAIN1 + 1], 1.0 + vec_ref[SCALE_A : SCALE_A + 1]
    centred = x - mean_rows(x)
    inv = lax.rsqrt(mean_rows(centred * centred) + EPSILON)
    nhat = centred * inv
    dn = e * (scale * gain)
    out_ref[...] = dmid_ref[...] + inv * (dn - mean_rows(dn) - nhat * mean_rows(dn * nhat))
    by_nhat = sum_tokens(e * nhat)
    stat_ref[...] = stat_in_ref[...]
    stat_ref[S_SHIFT_A : S_SHIFT_A + 1] = sum_tokens(e)
    stat_ref[S_SCALE_A : S_SCALE_A + 1] = by_nhat * gain
    stat_ref[S_GAIN1 : S_GAIN1 + 1] = by_nhat * scale


def norm_back_call(x, e, dmid, vecs, stat):
    return pl.pallas_call(
        norm_back_kernel,
        name="norm_back",
        out_shape=[struct(x.shape, F32), struct(stat.shape, F32)],
        in_specs=[VMEM] * 5,
        out_specs=[VMEM] * 2,
        compiler_params=params(),
        cost_estimate=cost(20 * x.size, 8e6),
    )(x, e, dmid, vecs, stat)


def stat_kernel(
    n_d, n_t, stat_ref, ada_ref, table_ref, cond_ref,
    got, mine, rows_out, rows_in, s_t, r_t, s_d, r_d, s_p, r_p, s_l,
):
    d, t = lax.axis_index("dp"), lax.axis_index("tensor")
    greet(n_d, n_t)
    copies = []
    for r in range(1, n_t):
        copy = remote(
            stat_ref, got.at[r - 1], s_t.at[r - 1], r_t.at[r - 1], d, lax.rem(t + r, n_t)
        )
        copy.start()
        copies.append(copy)
    total = stat_ref[...]
    for copy in copies:
        copy.wait()
    for r in range(1, n_t):
        total += got[r - 1]
    mine[...] = total
    own = pltpu.make_async_copy(mine, table_ref.at[d], s_l.at[0])
    own.start()
    copies = []
    for r in range(1, n_d):
        copy = remote(mine, table_ref.at[d], s_d.at[r - 1], r_d.at[r - 1], lax.rem(d + r, n_d), t)
        copy.start()
        copies.append(copy)
    own.wait()
    for copy in copies:
        copy.wait()
    columns = ada_ref.shape[1]
    features = table_ref.shape[2]
    flat = jnp.concatenate([table_ref[:, row, :] for row in range(6)], axis=1)
    moved = pltpu.roll(flat, lax.rem(n_d - d, n_d) * columns, 1)[:, :columns]
    product = lax.dot_general(
        moved, ada_ref[...].astype(F32), (((1,), (1,)), ((), ())),
        precision=lax.Precision.HIGHEST, preferred_element_type=F32,
    )
    rows_out[:, 0, :] = product
    own = pltpu.make_async_copy(rows_out.at[d], rows_in.at[d], s_l.at[1])
    own.start()
    copies = []
    for r in range(1, n_d):
        peer = lax.rem(d + r, n_d)
        copy = remote(rows_out.at[peer], rows_in.at[d], s_p.at[r - 1], r_p.at[r - 1], peer, t)
        copy.start()
        copies.append(copy)
    own.wait()
    for copy in copies:
        copy.wait()
    cond_ref[...] = jnp.sum(rows_in[:, 0, :], axis=0, keepdims=True)


def stat_call(stat, ada, n_d, n_t):
    width = ada.shape[0]
    return pl.pallas_call(
        partial(stat_kernel, n_d, n_t),
        name="gather_statistics",
        out_shape=[struct((n_d,) + stat.shape, F32), struct((1, width), F32)],
        in_specs=[VMEM, VMEM],
        out_specs=[VMEM, VMEM],
        scratch_shapes=[
            pltpu.VMEM((n_t - 1,) + stat.shape, F32),
            pltpu.VMEM(stat.shape, F32),
            pltpu.VMEM((n_d, 1, width), F32),
            pltpu.VMEM((n_d, 1, width), F32),
            DMA((n_t - 1,)), DMA((n_t - 1,)),
            DMA((n_d - 1,)), DMA((n_d - 1,)),
            DMA((n_d - 1,)), DMA((n_d - 1,)),
            DMA((2,)),
        ],
        compiler_params=params(4),
        cost_estimate=cost(1e6, 20e6),
    )(stat, ada)


def finish_kernel(n_units, count, table_ref, cond_ref, ada_ref, bias_ref, sum_ref, root_ref):
    n_d = table_ref.shape[0]
    features = table_ref.shape[2]
    for row in range(6):
        at = slice(row * features, (row + 1) * features)
        total = jnp.zeros((cond_ref.shape[0], features), F32)
        for s in range(n_d):
            total += cond_ref[:, s : s + 1] * table_ref[s, row : row + 1, :]
        ada_ref[:, at] = total
        bias_ref[:, at] = jnp.sum(table_ref[:, row, :], axis=0, keepdims=True)
    total = table_ref[0]
    for s in range(1, n_d):
        total += table_ref[s]
    sum_ref[...] = total
    for k, row in enumerate((S_SQ_A, S_SQ_M, S_SQ_R)):
        root_ref[k : k + 1] = jnp.broadcast_to(
            jnp.sqrt(jnp.sum(total[row : row + 1], axis=1, keepdims=True) / count),
            (1, root_ref.shape[1]),
        )


def finish_call(table, cond_t, count):
    features = table.shape[2]
    width = cond_t.shape[0]
    return pl.pallas_call(
        partial(finish_kernel, 0, count),
        name="finish",
        out_shape=[
            struct((width, 6 * features), F32),
            struct((1, 6 * features), F32),
            struct(table.shape[1:], F32),
            struct((3, 128), F32),
        ],
        in_specs=[VMEM] * 2,
        out_specs=[VMEM] * 4,
        compiler_params=params(),
        cost_estimate=cost(1e7, 4e6),
    )(table, cond_t)


def shards(
    block_input, condition, modulation_weight, modulation_bias, first_gain, qkv_weight, out_weight,
    second_gain, up_weight, up_bias, down_weight, down_bias, grad_output,
):
    n_t, n_d = lax.axis_size("tensor"), lax.axis_size("dp")
    rows, sequences, features = block_input.shape
    assert sequences == 1
    length = rows * n_t
    part, width = qkv_weight.shape[1:]
    units = up_weight.shape[1]
    assert units == features and n_t % CORES == 0 and n_d % INNER == 0
    cond_width = condition.shape[1]
    extra = -width % 128
    x = block_input.reshape(rows, features)
    g = grad_output.reshape(rows, features)

    pack = jnp.concatenate(
        [up_weight, down_weight.T, out_weight.T, jnp.zeros((part, extra), BF16)], axis=1
    )
    w_rest = lax.all_gather(pack, ("dp", "tensor"), axis=0, tiled=False)
    w_rest = w_rest.reshape(n_d, n_t, part, pack.shape[1])

    small = jnp.concatenate(
        [first_gain, second_gain, down_bias, up_bias]
    ).astype(F32)
    cond_at = -(-small.shape[0] // 128) * 128
    small = jnp.concatenate(
        [small, jnp.zeros((cond_at - small.shape[0],), F32), condition[0].astype(F32)]
    )[None]
    qkv = qkv_weight.transpose(1, 0, 2).reshape(part, 3 * width)
    x_all, w_qkv, small_all, mod_all = gather_call(
        x, qkv, small, modulation_weight, modulation_bias[None], cond_at, n_d, n_t
    )
    w_qkv = w_qkv.reshape(features, 3 * width)
    mod = mod_all.reshape(6, features)
    pick = lambda at, count: small_all[:, 0, at : at + count].reshape(-1, features)
    own = first_gain.shape[0]
    vecs = jnp.concatenate(
        [
            pick(0, own), mod[0:3], pick(own, own), mod[3:6], pick(2 * own, own),
            pick(3 * own, up_bias.shape[0]),
        ]
    )
    inverse = 10000.0 ** (-np.arange(HEAD_DIM // 2) * 2.0 / HEAD_DIM)
    angles = inverse[:, None] * np.arange(length)[None, :]
    cos, sin = jnp.asarray(np.cos(angles), F32), jnp.asarray(np.sin(angles), F32)

    attn_in, proj = project_call(x_all, w_qkv, vecs[:3], cos, sin)
    mix, lse = attend_call(proj)
    mix_own = swap_call(mix, n_t, 1)
    stat_rows = -(-(S_B_UP + n_t) // 8) * 8
    out, d_middle, d_mix, stat, grads = middle_call(
        mix_own, x, g, vecs, w_rest, n_d, n_t, stat_rows
    )
    g_rest = lax.psum_scatter(
        grads.reshape(n_d * n_t, part, pack.shape[1]), ("dp", "tensor"),
        scatter_dimension=0, tiled=False,
    ).astype(F32)
    d_mix_all = swap_call(d_mix, n_t, 2)
    d_proj = attend_back_call(proj, d_mix_all, mix, lse, cos, sin)
    shares, g_qkv = project_back_call(d_proj, attn_in, w_qkv, n_d)
    d_attn_in, g_qkv = reduce_call(shares, g_qkv, n_d, n_t)
    grad_input, stat = norm_back_call(x, d_attn_in, d_middle, vecs, stat)
    table, grad_cond = stat_call(stat, modulation_weight, n_d, n_t)
    cond_t = small_all[:, 0, cond_at:].T
    grad_ada, grad_ada_b, sums, roots = finish_call(table, cond_t, float(length * n_d * features))
    return (
        out.reshape(block_input.shape),
        grad_input.reshape(block_input.shape),
        grad_cond,
        grad_ada,
        grad_ada_b[0],
        sums[S_GAIN1],
        g_qkv.reshape(part, 3, width).transpose(1, 0, 2),
        g_rest[:, 2 * units : 2 * units + width].T,
        sums[S_GAIN2],
        g_rest[:, :units],
        sums[S_B_UP : S_B_UP + n_t].reshape(-1),
        g_rest[:, units : 2 * units].T,
        sums[S_B_DOWN],
        roots[:, 0],
    )


def solution(mesh):
    in_specs = (
        P("tensor", "dp", None),
        P("dp", None),
        P(None, "dp"),
        P("dp"),
        P("dp"),
        P(None, "dp", "tensor"),
        P("tensor", "dp"),
        P("dp"),
        P("dp", "tensor"),
        P("dp"),
        P("tensor", "dp"),
        P("dp"),
        P("tensor", "dp", None),
    )
    out_specs = (
        P("tensor", "dp", None),
        P("tensor", "dp", None),
        P("dp", None),
        P(),
        P(),
        P(),
        P(None, "dp", "tensor"),
        P("tensor", "dp"),
        P(),
        P("dp", "tensor"),
        P(),
        P("tensor", "dp"),
        P(),
        P(),
    )
    return jax.shard_map(shards, mesh=mesh, in_specs=in_specs, out_specs=out_specs, check_vma=False)
```

time: 1210 us -> 315 us (0.26)
  waiting for transfers between devices: 643 us -> 20.5 us
  Pallas kernels: 58.6 us -> 246 us
  blocking collectives: 175 us -> 0 us
  matrix products: 160 us -> 0 us
  other arithmetic: 77 us -> 3.8 us
  local copies, waits for them, and re-layouts: 61.4 us -> 24.7 us
  loops' own time: 15.9 us -> 0 us
    reduce_scatter x6 -> x1, waiting for transfers between devices: 290 us -> 7.67 us  [shards(): lax.psum_scatter(grads.reshape(n_d * n_t, part, pack.shape[1]), ('dp', 't...]
    pallas_call x0 -> x12, Pallas kernels: none -> 246 us  [the longest x1 38.1 us: attend_back_call(): pl.pallas_call(partial(attend_back_kernel, heads), name='attend_back', gr...]
    dot_general x36 -> x0, matrix products: 151 us -> none  [the longest x4 22.8 us: backward_block(): jnp.einsum('hqk,hke->hqe', d_scores, key_seq, preferred_element_type=jnp....]
    psum x1 -> x0, waiting for transfers between devices: 140 us -> none  [shards(): lax.psum((local_squares, cond_table, d_ada_w, d_ada_b, d_gain_one, d_gain...]
    all_gather x7 -> x1, waiting for transfers between devices: 123 us -> 12.8 us  [shards(): w_rest = lax.all_gather(pack, ('dp', 'tensor'), axis=0, tiled=False)]
    all_gather x3 -> x0, blocking collectives: 94.2 us -> none  [the longest x1 34.8 us: shards(): lax.all_gather(qkv_weight, 'dp', axis=1, tiled=True)]
    unnamed x18 -> x2, waiting for transfers between devices: 89.6 us -> 0.03 us
    dot_general x4 -> x0, Pallas kernels: 58.6 us -> none  [forward_block(): jnp.einsum('hqk,hke->hqe', probs, value_seq, preferred_element_type=jnp.f...]
  transfers between devices with their start and end apart: 16 -> 2, of which waited for: 14 -> 2; matrix products, arithmetic and copies ran while one was open for 9% -> 7% of each run, Pallas kernels for 0% -> 70%
where the time goes in v1:
time: 315 us; the launch traced here: 309 us
  Pallas kernels  246 us (78%)
  local copies, waits for them, and re-layouts  24.7 us (8%)
  waiting for transfers between devices  20.5 us (7%)
  between operations  14.4 us (5%)
  other arithmetic  3.8 us (1%)
    pallas_call x1, Pallas kernels, attend_back_call(): pl.pallas_call(partial(attend_back_kernel, heads), name='attend_back', gr...  38.1 us
    pallas_call x1, Pallas kernels, reduce_call(): pl.pallas_call(partial(reduce_kernel, n_d, n_t, parts), name='reduce_part...  37 us
    pallas_call x1, Pallas kernels, gather_call(): pl.pallas_call(partial(gather_kernel, n_d, n_t, parts, cond_at), name='ga...  36.8 us
    pallas_call x1, Pallas kernels, stat_call(): pl.pallas_call(partial(stat_kernel, n_d, n_t), name='gather_statistics',...  33.8 us
    pallas_call x1, Pallas kernels, middle_call(): pl.pallas_call(partial(middle_kernel, n_d, n_t), name='middle', out_shape...  29.1 us
    pallas_call x2, Pallas kernels, swap_call(): pl.pallas_call(partial(swap_kernel, n_t), name='swap_blocks', out_shape=s...  24.2 us
    pallas_call x1, Pallas kernels, attend_call(): pl.pallas_call(partial(attend_kernel, heads), name='attend', grid=(blocks...  22.2 us
    all_gather x1, waiting for transfers between devices, shards(): w_rest = lax.all_gather(pack, ('dp', 'tensor'), axis=0, tiled=False)  12.8 us
  transfers between devices with their start and end apart: 2, of which 2 were waited for; matrix products, arithmetic and copies ran while one was open for 7% of the time, Pallas kernels for 70%

profile of v1, /device:TPU:0, one launch (start us, length us, event | category | flops | bytes accessed | tf_op | source)
XLA Modules:
  0.0 309.4 jit_solution(15348816693056122533)
XLA Ops:
  7.2 0.0 all-gather.3.cloned.1.call-start
  7.2 0.9 copy.40
  8.1 1.8 concatenate.19
  9.9 0.0 all-gather.3.cloned.1.call-update
  10.0 0.0 reduce-scatter.2.cloned.1.call-start
  10.0 1.7 copy.39.ada_ref
  11.7 1.1 copy.37
  12.8 0.8 copy.38.w_ref
  13.6 0.8 maximum_convert_fusion
  14.4 0.7 bitcast_convert_fusion.1
  15.0 0.1 pad_maximum_fusion.1
  15.1 0.6 broadcast_in_dim.13.small_ref
  15.7 1.3 broadcast_in_dim.14.ada_b_ref
  17.0 36.8 %gather_tokens.1 = (bf16[4,512,768]{2,1,0:T(8,128)(2,1)}, bf16[8,96,576]{2,1,0:T(8,128)(2,1)}, f32[8,1,896]{2,1,0:T(1,128)}, f32[8,1,576]{2,1,0:T(1,128)}) custom-call(bf16[512,768]{1,0:T(8,128)(2,1)} %bitcast.30, bf16[96,576]{1,0:T(8,128)(2,1)} %copy.38.w_ref, f32[1,896]{1,0:T(1,128)} %broadcast_in_dim.13.small_ref, bf16[128,576]{1,0:T(8,128)(2,1)} %copy.39.ada_ref, ...), custom_call_target="tpu_custom_call" | custom-call | flops 1000000 | bytes 60000000 | tf_op jit(solution)/shard_map/gather_tokens/pallas_call | solution.py:171
  53.7 0.9 slice_reduce_fusion.3
  54.6 0.1 reshape_squeeze.12
  54.7 0.1 reshape_squeeze.13
  54.8 0.1 reshape_squeeze.14
  54.8 0.8 slice_reduce_fusion.1
  55.6 0.1 slice.57
  55.7 0.8 slice_reduce_fusion
  56.5 0.1 slice.61
  56.6 0.6 pad_maximum_fusion.vec_ref
  57.2 7.1 %project.1 = (bf16[4,512,768]{2,1,0:T(8,128)(2,1)}, bf16[4,576,512]{2,1,0:T(8,128)(2,1)}) custom-call(bf16[4,512,768]{2,1,0:T(8,128)(2,1)} %get-tuple-element.39.x_ref, bf16[768,576]{1,0:T(8,128)(2,1)} %bitcast.41, f32[3,768]{1,0:T(4,128)} %pad_maximum_fusion.vec_ref, f32[32,2048]{1,0:T(8,128)} %constant.8.clone.cos_ref, f32[32,2048]{1,0:T(8,128)} %constant.9.clone.sin_ref), custom_call_target="tpu_custom_call" | custom-call | flops 1811939328 | bytes 12000000 | tf_op jit(solution)/shard_map/project/pallas_call | solution.py:220
  64.3 22.2 %attend.1 = (bf16[4,192,512]{2,1,0:T(8,128)(2,1)}, f32[4,3,512]{2,1,0:T(4,128)}) custom-call(bf16[4,576,512]{2,1,0:T(8,128)(2,1)} %get-tuple-element.43.proj_ref), custom_call_target="tpu_custom_call" | custom-call | flops 12884901888 | bytes 4000000 | tf_op jit(solution)/shard_map/attend/pallas_call | solution.py:273
  86.5 14.5 %swap_blocks.2.mix_ref = bf16[4,192,512]{2,1,0:T(8,128)(2,1)} custom-call(bf16[4,192,512]{2,1,0:T(8,128)(2,1)} %get-tuple-element.44.src_ref.mix_ref), custom_call_target="tpu_custom_call" | custom-call | bytes 30000000 | tf_op jit(solution)/shard_map/swap_blocks/pallas_call | solution.py:310
  101.0 1.3 concatenate.18.vec_ref
  102.2 12.8 %all-gather.3.cloned.1.call-done = bf16[3072,1792]{1,0:T(8,128)(2,1)} async-done(((bf16[96,1792]{1,0:T(8,128)(2,1)}), bf16[3072,1792]{1,0:T(8,128)(2,1)}) %all-gather.3.cloned.1.call-update) | async-done | bytes 11010064 | tf_op jit(solution)/shard_map/all_gather | solution.py:867
  115.0 29.1 %middle.1 = (bf16[512,768]{1,0:T(8,128)(2,1)}, f32[512,768]{1,0:T(8,128)}, bf16[4,192,512]{2,1,0:T(8,128)(2,1)}, f32[16,768]{1,0:T(8,128)}, bf16[8,4,96,1792]{3,2,1,0:T(8,128)(2,1)}) custom-call(bf16[4,192,512]{2,1,0:T(8,128)(2,1)} %swap_blocks.2.mix_ref, bf16[512,768]{1,0:T(8,128)(2,1)} %bitcast.31, bf16[512,768]{1,0:T(8,128)(2,1)} %bitcast.43, ...), custom_call_target="tpu_custom_call" | custom-call | flops 16911433728 | bytes 30000000 | tf_op jit(solution)/shard_map/middle/pallas_call | solution.py:449
  144.1 0.0 copy-start.1
  144.2 0.0 reduce-scatter.2.cloned.1.call-update
  144.2 0.7 copy-done.1
  144.9 0.2 copy.42
  145.1 0.6 slice_bitcast_fusion.2.cond_ref
  145.7 9.7 %swap_blocks.3.dmix_ref = bf16[4,192,512]{2,1,0:T(8,128)(2,1)} custom-call(bf16[4,192,512]{2,1,0:T(8,128)(2,1)} %get-tuple-element.46.src_ref), custom_call_target="tpu_custom_call" | custom-call | bytes 30000000 | tf_op jit(solution)/shard_map/swap_blocks/pallas_call | solution.py:310
  155.5 38.1 %attend_back.1.dproj_ref = bf16[4,576,512]{2,1,0:T(8,128)(2,1)} custom-call(bf16[4,576,512]{2,1,0:T(8,128)(2,1)} %get-tuple-element.43.proj_ref, bf16[4,192,512]{2,1,0:T(8,128)(2,1)} %swap_blocks.3.dmix_ref, bf16[4,192,512]{2,1,0:T(8,128)(2,1)} %get-tuple-element.44.src_ref.mix_ref, f32[4,3,512]{2,1,0:T(4,128)} %get-tuple-element.47.lse_ref, ...), custom_call_target="tpu_custom_call" | custom-call | flops 32212254720 | bytes 6000000 | tf_op jit(solution)/shard_map/attend_back/pallas_call | solution.py:542
  193.6 9.3 %project_back.1 = (bf16[4,512,768]{2,1,0:T(8,128)(2,1)}, bf16[8,96,576]{2,1,0:T(8,128)(2,1)}) custom-call(bf16[4,576,512]{2,1,0:T(8,128)(2,1)} %attend_back.1.dproj_ref, bf16[4,512,768]{2,1,0:T(8,128)(2,1)} %get-tuple-element.48.in_ref, bf16[768,576]{1,0:T(8,128)(2,1)} %bitcast.42), custom_call_target="tpu_custom_call" | custom-call | flops 3623878656 | bytes 12000000 | tf_op jit(solution)/shard_map/project_back/pallas_call | solution.py:580
  202.9 37.0 %reduce_parts.1 = (f32[512,768]{1,0:T(8,128)}, f32[96,576]{1,0:T(8,128)}) custom-call(bf16[4,512,768]{2,1,0:T(8,128)(2,1)} %get-tuple-element.49.part_ref, bf16[4,2,96,576]{3,2,1,0:T(8,128)(2,1)} %bitcast.35), custom_call_target="tpu_custom_call" | custom-call | flops 1000000 | bytes 60000000 | tf_op jit(solution)/shard_map/reduce_parts/pallas_call | solution.py:682
  239.8 4.4 %norm_back.1 = (f32[512,768]{1,0:T(8,128)}, f32[16,768]{1,0:T(8,128)}) custom-call(bf16[512,768]{1,0:T(8,128)(2,1)} %bitcast.32, f32[512,768]{1,0:T(8,128)} %get-tuple-element.51.e_ref, f32[512,768]{1,0:T(8,128)} %get-tuple-element.52.dmid_ref, f32[13,768]{1,0:T(8,128)} %concatenate.18.vec_ref, f32[16,768]{1,0:T(8,128)} %get-tuple-element.53.stat_in_ref), custom_call_target="tpu_custom_call" | custom-call | flops 7864320 | bytes 8000000 | tf_op jit(solution)/shard_map/norm_back/pallas_call | solution.py:722
  244.3 0.0 copy-start
  244.3 33.8 %gather_statistics.1 = (f32[8,16,768]{2,1,0:T(8,128)}, f32[1,128]{1,0:T(1,128)}) custom-call(f32[16,768]{1,0:T(8,128)} %get-tuple-element.55.stat_ref, bf16[128,576]{1,0:T(8,128)(2,1)} %copy.39.ada_ref), custom_call_target="tpu_custom_call" | custom-call | flops 1000000 | bytes 20000000 | tf_op jit(solution)/shard_map/gather_statistics/pallas_call | solution.py:787
  278.1 4.1 %finish.1 = (f32[128,4608]{1,0:T(8,128)}, f32[1,4608]{1,0:T(1,128)}, f32[16,768]{1,0:T(8,128)}, f32[3,128]{1,0:T(4,128)}) custom-call(f32[8,16,768]{2,1,0:T(8,128)} %get-tuple-element.57.table_ref, f32[128,8]{1,0:T(8,128)} %slice_bitcast_fusion.2.cond_ref), custom_call_target="tpu_custom_call" | custom-call | flops 10000000 | bytes 4000000 | tf_op jit(solution)/shard_map/finish/pallas_call | solution.py:832
  282.1 0.0 copy-start.2
  282.1 0.0 copy-start.3
  282.1 0.8 slice.69
  282.9 0.6 reshape.78
  283.5 4.2 %copy.44 = f32[512,1,768]{2,1,0:T(1,128)} copy(f32[512,1,768]{2,0,1:T(8,128)} %bitcast.33) | data formatting | bytes 3145728
  287.8 0.0 copy-start.4
  287.8 0.0 copy-done
  287.8 0.1 copy.43
  287.9 0.9 copy.45
  288.8 0.0 copy-done.2
  288.8 0.7 reduce.6
  289.4 0.0 copy-done.3
  289.4 0.6 slice_reduce_fusion.9
  290.1 1.4 slice_reduce_fusion.6
  291.5 7.7 %reduce-scatter.2.cloned.1.call-done = bf16[1,96,1792]{2,1,0:T(8,128)(2,1)} async-done(((bf16[32,96,1792]{2,1,0:T(8,128)(2,1)}), bf16[1,96,1792]{2,1,0:T(8,128)(2,1)}) %reduce-scatter.2.cloned.1.call-update) | async-done | bytes 344080 | tf_op jit(solution)/shard_map/reduce_scatter | solution.py:902
  299.2 1.0 bitcast_convert_fusion
  300.2 0.9 slice_bitcast_fusion
  301.1 0.7 copy.46
  301.8 0.0 copy-done.4
  301.8 0.5 copy.48
  (4 shorter events, 0.0 us)
Async XLA Ops:
  7.2 107.8 %all-gather.3.cloned.1.call-start = ((), (), s32[]{:S(2)}) async-start(), calls=%async_computation.2 | async-start | bytes 11354112 | tf_op jit(solution)/shard_map/all_gather | solution.py:867
  10.0 289.2 %reduce-scatter.2.cloned.1.call-start = ((), (), s32[]{:S(2)}) async-start(), calls=%async_computation.1 | async-start | bytes 11354112 | tf_op jit(solution)/shard_map/reduce_scatter | solution.py:902
  144.1 0.7 copy-start.1
  244.3 43.5 %copy-start = (f32[96,576]{1,0:T(8,128)S(1)}, f32[96,576]{1,0:T(8,128)}, u32[]{:S(2)}) copy-start(f32[96,576]{1,0:T(8,128)} %get-tuple-element.61) | copy-start | bytes 663556
  282.1 6.6 %copy-start.2 = (f32[1,4608]{1,0:T(1,128)S(1)}, f32[1,4608]{1,0:T(1,128)}, u32[]{:S(2)}) copy-start(f32[1,4608]{1,0:T(1,128)} %get-tuple-element.59) | copy-start | bytes 55300
  282.1 7.3 %copy-start.3 = (f32[3,128]{1,0:T(4,128)S(1)}, f32[3,128]{1,0:T(4,128)}, u32[]{:S(2)}) copy-start(f32[3,128]{1,0:T(4,128)} %get-tuple-element.63) | copy-start | bytes 4612
  287.8 14.1 %copy-start.4 = (f32[1,128]{1,0:T(1,128)S(1)}, f32[1,128]{1,0:T(1,128)}, u32[]{:S(2)}) copy-start(f32[1,128]{1,0:T(1,128)} %get-tuple-element.118) | copy-start | bytes 1540
Sparse Core Ops, SparseCore 0:
  11.5 103.4 all-gather.2
  144.3 154.8 reduce-scatter.1

commit v2 on v1

v2 whole, which is shorter than its diff:
```python
from functools import partial

import jax
import jax.numpy as jnp
import numpy as np
from jax import lax
from jax.experimental import pallas as pl
from jax.experimental.pallas import tpu as pltpu
from jax.sharding import PartitionSpec as P

HEAD_DIM = 64
EPSILON = 1e-05
CORES = 2
INNER = 2
MESH = pl.DeviceIdType.MESH
VMEM_LIMIT = 58 << 20
GELU_C = float(np.sqrt(2.0 / np.pi))
GELU_A = 0.044715
F32 = jnp.float32
BF16 = jnp.bfloat16
ANY = pl.BlockSpec(memory_space=pl.ANY)
VMEM = pl.BlockSpec(memory_space=pltpu.VMEM)
DMA = pltpu.SemaphoreType.DMA


def dot(lhs, rhs, lhs_dim, rhs_dim):
    return lax.dot_general(
        lhs, rhs, (((lhs_dim,), (rhs_dim,)), ((), ())), preferred_element_type=F32
    )


def params(collective_id=None, **more):
    if collective_id is not None:
        more.update(collective_id=collective_id, has_side_effects=True)
    return pltpu.CompilerParams(vmem_limit_bytes=VMEM_LIMIT, **more)


def cost(flops, moved, special=0):
    return pl.CostEstimate(flops=int(flops), bytes_accessed=int(moved), transcendentals=int(special))


def struct(shape, dtype):
    return jax.ShapeDtypeStruct(shape, dtype)


def mean_rows(values):
    return jnp.mean(values, axis=-1, keepdims=True)


def sum_tokens(values):
    return jnp.sum(values, axis=0, keepdims=True)


GAIN1, SHIFT_A, SCALE_A, GATE_A, GAIN2, SHIFT_M, SCALE_M, GATE_M, B_DOWN, B_UP = range(10)
MOD_ROWS = (SHIFT_A, SCALE_A, GATE_A, SHIFT_M, SCALE_M, GATE_M)
S_GATE_A, S_SHIFT_M, S_SCALE_M, S_GATE_M, S_GAIN2, S_B_DOWN, S_SQ_A, S_SQ_M, S_SQ_R, S_B_UP = range(10)
L_SHIFT_A, L_SCALE_A, L_GAIN1 = range(3)


def order(k, xi, ci, nx):
    return lax.rem(xi + k // CORES, nx) * CORES + lax.rem(ci + k % CORES, CORES)


def mirror(k, nx):
    return (nx - k // CORES) % nx * CORES + (CORES - k % CORES) % CORES


def place(n_d, n_t):
    d, t = lax.axis_index("dp"), lax.axis_index("tensor")
    return d, t, d // INNER, lax.rem(d, INNER), t // CORES, lax.rem(t, CORES)


def greet(n_d, n_t):
    d, t = lax.axis_index("dp"), lax.axis_index("tensor")
    barrier = pltpu.get_barrier_semaphore()
    for r in range(1, n_t):
        pl.semaphore_signal(
            barrier, 1, device_id=(d, lax.rem(t + r, n_t)), device_id_type=MESH
        )
    for r in range(1, n_d):
        pl.semaphore_signal(
            barrier, 1, device_id=(lax.rem(d + r, n_d), t), device_id_type=MESH
        )
    pl.semaphore_wait(barrier, n_t - 1 + n_d - 1)


def remote(src, dst, send, recv, d, t):
    return pltpu.make_async_remote_copy(
        src_ref=src, dst_ref=dst, send_sem=send, recv_sem=recv, device_id=(d, t), device_id_type=MESH
    )

def front_kernel(
    n_d, n_t, parts, heads, cond_at, bias_at, sizes, chunks, plan, hand,
    x_ref, qkv_ref, small_ref, ada_ref, up_ref, down_ref, outw_ref, cos_ref, sin_ref,
    in_all, proj_ref, mix_ref, lse_ref, mix_own, vec_ref, cond_ref, w_all, w_up, w_down, w_out,
    x_all, w_pack, wt_ref, out_pack, small_all, mod_all, mod_rows, key_ref,
    s_x, r_x, s_c, r_c, s_f, r_f, s_z, r_z, s_y, r_y, s_s, r_s, s_m, r_m, s_l,
    s_w, r_w, s_k, r_k, s_o, r_o,
):
    d, t, oi, ii, xi, ci = place(n_d, n_t)
    nx, no = n_t // CORES, n_d // INNER
    other = xi * CORES + (1 - ci)
    piece = x_ref.shape[0] // parts
    rows, features = x_ref.shape
    width = qkv_ref.shape[2]
    half = HEAD_DIM // 2
    for j in range(3):
        w_pack[:, j * width : (j + 1) * width] = qkv_ref[j]
    out_pack[:, :width] = outw_ref[...].T
    if out_pack.shape[1] > width:
        out_pack[:, width:] = jnp.zeros((out_pack.shape[0], out_pack.shape[1] - width), BF16)
    greet(n_d, n_t)
    s_copies = []
    for r in range(1, n_d):
        copy = remote(
            small_ref, small_all.at[d], s_s.at[r - 1], r_s.at[r - 1], lax.rem(d + r, n_d), t
        )
        copy.start()
        s_copies.append(copy)
    x_copies = []
    for r in range(1, nx):
        peer = lax.rem(xi + r, nx) * CORES + ci
        for p in range(parts):
            at = pl.ds(p * piece, piece)
            copy = remote(
                x_ref.at[at], x_all.at[t, at], s_x.at[r - 1, p], r_x.at[r - 1, p], d, peer
            )
            copy.start()
            x_copies.append((r, p, copy))
    z_copies = []
    for r in range(1, no):
        copy = remote(
            w_pack, w_all.at[d], s_z.at[r - 1], r_z.at[r - 1], lax.rem(oi + r, no) * INNER + ii, t
        )
        copy.start()
        z_copies.append(copy)
    y_copies = []
    for q in range(1, INNER):
        copy = remote(
            w_pack, w_all.at[d], s_y.at[q - 1, 0], r_y.at[q - 1, 0],
            oi * INNER + lax.rem(ii + q, INNER), t,
        )
        copy.start()
        y_copies.append(copy)
    core_copy = remote(x_ref, x_all.at[t], s_c, r_c, d, other)
    core_copy.start()
    local = []
    for n, (src, dst) in enumerate(
        (
            (small_ref, small_all.at[d]),
            (x_ref, x_all.at[t]),
            (w_pack, w_all.at[d]),
            (up_ref, w_up.at[oi, ii, xi, ci]),
            (down_ref, w_down.at[oi, ii, xi, ci]),
            (out_pack, w_out.at[oi, ii, xi, ci]),
        )
    ):
        copy = pltpu.make_async_copy(src, dst, s_l.at[n])
        copy.start()
        local.append(copy)

    every = slice(None)
    axes = {"z": (0, no), "y": (1, INNER), "x": (2, nx)}
    me = (oi, ii, xi)
    arrays = (w_up, w_down, w_out)
    sources = (up_ref, down_ref, out_pack)
    flights = {}
    k_copies = []

    def launch(c, s):
        which, lanes, path = chunks[c]
        array = arrays[which]
        spot = [oi, ii, xi, ci, every, lanes]
        for axis in path[:s]:
            spot[axes[axis][0]] = every
        dim, count = axes[path[s]]
        flights[c, s] = []
        for r in range(1, count):
            peer = list(me)
            peer[dim] = lax.rem(me[dim] + r, count)
            src = sources[which].at[:, lanes] if s == 0 else array.at[tuple(spot)]
            flights[c, s].append(
                remote(
                    src, array.at[tuple(spot)], s_w.at[3 * c + s, r - 1], r_w.at[3 * c + s, r - 1],
                    peer[0] * INNER + peer[1], peer[2] * CORES + ci,
                )
            )
        return flights[c, s]

    def hand_over(c, s):
        which, lanes, path = chunks[c]
        array = arrays[which]
        spot = [oi, ii, xi, ci, every, lanes]
        for axis in path[: min(s, 2)]:
            spot[axes[axis][0]] = every
        dim, count = axes[path[2]]
        copies = []
        for r in range(1, count) if s == 3 else (0,):
            spot[dim] = lax.rem(me[dim] + r, count)
            n = c * hand + (r if s == 3 else 0)
            copies.append(
                remote(
                    array.at[tuple(spot)], array.at[tuple(spot)], s_k.at[n], r_k.at[n], d, other
                )
            )
        k_copies.extend(copies)
        return copies

    for s in range(3):
        for c in range(len(chunks)):
            launch(c, s)
    given = {(c, s): hand_over(c, s) for s in (2, 3) for c in range(len(chunks))}

    def advance(c, s):
        for copy in flights[c, s]:
            copy.wait()
        if s < 2:
            for copy in flights[c, s + 1]:
                copy.start()
        for copy in given.get((c, s + 1), ()):
            copy.start()

    for c in range(len(chunks)):
        for copy in flights[c, 0]:
            copy.start()

    local[0].wait()
    for copy in s_copies:
        copy.wait()
    cond = small_all[:, 0, cond_at : cond_at + ada_ref.shape[1]]
    for s in range(n_d):
        cond_ref[:, s : s + 1] = cond[s : s + 1].T
    bias = small_ref[:, bias_at : bias_at + ada_ref.shape[0]]
    mod_rows[:, 0, :] = dot(cond.astype(BF16), ada_ref[...], 1, 1) + bias
    own_mod = pltpu.make_async_copy(mod_rows.at[d], mod_all.at[d], s_l.at[6])
    own_mod.start()
    m_copies = []
    for r in range(1, n_d):
        peer = lax.rem(d + r, n_d)
        copy = remote(mod_rows.at[peer], mod_all.at[d], s_m.at[r - 1], r_m.at[r - 1], peer, t)
        copy.start()
        m_copies.append(copy)
    for r in range(1, no):
        z_copies[r - 1].wait()
        origin = lax.rem(oi + no - r, no) * INNER + ii
        for q in range(1, INNER):
            copy = remote(
                w_all.at[origin], w_all.at[origin], s_y.at[q - 1, r], r_y.at[q - 1, r],
                oi * INNER + lax.rem(ii + q, INNER), t,
            )
            copy.start()
            y_copies.append(copy)
    f_copies = []
    for r, p, copy in x_copies:
        copy.wait()
        origin = lax.rem(xi + nx - r, nx) * CORES + ci
        at = pl.ds(p * piece, piece)
        copy = remote(
            x_all.at[origin, at], x_all.at[origin, at],
            s_f.at[r - 1, p], r_f.at[r - 1, p], d, other,
        )
        copy.start()
        f_copies.append(copy)

    for copy in m_copies + [own_mod]:
        copy.wait()
    def put(first, piece_of, count):
        for s in range(n_d):
            value = piece_of(s)
            start = s * count
            done = 0
            while done < count:
                row, column = divmod(start + done, features)
                take = min(count - done, features - column)
                vec_ref[first + row : first + row + 1, column : column + take] = value[
                    :, done : done + take
                ]
                done += take

    vec_ref[...] = jnp.zeros_like(vec_ref)
    at = 0
    for first, count in sizes:
        put(first, lambda s: small_all[s, :, at : at + count], count)
        at += count
    columns = ada_ref.shape[0]
    for s in range(n_d):
        done = 0
        while done < columns:
            row, column = divmod(s * columns + done, features)
            take = min(columns - done, features - column)
            row = MOD_ROWS[row]
            vec_ref[row : row + 1, column : column + take] = mod_all[s, :, done : done + take]
            done += take

    for copy in y_copies + f_copies + local[1:3] + [core_copy]:
        copy.wait()
    wt_ref[...] = w_all[...].reshape(features, 3 * width).T

    for copy in local[3:]:
        copy.wait()
    for step in plan[0]:
        advance(*step)

    def project(b, carry):
        x = x_all[b].astype(F32)
        centred = x - mean_rows(x)
        normed = centred * lax.rsqrt(mean_rows(centred * centred) + EPSILON)
        normed = normed * vec_ref[GAIN1 : GAIN1 + 1]
        low = (normed * (1.0 + vec_ref[SCALE_A : SCALE_A + 1]) + vec_ref[SHIFT_A : SHIFT_A + 1])
        low = low.astype(BF16)
        in_all[b] = low
        proj = dot(wt_ref[...], low, 1, 1)
        lanes = pl.ds(pl.multiple_of(b * rows, rows), rows)
        cos, sin = cos_ref[:, lanes], sin_ref[:, lanes]
        for j in range(2):
            factor = HEAD_DIM**-0.5 if j == 0 else 1.0
            for h in range(heads):
                at = j * width + h * HEAD_DIM
                first, last = proj[at : at + half], proj[at + half : at + HEAD_DIM]
                top = ((first * cos - last * sin) * factor).astype(BF16)
                bottom = ((last * cos + first * sin) * factor).astype(BF16)
                proj_ref[b, at : at + half] = top
                proj_ref[b, at + half : at + HEAD_DIM] = bottom
                if j == 1:
                    key_ref[h, lanes, :] = jnp.concatenate([top, bottom], axis=0).T
        proj_ref[b, 2 * width :] = proj[2 * width :].astype(BF16)
        return carry

    lax.fori_loop(0, n_t, project, 0)

    def attend(k, carry):
        shift = n_t - 1 - k
        b = lax.rem(xi + shift // CORES, nx) * CORES + lax.rem(ci + lax.rem(shift, CORES), CORES)
        for h in range(heads):
            at = h * HEAD_DIM
            scores = dot(key_ref[h], proj_ref[b, at : at + HEAD_DIM], 1, 0)
            top = jnp.max(scores, axis=0, keepdims=True)
            grown = jnp.exp(scores - top)
            total = jnp.sum(grown, axis=0, keepdims=True)
            low = grown.astype(BF16)
            mixed = jnp.zeros((HEAD_DIM, rows), F32)
            for v in range(n_t):
                value = proj_ref[v, 2 * width + at : 2 * width + at + HEAD_DIM]
                mixed += dot(value, low[v * rows : (v + 1) * rows], 1, 0)
            mix_ref[b, at : at + HEAD_DIM] = (mixed / total).astype(BF16)
            lse_ref[b, h : h + 1] = top + jnp.log(total)
        for m in range(1, n_t):
            @pl.when(k == n_t - 1 - m)
            def _(m=m):
                o_copies[m].start()

        for n in range(1, n_t):
            if n < len(plan) - 1 and plan[n]:
                @pl.when(k == n - 1)
                def _(n=n):
                    for step in plan[n]:
                        advance(*step)

        return carry

    o_copies = {}
    for m in range(1, n_t):
        b = order(m, xi, ci, nx)
        o_copies[m] = remote(
            mix_ref.at[b], mix_own.at[t], s_o.at[m - 1], r_o.at[mirror(m, nx) - 1], d, b
        )
    lax.fori_loop(0, n_t, attend, 0)
    mine = pltpu.make_async_copy(mix_ref.at[t], mix_own.at[t], s_l.at[7])
    mine.start()
    for step in plan[-1]:
        advance(*step)
    mine.wait()
    for copy in list(o_copies.values()) + k_copies:
        copy.wait()


def front_call(x, qkv, small, ada_t, up, down_t, outw, cos, sin, cond_at, bias_at, sizes, n_d, n_t):
    parts = 4
    nx, no = n_t // CORES, n_d // INNER
    rows, features = x.shape
    part, width = qkv.shape[1:]
    heads = width // HEAD_DIM
    length = rows * n_t
    wide = -(-width // 128) * 128
    units = up.shape[1]
    steps = max(no, INNER, nx) - 1
    hand = max(no, INNER, nx)
    cut = units // 2
    low, high = slice(0, cut), slice(cut, units)
    chunks = (
        (0, low, "zyx"), (1, low, "xzy"), (0, high, "zyx"), (1, high, "xzy"),
        (2, slice(0, wide), "yzx"),
    )
    plan = (
        [(1, 0), (3, 0), (4, 0), (0, 0), (2, 0)],
        [(0, 1), (1, 1)],
        [(2, 1), (4, 1)],
        [(3, 1)],
        [(4, 2), (0, 2), (1, 2), (2, 2), (3, 2)],
    )
    grid_of = (no, INNER, nx, CORES, part)
    columns = ada_t.shape[0]
    return pl.pallas_call(
        partial(front_kernel, n_d, n_t, parts, heads, cond_at, bias_at, sizes, chunks, plan, hand),
        name="front",
        out_shape=[
            struct((n_t, rows, features), BF16),
            struct((n_t, 3 * width, rows), BF16),
            struct((n_t, width, rows), BF16),
            struct((n_t, heads, rows), F32),
            struct((n_t, width, rows), BF16),
            struct((16, features), F32),
            struct((ada_t.shape[1], n_d), F32),
            struct((n_d, part, 3 * width), BF16),
            struct(grid_of + (units,), BF16),
            struct(grid_of + (units,), BF16),
            struct(grid_of + (wide,), BF16),
        ],
        in_specs=[VMEM, VMEM, VMEM, VMEM, ANY, ANY, VMEM, VMEM, VMEM],
        out_specs=[VMEM] * 8 + [ANY] * 3,
        scratch_shapes=[
            pltpu.VMEM((n_t, rows, features), BF16),
            pltpu.VMEM((part, 3 * width), BF16),
            pltpu.VMEM((3 * width, features), BF16),
            pltpu.VMEM((part, wide), BF16),
            pltpu.VMEM((n_d,) + small.shape, F32),
            pltpu.VMEM((n_d, 1, columns), F32),
            pltpu.VMEM((n_d, 1, columns), F32),
            pltpu.VMEM((heads, length, HEAD_DIM), BF16),
            DMA((nx - 1, parts)), DMA((nx - 1, parts)), DMA, DMA,
            DMA((nx - 1, parts)), DMA((nx - 1, parts)),
            DMA((no - 1,)), DMA((no - 1,)),
            DMA((INNER - 1, no)), DMA((INNER - 1, no)),
            DMA((n_d - 1,)), DMA((n_d - 1,)), DMA((n_d - 1,)), DMA((n_d - 1,)),
            DMA((8,)),
            DMA((3 * len(chunks), steps)), DMA((3 * len(chunks), steps)),
            DMA((len(chunks) * hand,)), DMA((len(chunks) * hand,)),
            DMA((n_t - 1,)), DMA((n_t - 1,)),
        ],
        compiler_params=params(0),
        cost_estimate=cost(20 * heads * length * length * HEAD_DIM, 40e6, heads * length * length),
    )(x, qkv, small, ada_t, up, down_t, outw, cos, sin)


def middle_kernel(
    mix_ref, x_ref, g_ref, vec_ref, up_ref, down_ref, wout_ref,
    out_ref, dmid_ref, dmix_ref, stat_ref, gup_ref, gdown_ref, gout_ref,
    up_buf, down_buf, o_buf, gu_buf, gd_buf, go_buf,
    mid_ref, attn_ref, low_ref, lowt_ref, dl_ref, dlt_ref, acc_out, acc_in, s_u, s_d, s_o, s_gu, s_gd,
):
    rows, features = x_ref.shape
    n_d, n_t = up_ref.shape[:2]
    width = mix_ref.shape[1]
    units = up_ref.shape[3]
    wide = wout_ref.shape[3]
    load_out = pltpu.make_async_copy(wout_ref, o_buf, s_o)
    load_up = lambda b: pltpu.make_async_copy(up_ref.at[:, b], up_buf.at[b], s_u.at[b])
    load_down = lambda b: pltpu.make_async_copy(down_ref.at[:, b], down_buf.at[b], s_d.at[b])
    keep_up = lambda b: pltpu.make_async_copy(gu_buf.at[b], gup_ref.at[:, b], s_gu.at[b])
    keep_down = lambda b: pltpu.make_async_copy(gd_buf.at[b], gdown_ref.at[:, b], s_gd.at[b])
    load_out.start()
    for b in range(n_t):
        load_up(b).start()
        load_down(b).start()
    vec = lambda row: vec_ref[row : row + 1]
    cot = g_ref[...].astype(F32)
    d_mlp = (vec(GATE_M) * cot).astype(BF16)
    dl_ref[...] = d_mlp
    dlt_ref[...] = d_mlp.T
    stat_ref[...] = jnp.zeros_like(stat_ref)
    stat_ref[S_B_DOWN : S_B_DOWN + 1] = sum_tokens(d_mlp.astype(F32))
    go_buf[...] = jnp.zeros_like(go_buf)
    load_out.wait()
    w_out = lambda b: o_buf[:, b].reshape(features, wide)[:, :width]
    attn_out = jnp.zeros((rows, features), F32)
    for b in range(n_t):
        attn_out += dot(mix_ref[b].T, w_out(b), 1, 1)
    attn_ref[...] = attn_out
    branch = vec(GATE_A) * attn_out
    stat_ref[S_SQ_A : S_SQ_A + 1] = sum_tokens(branch * branch)
    middle = x_ref[...].astype(F32) + branch
    mid_ref[...] = middle
    centred = middle - mean_rows(middle)
    inv = lax.rsqrt(mean_rows(centred * centred) + EPSILON)
    low = (centred * inv * vec(GAIN2) * (1.0 + vec(SCALE_M)) + vec(SHIFT_M)).astype(BF16)
    low_ref[...] = low
    lowt_ref[...] = low.T
    acc_out[...] = jnp.zeros_like(acc_out)
    acc_in[...] = jnp.zeros_like(acc_in)

    def block(b, carry):
        load_up(b).wait()
        load_down(b).wait()
        up = up_buf[b].reshape(features, units)
        down = down_buf[b].reshape(features, units)
        hidden = dot(low_ref[...], up, 1, 0) + vec_ref[pl.ds(B_UP + b, 1)]
        square = hidden * hidden
        bent = jnp.tanh(GELU_C * hidden * (1.0 + GELU_A * square))
        half = 0.5 * (1.0 + bent)
        active = (hidden * half).astype(BF16)
        slope = half + (0.5 * GELU_C) * hidden * (1.0 - bent * bent) * (
            1.0 + (3.0 * GELU_A) * square
        )
        acc_out[...] += dot(active, down, 1, 1)
        gd_buf[b] = dot(dlt_ref[...], active, 1, 0).astype(BF16).reshape(n_d, -1, units)
        keep_down(b).start()
        d_hidden = (dot(dl_ref[...], down, 1, 0) * slope).astype(BF16)
        stat_ref[pl.ds(S_B_UP + b, 1)] = sum_tokens(d_hidden.astype(F32))
        gu_buf[b] = dot(lowt_ref[...], d_hidden, 1, 0).astype(BF16).reshape(n_d, -1, units)
        keep_up(b).start()
        acc_in[...] += dot(d_hidden, up, 1, 1)
        return carry

    lax.fori_loop(0, n_t, block, 0)
    middle = mid_ref[...]
    mlp_out = acc_out[...] + vec(B_DOWN)
    mlp_branch = vec(GATE_M) * mlp_out
    result = middle + mlp_branch
    out_ref[...] = result.astype(BF16)
    cot = g_ref[...].astype(F32)
    stat_ref[S_SQ_M : S_SQ_M + 1] = sum_tokens(mlp_branch * mlp_branch)
    stat_ref[S_SQ_R : S_SQ_R + 1] = sum_tokens(result * result)
    stat_ref[S_GATE_M : S_GATE_M + 1] = sum_tokens(cot * mlp_out)
    e = acc_in[...]
    centred = middle - mean_rows(middle)
    inv = lax.rsqrt(mean_rows(centred * centred) + EPSILON)
    nhat = centred * inv
    gain, scale = vec(GAIN2), 1.0 + vec(SCALE_M)
    by_nhat = sum_tokens(e * nhat)
    stat_ref[S_SHIFT_M : S_SHIFT_M + 1] = sum_tokens(e)
    stat_ref[S_SCALE_M : S_SCALE_M + 1] = by_nhat * gain
    stat_ref[S_GAIN2 : S_GAIN2 + 1] = by_nhat * scale
    dn = e * (scale * gain)
    d_middle = cot + inv * (dn - mean_rows(dn) - nhat * mean_rows(dn * nhat))
    dmid_ref[...] = d_middle
    stat_ref[S_GATE_A : S_GATE_A + 1] = sum_tokens(d_middle * attn_ref[...])
    d_attn = (vec(GATE_A) * d_middle).astype(BF16)
    d_attn_t = d_attn.T
    for b in range(n_t):
        dmix_ref[b] = dot(d_attn, w_out(b), 1, 0).astype(BF16).T
        go_buf[:, b, :, :width] = (
            dot(d_attn_t, mix_ref[b], 1, 1).astype(BF16).reshape(n_d, -1, width)
        )
    copy = pltpu.make_async_copy(go_buf, gout_ref, s_o)
    copy.start()
    for b in range(n_t):
        keep_up(b).wait()
        keep_down(b).wait()
    copy.wait()


def middle_call(mix, x, g, vecs, w_up, w_down, w_out, stat_rows):
    rows, features = x.shape
    n_d, n_t, part, units = w_up.shape
    wide = w_out.shape[3]
    width = mix.shape[1]
    per = (n_t, n_d, part, units)
    return pl.pallas_call(
        middle_kernel,
        name="middle",
        out_shape=[
            struct((rows, features), BF16),
            struct((rows, features), F32),
            struct((n_t, width, rows), BF16),
            struct((stat_rows, features), F32),
            struct(w_up.shape, BF16),
            struct(w_down.shape, BF16),
            struct(w_out.shape, BF16),
        ],
        in_specs=[VMEM] * 4 + [ANY] * 3,
        out_specs=[VMEM] * 4 + [ANY] * 3,
        scratch_shapes=[
            pltpu.VMEM(per, BF16), pltpu.VMEM(per, BF16), pltpu.VMEM(w_out.shape, BF16),
            pltpu.VMEM(per, BF16), pltpu.VMEM(per, BF16), pltpu.VMEM(w_out.shape, BF16),
            pltpu.VMEM((rows, features), F32),
            pltpu.VMEM((rows, features), F32),
            pltpu.VMEM((rows, features), BF16),
            pltpu.VMEM((features, rows), BF16),
            pltpu.VMEM((rows, features), BF16),
            pltpu.VMEM((features, rows), BF16),
            pltpu.VMEM((rows, features), F32),
            pltpu.VMEM((rows, features), F32),
            DMA((n_t,)), DMA((n_t,)), DMA, DMA((n_t,)), DMA((n_t,)),
        ],
        compiler_params=params(),
        cost_estimate=cost(2 * rows * features * features * (6 * n_t + 4), 30e6),
    )(mix, x, g, vecs, w_up, w_down, w_out)


def back_kernel(
    n_d, n_t, parts, heads, chunks, plan,
    dmix_ref, proj_ref, mix_ref, lse_ref, cos_ref, sin_ref, in_hbm, wq_hbm, stat_ref,
    gup_ref, gdown_ref, gout_ref,
    sum_ref, gq_ref, up_ref, down_ref, out_ref, table_ref,
    dmix_all, key_ref, keyt_ref, val_ref, dkey_ref, dval_ref, dproj_ref, in_ref, wq_ref,
    acc_ref, grad_ref, rc, rx, ry, sz, rz, got_ref, mine_ref, *more,
):
    n_chunks = len(chunks)
    held = more[:n_chunks]
    met = more[n_chunks : 2 * n_chunks]
    arrived = more[2 * n_chunks : 5 * n_chunks]
    (
        s_a, r_a, s_l, s_h, s_e, r_e, s_g, r_g, s_t, r_t, s_d, r_d,
        s_c, r_c, s_x, r_x, s_y, r_y, s_z, r_z,
    ) = more[5 * n_chunks :]
    d, t, oi, ii, xi, ci = place(n_d, n_t)
    nx, no = n_t // CORES, n_d // INNER
    other = xi * CORES + (1 - ci)
    blocks, total, rows = proj_ref.shape
    width = total // 3
    half = HEAD_DIM // 2
    length = blocks * rows
    every = slice(None)
    axes = {"z": (0, no), "y": (1, INNER), "x": (2, nx)}
    me = (oi, ii, xi)
    sources = (gup_ref, gdown_ref, gout_ref)
    results = (up_ref, down_ref, out_ref)

    firsts = []
    for c, (which, lanes, path) in enumerate(chunks):
        array = sources[which]
        firsts.append(
            (
                pltpu.make_async_copy(
                    array.at[:, :, :, ci, :, lanes], held[c], s_h.at[c]
                ),
                remote(
                    array.at[:, :, :, 1 - ci, :, lanes], met[c], s_e.at[c], r_e.at[c], d, other
                ),
            )
        )
    flights = {}
    for c, (which, lanes, path) in enumerate(chunks):
        for s in range(3):
            dim, count = axes[path[s]]
            flights[c, s] = []
            for r in range(1, count):
                to = lax.rem(me[dim] + r, count)
                spot = [every, every, every]
                for axis in path[:s]:
                    spot[axes[axis][0]] = me[axes[axis][0]]
                spot[dim] = to
                peer = list(me)
                peer[dim] = to
                flights[c, s].append(
                    remote(
                        held[c].at[tuple(spot)], arrived[3 * c + s].at[r - 1],
                        s_g.at[3 * c + s, r - 1], r_g.at[3 * c + s, r - 1],
                        peer[0] * INNER + peer[1], peer[2] * CORES + ci,
                    )
                )

    def begin(c):
        for copy in firsts[c]:
            copy.wait()
        block = held[c].shape[1:3]

        def add(n, carry):
            at = (n // (block[0] * block[1]), lax.rem(n // block[1], block[0]), lax.rem(n, block[1]))
            held[c][at] = (held[c][at].astype(F32) + met[c][at].astype(F32)).astype(BF16)
            return carry

        lax.fori_loop(0, held[c].shape[0] * block[0] * block[1], add, 0)
        for copy in flights[c, 0]:
            copy.start()

    def advance(c, s):
        if s < 0:
            return begin(c)
        which, lanes, path = chunks[c]
        for copy in flights[c, s]:
            copy.wait()
        got = arrived[3 * c + s]
        left = [axes[a][0] for a in "zyx" if a in path[s + 1 :]]
        sizes = [axes[a][1] for a in "zyx" if a in path[s + 1 :]]

        def fold(n, carry):
            spot = list(me)
            slot = []
            for dim, size in reversed(list(zip(left, sizes))):
                spot[dim] = lax.rem(n, size)
                slot.insert(0, spot[dim])
                n = n // size
            value = held[c][tuple(spot)].astype(F32)
            for r in range(axes[path[s]][1] - 1):
                value += got[(r,) + tuple(slot)].astype(F32)
            if s == 2:
                results[which][:, lanes] = value
            else:
                held[c][tuple(spot)] = value.astype(BF16)
            return carry

        if sizes:
            lax.fori_loop(0, int(np.prod(sizes)), fold, 0)
        else:
            fold(0, 0)
        if s < 2:
            for copy in flights[c, s + 1]:
                copy.start()

    greet(n_d, n_t)
    a_copies = {}
    for m in range(1, n_t):
        b = order(m, xi, ci, nx)
        a_copies[mirror(m, nx)] = remote(
            dmix_ref.at[b], dmix_all.at[t], s_a.at[m - 1], r_a.at[mirror(m, nx) - 1], d, b
        )
    for m in range(n_t - 1, 0, -1):
        a_copies[mirror(m, nx)].start()
    loads = [
        pltpu.make_async_copy(dmix_ref.at[t], dmix_all.at[t], s_l.at[0]),
        pltpu.make_async_copy(in_hbm, in_ref, s_l.at[1]),
        pltpu.make_async_copy(wq_hbm, wq_ref, s_l.at[2]),
    ]
    for copy in loads:
        copy.start()
    t_copies = []
    for r in range(1, n_t):
        copy = remote(
            stat_ref, got_ref.at[r - 1], s_t.at[r - 1], r_t.at[r - 1], d, lax.rem(t + r, n_t)
        )
        copy.start()
        t_copies.append(copy)
    for pair in firsts:
        for copy in pair:
            copy.start()
    d_copies = [pltpu.make_async_copy(mine_ref, table_ref.at[d], s_l.at[3])]
    for r in range(1, n_d):
        d_copies.append(
            remote(mine_ref, table_ref.at[d], s_d.at[r - 1], r_d.at[r - 1], lax.rem(d + r, n_d), t)
        )

    def share_statistics():
        for copy in t_copies:
            copy.wait()
        value = stat_ref[...]
        for r in range(1, n_t):
            value += got_ref[r - 1]
        mine_ref[...] = value
        for copy in d_copies:
            copy.start()

    dkey_ref[...] = jnp.zeros_like(dkey_ref)
    dval_ref[...] = jnp.zeros_like(dval_ref)

    def turn(b, carry):
        lanes = pl.ds(pl.multiple_of(b * rows, rows), rows)
        keyt_ref[:, lanes] = proj_ref[b, width : 2 * width]
        for h in range(heads):
            at = h * HEAD_DIM
            key_ref[h, lanes] = proj_ref[b, width + at : width + at + HEAD_DIM].T
            val_ref[h, lanes] = proj_ref[b, 2 * width + at : 2 * width + at + HEAD_DIM].T
        return carry

    lax.fori_loop(0, blocks, turn, 0)
    loads[0].wait()

    def unrotate(block, at, factor, first, last):
        lanes = pl.ds(pl.multiple_of(block * rows, rows), rows)
        cos, sin = cos_ref[:, lanes], sin_ref[:, lanes]
        dproj_ref[block, at : at + half] = ((first * cos + last * sin) * factor).astype(BF16)
        dproj_ref[block, at + half : at + HEAD_DIM] = ((last * cos - first * sin) * factor).astype(
            BF16
        )

    def attend(k, carry):
        for m in range(1, n_t):
            @pl.when(k == m)
            def _(m=m):
                a_copies[m].wait()
        i = lax.rem(xi + k // CORES, nx) * CORES + lax.rem(ci + lax.rem(k, CORES), CORES)
        for h in range(heads):
            at = h * HEAD_DIM
            query_t = proj_ref[i, at : at + HEAD_DIM]
            dmix_t = dmix_all[i, at : at + HEAD_DIM]
            mix_t = mix_ref[i, at : at + HEAD_DIM]
            inner = jnp.sum(dmix_t.astype(F32) * mix_t.astype(F32), axis=0, keepdims=True)
            d_query = jnp.zeros((HEAD_DIM, rows), F32)
            for v in range(2):
                keys = slice(v * length // 2, (v + 1) * length // 2)
                probs = jnp.exp(dot(key_ref[h, keys], query_t, 1, 0) - lse_ref[i, h : h + 1])
                d_probs = dot(val_ref[h, keys], dmix_t, 1, 0)
                d_scores = (probs * (d_probs - inner)).astype(BF16)
                dval_ref[h, keys] += dot(probs.astype(BF16), dmix_t.T, 1, 0)
                dkey_ref[h, keys] += dot(d_scores, query_t.T, 1, 0)
                d_query += dot(keyt_ref[at : at + HEAD_DIM, keys], d_scores, 1, 0)
            unrotate(i, at, HEAD_DIM**-0.5, d_query[:half], d_query[half:])
        for n in range(n_t):
            @pl.when(k == n)
            def _(n=n):
                for step in plan[n]:
                    advance(*step)
                if n == 1:
                    share_statistics()
        return carry

    lax.fori_loop(0, n_t, attend, 0)
    loads[1].wait()
    loads[2].wait()
    acc_ref[...] = jnp.zeros_like(acc_ref)

    def project(b, carry):
        lanes = pl.ds(pl.multiple_of(b * rows, rows), rows)
        for h in range(heads):
            at = h * HEAD_DIM
            d_key = dkey_ref[h, lanes].T
            unrotate(b, width + at, 1.0, d_key[:half], d_key[half:])
            dproj_ref[b, 2 * width + at : 2 * width + at + HEAD_DIM] = (
                dval_ref[h, lanes].T.astype(BF16)
            )
        acc_ref[...] += dot(dproj_ref[b], in_ref[b], 1, 0)
        return carry

    lax.fori_loop(0, blocks, project, 0)
    grad_ref[...] = acc_ref[...].T.astype(BF16).reshape(grad_ref.shape)
    y_copies = []
    for q in range(1, INNER):
        to = lax.rem(ii + q, INNER)
        copy = remote(
            grad_ref.at[:, to], ry.at[q - 1], s_y.at[q - 1], r_y.at[q - 1], oi * INNER + to, t
        )
        copy.start()
        y_copies.append(copy)
    for step in plan[n_t]:
        advance(*step)

    part_ref = in_ref
    c_copies = {}
    for r in range(nx):
        for p in range(parts):
            c_copies[r, p] = remote(
                part_ref.at[lax.rem(xi + r, nx) * CORES + 1 - ci, pl.ds(p * (rows // parts), rows // parts)],
                rc.at[r, pl.ds(p * (rows // parts), rows // parts)],
                s_c.at[r, p], r_c.at[r, p], d, other,
            )

    def share(k, carry):
        shift = n_t - 1 - k
        b = lax.rem(xi + shift // CORES, nx) * CORES + lax.rem(ci + lax.rem(shift, CORES), CORES)
        part_ref[b] = dot(dproj_ref[b].T, wq_ref[...], 1, 1).astype(BF16)
        for r in range(nx):
            @pl.when(k == n_t - 1 - (r * CORES + 1))
            def _(r=r):
                for p in range(parts):
                    c_copies[r, p].start()
        return carry

    lax.fori_loop(0, n_t, share, 0)
    x_copies = []
    for r in range(1, nx):
        for p in range(parts):
            at = pl.ds(p * (rows // parts), rows // parts)
            c_copies[r, p].wait()
            to = lax.rem(xi + r, nx) * CORES + ci
            part_ref[to, at] = (part_ref[to, at].astype(F32) + rc[r, at].astype(F32)).astype(BF16)
            copy = remote(
                part_ref.at[to, at], rx.at[r - 1, at], s_x.at[r - 1, p], r_x.at[r - 1, p], d, to
            )
            copy.start()
            x_copies.append(copy)
    for copy in y_copies:
        copy.wait()
    z_copies = []
    for r in range(1, no):
        to = lax.rem(oi + r, no)
        value = grad_ref[to, ii].astype(F32)
        for q in range(1, INNER):
            value += ry[q - 1, to].astype(F32)
        sz[r - 1] = value.astype(BF16)
        copy = remote(sz.at[r - 1], rz.at[r - 1], s_z.at[r - 1], r_z.at[r - 1], to * INNER + ii, t)
        copy.start()
        z_copies.append(copy)
    for step in plan[n_t + 1]:
        advance(*step)
    value = grad_ref[oi, ii].astype(F32)
    for q in range(1, INNER):
        value += ry[q - 1, oi].astype(F32)
    for copy in z_copies:
        copy.wait()
    for r in range(1, no):
        value += rz[r - 1].astype(F32)
    for j in range(3):
        gq_ref[j] = value[:, j * width : (j + 1) * width]
    for copy in d_copies:
        copy.wait()
    for p in range(parts):
        c_copies[0, p].wait()
    for copy in x_copies:
        copy.wait()
    for p in range(parts):
        at = pl.ds(p * (rows // parts), rows // parts)
        value = part_ref[t, at].astype(F32) + rc[0, at].astype(F32)
        for r in range(1, nx):
            value += rx[r - 1, at].astype(F32)
        sum_ref[at] = value


def back_call(dmix, proj, mix, lse, cos, sin, attn_in, w_qkv, stat, g_up, g_down, g_out, n_d, n_t):
    parts = 4
    nx, no = n_t // CORES, n_d // INNER
    blocks, total, rows = proj.shape
    width = total // 3
    heads = width // HEAD_DIM
    length = blocks * rows
    features = attn_in.shape[2]
    part = features // n_d
    units, wide = g_up.shape[-1], g_out.shape[-1]
    grid_of = (no, INNER, nx, CORES, part)
    g_up, g_down = g_up.reshape(grid_of + (units,)), g_down.reshape(grid_of + (units,))
    g_out = g_out.reshape(grid_of + (wide,))
    cut = units // 2
    low, high = slice(0, cut), slice(cut, units)
    chunks = (
        (0, low, "xyz"), (1, low, "yzx"), (2, slice(0, wide), "xzy"),
        (0, high, "xyz"), (1, high, "yzx"),
    )
    plan = (
        [(0, -1), (1, -1), (2, -1), (3, -1), (4, -1)],
        [(0, 0), (1, 0)],
        [(2, 0), (4, 0)],
        [(3, 0), (0, 1), (1, 1)],
        [(2, 1), (4, 1)],
        [(3, 1), (0, 2), (1, 2), (2, 2), (4, 2), (3, 2)],
    )
    sizes = {"z": no, "y": INNER, "x": nx}
    held, arrived = [], []
    for which, lanes, path in chunks:
        tail = (part, lanes.stop - lanes.start)
        held.append(pltpu.VMEM((no, INNER, nx) + tail, BF16))
        for s in range(3):
            rest = tuple(sizes[a] for a in "zyx" if a in path[s + 1 :])
            arrived.append(pltpu.VMEM((sizes[path[s]] - 1,) + rest + tail, BF16))
    n_chunks = len(chunks)
    steps = max(no, INNER, nx) - 1
    return pl.pallas_call(
        partial(back_kernel, n_d, n_t, parts, heads, chunks, plan),
        name="back",
        out_shape=[
            struct((rows, features), F32),
            struct((3, part, width), F32),
            struct((part, units), F32),
            struct((part, units), F32),
            struct((part, wide), F32),
            struct((n_d,) + stat.shape, F32),
        ],
        in_specs=[VMEM] * 6 + [ANY] * 2 + [VMEM] + [ANY] * 3,
        out_specs=[VMEM] * 5 + [ANY],
        scratch_shapes=[
            pltpu.VMEM(dmix.shape, BF16),
            pltpu.VMEM((heads, length, HEAD_DIM), BF16),
            pltpu.VMEM((width, length), BF16),
            pltpu.VMEM((heads, length, HEAD_DIM), BF16),
            pltpu.VMEM((heads, length, HEAD_DIM), F32),
            pltpu.VMEM((heads, length, HEAD_DIM), F32),
            pltpu.VMEM(proj.shape, BF16),
            pltpu.VMEM(attn_in.shape, BF16),
            pltpu.VMEM(w_qkv.shape, BF16),
            pltpu.VMEM((total, features), F32),
            pltpu.VMEM((no, INNER, part, total), BF16),
            pltpu.VMEM((nx, rows, features), BF16),
            pltpu.VMEM((nx - 1, rows, features), BF16),
            pltpu.VMEM((INNER - 1, no, part, total), BF16),
            pltpu.VMEM((no - 1, part, total), BF16),
            pltpu.VMEM((no - 1, part, total), BF16),
            pltpu.VMEM((n_t - 1,) + stat.shape, F32),
            pltpu.VMEM(stat.shape, F32),
        ]
        + held + held + arrived
        + [
            DMA((n_t - 1,)), DMA((n_t - 1,)), DMA((4,)), DMA((n_chunks,)),
            DMA((n_chunks,)), DMA((n_chunks,)),
            DMA((3 * n_chunks, steps)), DMA((3 * n_chunks, steps)),
            DMA((n_t - 1,)), DMA((n_t - 1,)), DMA((n_d - 1,)), DMA((n_d - 1,)),
            DMA((nx, parts)), DMA((nx, parts)), DMA((nx - 1, parts)), DMA((nx - 1, parts)),
            DMA((INNER - 1,)), DMA((INNER - 1,)), DMA((no - 1,)), DMA((no - 1,)),
        ],
        compiler_params=params(1),
        cost_estimate=cost(45 * heads * length * length * HEAD_DIM, 40e6, heads * length * length),
    )(dmix, proj, mix, lse, cos, sin, attn_in, w_qkv, stat, g_up, g_down, g_out)


def tail_kernel(
    n_d, n_t, count,
    x_ref, e_ref, dmid_ref, vec_ref, ada_ref, table_ref, cond_ref,
    grad_ref, gada_ref, bias_ref, gcond_ref, sum_ref, gain_ref, root_ref,
    late_ref, got_ref, mine_ref, late_all, flat_ref, rows_out, rows_in, s_t, r_t, s_d, r_d, s_p, r_p, s_l,
):
    d, t = lax.axis_index("dp"), lax.axis_index("tensor")
    features = x_ref.shape[1]
    x = x_ref[...].astype(F32)
    e = e_ref[...]
    gain, scale = vec_ref[GAIN1 : GAIN1 + 1], 1.0 + vec_ref[SCALE_A : SCALE_A + 1]
    centred = x - mean_rows(x)
    inv = lax.rsqrt(mean_rows(centred * centred) + EPSILON)
    nhat = centred * inv
    by_nhat = sum_tokens(e * nhat)
    late_ref[:, :features] = sum_tokens(e)
    late_ref[:, features : 2 * features] = by_nhat * gain
    late_ref[:, 2 * features :] = by_nhat * scale
    greet(n_d, n_t)
    copies = []
    for r in range(1, n_t):
        copy = remote(
            late_ref, got_ref.at[r - 1], s_t.at[r - 1], r_t.at[r - 1], d, lax.rem(t + r, n_t)
        )
        copy.start()
        copies.append(copy)
    dn = e * (scale * gain)
    grad_ref[...] = dmid_ref[...] + inv * (dn - mean_rows(dn) - nhat * mean_rows(dn * nhat))
    value = late_ref[...]
    for r in range(1, n_t):
        copies[r - 1].wait()
        value += got_ref[r - 1]
    mine_ref[...] = value
    copies = [pltpu.make_async_copy(mine_ref, late_all.at[d], s_l.at[0])]
    for r in range(1, n_d):
        copies.append(
            remote(mine_ref, late_all.at[d], s_d.at[r - 1], r_d.at[r - 1], lax.rem(d + r, n_d), t)
        )
    for copy in copies:
        copy.start()
    total = table_ref[0]
    for s in range(1, n_d):
        total += table_ref[s]
    sum_ref[...] = total
    for k, row in enumerate((S_SQ_A, S_SQ_M, S_SQ_R)):
        root_ref[k : k + 1] = jnp.broadcast_to(
            jnp.sqrt(jnp.sum(total[row : row + 1], axis=1, keepdims=True) / count),
            (1, root_ref.shape[1]),
        )

    def outer(block, row_of):
        at = slice(block * features, (block + 1) * features)
        value = jnp.zeros((cond_ref.shape[0], features), F32)
        for s in range(n_d):
            value += cond_ref[:, s : s + 1] * row_of(s)
        gada_ref[:, at] = value

    early = ((2, S_GATE_A), (3, S_SHIFT_M), (4, S_SCALE_M), (5, S_GATE_M))
    for block, row in early:
        outer(block, lambda s: table_ref[s, row : row + 1, :])
    for copy in copies:
        copy.wait()
    for s in range(n_d):
        flat_ref[s : s + 1, : 2 * features] = late_all[s, :, : 2 * features]
        for block, row in early:
            flat_ref[s : s + 1, block * features : (block + 1) * features] = table_ref[
                s, row : row + 1
            ]
    flat = flat_ref[...]
    columns = ada_ref.shape[0]
    moved = pltpu.roll(flat, lax.rem(n_d - d, n_d) * columns, 1)[:, :columns]
    rows_out[:, 0, :] = lax.dot_general(
        moved, ada_ref[...].astype(F32), (((1,), (0,)), ((), ())),
        precision=lax.Precision.HIGHEST, preferred_element_type=F32,
    )
    copies = [pltpu.make_async_copy(rows_out.at[d], rows_in.at[d], s_l.at[1])]
    for r in range(1, n_d):
        peer = lax.rem(d + r, n_d)
        copies.append(remote(rows_out.at[peer], rows_in.at[d], s_p.at[r - 1], r_p.at[r - 1], peer, t))
    for copy in copies:
        copy.start()
    for block in (0, 1):
        outer(block, lambda s: late_all[s, :, block * features : (block + 1) * features])
    bias_ref[...] = jnp.sum(flat, axis=0, keepdims=True)
    value = late_all[0, :, 2 * features :]
    for s in range(1, n_d):
        value += late_all[s, :, 2 * features :]
    gain_ref[...] = value
    for copy in copies:
        copy.wait()
    gcond_ref[...] = jnp.sum(rows_in[:, 0, :], axis=0, keepdims=True)


def tail_call(x, e, dmid, vecs, ada_t, table, cond_t, count, n_d, n_t):
    features = x.shape[1]
    width = ada_t.shape[1]
    return pl.pallas_call(
        partial(tail_kernel, n_d, n_t, count),
        name="tail",
        out_shape=[
            struct(x.shape, F32),
            struct((width, 6 * features), F32),
            struct((1, 6 * features), F32),
            struct((1, width), F32),
            struct(table.shape[1:], F32),
            struct((1, features), F32),
            struct((3, 128), F32),
        ],
        in_specs=[VMEM] * 7,
        out_specs=[VMEM] * 7,
        scratch_shapes=[
            pltpu.VMEM((1, 3 * features), F32),
            pltpu.VMEM((n_t - 1, 1, 3 * features), F32),
            pltpu.VMEM((1, 3 * features), F32),
            pltpu.VMEM((n_d, 1, 3 * features), F32),
            pltpu.VMEM((n_d, 6 * features), F32),
            pltpu.VMEM((n_d, 1, width), F32),
            pltpu.VMEM((n_d, 1, width), F32),
            DMA((n_t - 1,)), DMA((n_t - 1,)),
            DMA((n_d - 1,)), DMA((n_d - 1,)),
            DMA((n_d - 1,)), DMA((n_d - 1,)),
            DMA((2,)),
        ],
        compiler_params=params(2),
        cost_estimate=cost(20 * x.size, 10e6),
    )(x, e, dmid, vecs, ada_t, table, cond_t)


def shards(
    block_input, condition, modulation_weight, modulation_bias, first_gain, qkv_weight, out_weight,
    second_gain, up_weight, up_bias, down_weight, down_bias, grad_output,
):
    n_t, n_d = lax.axis_size("tensor"), lax.axis_size("dp")
    rows, sequences, features = block_input.shape
    assert sequences == 1
    length = rows * n_t
    part, width = qkv_weight.shape[1:]
    units = up_weight.shape[1]
    assert units == features and n_t % CORES == 0 and n_d % INNER == 0
    x = block_input.reshape(rows, features)
    g = grad_output.reshape(rows, features)
    ada_t = modulation_weight.T

    small = jnp.concatenate([first_gain, second_gain, down_bias, up_bias]).astype(F32)
    cond_at = -(-small.shape[0] // 128) * 128
    bias_at = cond_at + condition.shape[1]
    small = jnp.concatenate(
        [
            small, jnp.zeros((cond_at - small.shape[0],), F32),
            condition[0].astype(F32), modulation_bias.astype(F32),
        ]
    )[None]
    own = first_gain.shape[0]
    sizes = ((GAIN1, own), (GAIN2, own), (B_DOWN, own), (B_UP, up_bias.shape[0]))
    inverse = 10000.0 ** (-np.arange(HEAD_DIM // 2) * 2.0 / HEAD_DIM)
    angles = inverse[:, None] * np.arange(length)[None, :]
    cos, sin = jnp.asarray(np.cos(angles), F32), jnp.asarray(np.sin(angles), F32)

    attn_in, proj, mix, lse, mix_own, vecs, cond_t, w_qkv, w_up, w_down, w_out = front_call(
        x, qkv_weight, small, ada_t, up_weight, down_weight.T, out_weight, cos, sin,
        cond_at, bias_at, sizes, n_d, n_t,
    )
    merge = lambda a: a.reshape((n_d, n_t) + a.shape[4:])
    stat_rows = -(-(S_B_UP + n_t) // 8) * 8
    out, d_middle, d_mix, stat, g_up, g_down, g_out = middle_call(
        mix_own, x, g, vecs, merge(w_up), merge(w_down), merge(w_out), stat_rows
    )
    d_attn_in, g_qkv, g_up, g_down, g_out, table = back_call(
        d_mix, proj, mix, lse, cos, sin, attn_in, w_qkv.reshape(features, 3 * width), stat,
        g_up, g_down, g_out, n_d, n_t,
    )
    grad_input, grad_ada, grad_ada_b, grad_cond, sums, gain1, roots = tail_call(
        x, d_attn_in, d_middle, vecs, ada_t, table, cond_t, float(length * n_d * features), n_d, n_t
    )
    return (
        out.reshape(block_input.shape),
        grad_input.reshape(block_input.shape),
        grad_cond,
        grad_ada,
        grad_ada_b[0],
        gain1[0],
        g_qkv,
        g_out[:, :width].T,
        sums[S_GAIN2],
        g_up,
        sums[S_B_UP : S_B_UP + n_t].reshape(-1),
        g_down.T,
        sums[S_B_DOWN],
        roots[:, 0],
    )


def solution(mesh):
    in_specs = (
        P("tensor", "dp", None),
        P("dp", None),
        P(None, "dp"),
        P("dp"),
        P("dp"),
        P(None, "dp", "tensor"),
        P("tensor", "dp"),
        P("dp"),
        P("dp", "tensor"),
        P("dp"),
        P("tensor", "dp"),
        P("dp"),
        P("tensor", "dp", None),
    )
    out_specs = (
        P("tensor", "dp", None),
        P("tensor", "dp", None),
        P("dp", None),
        P(),
        P(),
        P(),
        P(None, "dp", "tensor"),
        P("tensor", "dp"),
        P(),
        P("dp", "tensor"),
        P(),
        P("tensor", "dp"),
        P(),
        P(),
    )
    return jax.shard_map(shards, mesh=mesh, in_specs=in_specs, out_specs=out_specs, check_vma=False)
```

time: 315 us -> 269 us (0.85); the launches traced: 309 us -> 269 us
  waiting for transfers between devices: 20.5 us -> 0 us
  between operations: 14.4 us -> 0.73 us
  local copies, waits for them, and re-layouts: 24.7 us -> 14.8 us
  Pallas kernels: 246 us -> 250 us
    all_gather x1 -> x0, waiting for transfers between devices: 12.8 us -> none  [shards(): w_rest = lax.all_gather(pack, ('dp', 'tensor'), axis=0, tiled=False)]
    reduce_scatter x1 -> x0, waiting for transfers between devices: 7.67 us -> none  [shards(): lax.psum_scatter(grads.reshape(n_d * n_t, part, pack.shape[1]), ('dp', 't...]
    pallas_call x12 -> x4, Pallas kernels: 246 us -> 250 us  [the longest x1 101 us: back_call(): pl.pallas_call(partial(back_kernel, n_d, n_t, parts, heads, chunks, plan)...]
    unnamed x16 -> x23, local copies, waits for them, and re-layouts: 9.69 us -> 9.15 us
  transfers between devices with their start and end apart: 2 -> 0, of which waited for: 2 -> 0; matrix products, arithmetic and copies ran while one was open for 7% -> 0% of each run, Pallas kernels for 70% -> 0%
where the time goes in v2:
time: 269 us
  Pallas kernels  250 us (93%)
  local copies, waits for them, and re-layouts  14.8 us (6%)
  other arithmetic  2.7 us (1%)
    pallas_call x1, Pallas kernels, back_call(): pl.pallas_call(partial(back_kernel, n_d, n_t, parts, heads, chunks, plan)...  101 us
    pallas_call x1, Pallas kernels, front_call(): pl.pallas_call(partial(front_kernel, n_d, n_t, parts, heads, cond_at, bia...  97.7 us
    pallas_call x1, Pallas kernels, middle_call(): pl.pallas_call(middle_kernel, name='middle', out_shape=[struct((rows, fea...  30.4 us
    pallas_call x1, Pallas kernels, tail_call(): pl.pallas_call(partial(tail_kernel, n_d, n_t, count), name='tail', out_sh...  20.8 us
    unnamed x23, local copies, waits for them, and re-layouts  9.15 us

profile of v2, /device:TPU:0, one launch (start us, length us, event | category | flops | bytes accessed | tf_op | source)
XLA Modules:
  0.0 268.5 jit_solution(8694591226314036517)
XLA Ops:
  0.6 0.7 bitcast_convert_fusion
  1.3 0.8 maximum_convert_fusion
  2.1 0.8 concatenate.7
  2.8 0.6 broadcast_in_dim.7.small_ref
  3.4 97.7 %front.1 = (bf16[4,512,768]{2,1,0:T(8,128)(2,1)}, bf16[4,576,512]{2,1,0:T(8,128)(2,1)}, bf16[4,192,512]{2,1,0:T(8,128)(2,1)}, f32[4,3,512]{2,1,0:T(4,128)}, bf16...) custom-call(bf16[512,768]{1,0:T(8,128)(2,1)} %bitcast.20, ...), custom_call_target="tpu_custom_call" | custom-call | flops 16106127360 | bytes 40000000 | tf_op jit(solution)/shard_map/front/pallas_call | solution.py:403
  101.2 30.4 %middle.1 = (bf16[512,768]{1,0:T(8,128)(2,1)}, f32[512,768]{1,0:T(8,128)}, bf16[4,192,512]{2,1,0:T(8,128)(2,1)}, f32[16,768]{1,0:T(8,128)}, bf16[8,4,96,768]{3,2...) custom-call(bf16[4,192,512]{2,1,0:T(8,128)(2,1)} %get-tuple-element.45.mix_ref, ...), custom_call_target="tpu_custom_call" | custom-call | flops 16911433728 | bytes 30000000 | tf_op jit(solution)/shard_map/middle/pallas_call | solution.py:558
  131.5 101.4 %back.1 = (f32[512,768]{1,0:T(8,128)}, f32[3,96,192]{2,1,0:T(8,128)}, f32[96,768]{1,0:T(8,128)}, f32[96,768]{1,0:T(8,128)}, f32[96,256]{1,0:T(8,128)}, /*index=5*/f32[8,16,768]{2,1,0:T(8,128)}) custom-call(bf16[4,192,512]{2,1,0:T(8,128)(2,1)} %get-tuple-element.51.dmix_ref, bf16[4,576,512]{2,1,0:T(8,128)(2,1)} %get-tuple-element.52.proj_ref, ...), custom_call_target="tpu_custom_call" | custom-call | flops 36238786560 | bytes 40000000 | tf_op jit(solution)/shard_map/back/pallas_call | solution.py:935
  232.9 0.9 slice_bitcast_fusion
  233.8 0.7 copy.32
  234.6 20.8 %tail.1 = (f32[512,768]{1,0:T(8,128)}, f32[128,4608]{1,0:T(8,128)}, f32[1,4608]{1,0:T(1,128)}, f32[1,128]{1,0:T(1,128)}, f32[16,768]{1,0:T(8,128)}, /*index=5*/f32[1,768]{1,0:T(1,128)}, f32[3,128]{1,0:T(4,128)}) custom-call(bf16[512,768]{1,0:T(8,128)(2,1)} %bitcast.22, f32[512,768]{1,0:T(8,128)} %get-tuple-element.61.e_ref, ...), custom_call_target="tpu_custom_call" | custom-call | flops 7864320 | bytes 10000000 | tf_op jit(solution)/shard_map/tail/pallas_call | solution.py:1078
  255.4 0.0 copy-start.6
  255.4 0.0 copy-start.5
  255.4 0.0 copy-start.4
  255.4 0.0 copy-start.7
  255.5 0.0 copy-start
  255.5 4.3 %copy.31 = f32[512,1,768]{2,1,0:T(1,128)} copy(f32[512,1,768]{2,0,1:T(8,128)} %bitcast.19) | data formatting | bytes 3145728
  259.8 0.0 copy-done.6
  259.8 0.6 slice_reduce_fusion.2
  260.4 0.0 copy-done.5
  260.4 0.6 reduce.1
  261.0 0.0 copy-done.4
  261.0 0.7 reduce
  261.7 1.4 slice_reduce_fusion
  263.1 0.7 slice.17
  263.8 0.6 reshape.77
  264.5 0.0 copy-done.7
  264.5 0.5 copy.38
  265.0 0.0 copy-done
  265.0 0.0 copy-start.3
  265.0 0.0 copy-start.2
  265.0 0.0 copy-start.1
  265.0 1.4 copy.39
  266.4 0.0 copy-done.3
  266.4 0.7 copy.40
  267.1 0.0 copy-done.2
  267.1 0.7 copy.41
  267.8 0.0 copy-done.1
  267.8 0.7 copy.42
  (1 shorter events, 0.0 us)
Async XLA Ops:
  255.4 4.4 %copy-start.6 = (f32[3,128]{1,0:T(4,128)S(1)}, f32[3,128]{1,0:T(4,128)}, u32[]{:S(2)}) copy-start(f32[3,128]{1,0:T(4,128)} %get-tuple-element.75) | copy-start | bytes 4612
  255.4 5.0 %copy-start.5 = (f32[1,768]{1,0:T(1,128)S(1)}, f32[1,768]{1,0:T(1,128)}, u32[]{:S(2)}) copy-start(f32[1,768]{1,0:T(1,128)} %get-tuple-element.69) | copy-start | bytes 9220
  255.4 5.6 %copy-start.4 = (f32[1,4608]{1,0:T(1,128)S(1)}, f32[1,4608]{1,0:T(1,128)}, u32[]{:S(2)}) copy-start(f32[1,4608]{1,0:T(1,128)} %get-tuple-element.68) | copy-start | bytes 55300
  255.4 9.0 %copy-start.7 = (f32[1,128]{1,0:T(1,128)S(1)}, f32[1,128]{1,0:T(1,128)}, u32[]{:S(2)}) copy-start(f32[1,128]{1,0:T(1,128)} %get-tuple-element.122) | copy-start | bytes 1540
  255.5 9.5 %copy-start = (f32[128,4608]{1,0:T(8,128)S(1)}, f32[128,4608]{1,0:T(8,128)}, u32[]{:S(2)}) copy-start(f32[128,4608]{1,0:T(8,128)} %get-tuple-element.123) | copy-start | bytes 7077892
  265.0 1.4 copy-start.3
  265.0 2.1 copy-start.2
  265.0 2.8 %copy-start.1 = (f32[96,768]{1,0:T(8,128)S(1)}, f32[96,768]{1,0:T(8,128)}, u32[]{:S(2)}) copy-start(f32[96,768]{1,0:T(8,128)} %get-tuple-element.74) | copy-start | bytes 884740

commit v3 on v2

v3 whole, which is shorter than its diff:
```python
from functools import partial

import jax
import jax.numpy as jnp
import numpy as np
from jax import lax
from jax.experimental import pallas as pl
from jax.experimental.pallas import tpu as pltpu
from jax.sharding import PartitionSpec as P

HEAD_DIM = 64
EPSILON = 1e-05
CORES = 2
INNER = 2
MESH = pl.DeviceIdType.MESH
VMEM_LIMIT = 58 << 20
GELU_C = float(np.sqrt(2.0 / np.pi))
GELU_A = 0.044715
F32 = jnp.float32
BF16 = jnp.bfloat16
ANY = pl.BlockSpec(memory_space=pl.ANY)
VMEM = pl.BlockSpec(memory_space=pltpu.VMEM)
DMA = pltpu.SemaphoreType.DMA


def dot(lhs, rhs, lhs_dim, rhs_dim):
    return lax.dot_general(
        lhs, rhs, (((lhs_dim,), (rhs_dim,)), ((), ())), preferred_element_type=F32
    )


def params(collective_id=None, **more):
    if collective_id is not None:
        more.update(collective_id=collective_id, has_side_effects=True)
    return pltpu.CompilerParams(vmem_limit_bytes=VMEM_LIMIT, **more)


def cost(flops, moved, special=0):
    return pl.CostEstimate(flops=int(flops), bytes_accessed=int(moved), transcendentals=int(special))


def struct(shape, dtype):
    return jax.ShapeDtypeStruct(shape, dtype)


def mean_rows(values):
    return jnp.mean(values, axis=-1, keepdims=True)


def sum_tokens(values):
    return jnp.sum(values, axis=0, keepdims=True)


GAIN1, SHIFT_A, SCALE_A, GATE_A, GAIN2, SHIFT_M, SCALE_M, GATE_M, B_DOWN, B_UP = range(10)
MOD_ROWS = (SHIFT_A, SCALE_A, GATE_A, SHIFT_M, SCALE_M, GATE_M)
S_GATE_A, S_SHIFT_M, S_SCALE_M, S_GATE_M, S_GAIN2, S_B_DOWN, S_SQ_A, S_SQ_M, S_SQ_R, S_B_UP = range(10)
L_SHIFT_A, L_SCALE_A, L_GAIN1 = range(3)


def order(k, xi, ci, nx):
    return lax.rem(xi + k // CORES, nx) * CORES + lax.rem(ci + k % CORES, CORES)


def mirror(k, nx):
    return (nx - k // CORES) % nx * CORES + (CORES - k % CORES) % CORES


def place(n_d, n_t):
    d, t = lax.axis_index("dp"), lax.axis_index("tensor")
    return d, t, d // INNER, lax.rem(d, INNER), t // CORES, lax.rem(t, CORES)


def greet(n_d, n_t):
    d, t = lax.axis_index("dp"), lax.axis_index("tensor")
    barrier = pltpu.get_barrier_semaphore()
    for r in range(1, n_t):
        pl.semaphore_signal(
            barrier, 1, device_id=(d, lax.rem(t + r, n_t)), device_id_type=MESH
        )
    for r in range(1, n_d):
        pl.semaphore_signal(
            barrier, 1, device_id=(lax.rem(d + r, n_d), t), device_id_type=MESH
        )
    pl.semaphore_wait(barrier, n_t - 1 + n_d - 1)


def remote(src, dst, send, recv, d, t):
    return pltpu.make_async_remote_copy(
        src_ref=src, dst_ref=dst, send_sem=send, recv_sem=recv, device_id=(d, t), device_id_type=MESH
    )


class Places:
    def __init__(self, n_d, n_t):
        d, t = lax.axis_index("dp"), lax.axis_index("tensor")
        self.d, self.t = d, t
        self.me = {"z": d // INNER, "y": lax.rem(d, INNER), "x": t // CORES, "c": lax.rem(t, CORES)}
        self.count = counts(n_d, n_t)

    def peer(self, axis, r):
        at = dict(self.me)
        at[axis] = lax.rem(at[axis] + r, self.count[axis])
        return at[axis], (at["z"] * INNER + at["y"], at["x"] * CORES + at["c"])


def counts(n_d, n_t):
    return {"z": n_d // INNER, "y": INNER, "x": n_t // CORES, "c": CORES}


class Spread:
    def __init__(self, places, dims, known, path, array, source, send, recv, row, lanes=slice(None)):
        self.path, self.flights = path, []
        for s, axis in enumerate(path):
            region = tuple(
                slice(None) if a in known or a in path[:s] else places.me[a] for a in dims
            ) + (slice(None), lanes)
            src = source if s == 0 else array.at[region]
            self.flights.append([])
            for r in range(1, places.count[axis]):
                _, (d, t) = places.peer(axis, r)
                self.flights[s].append(
                    remote(
                        src, array.at[region], send.at[row + s, r - 1], recv.at[row + s, r - 1], d, t
                    )
                )

    def start(self, s):
        for copy in self.flights[s]:
            copy.start()

    def wait(self, s):
        for copy in self.flights[s]:
            copy.wait()

    def advance(self, s, last=None):
        self.wait(s)
        if s + 1 < len(self.path) and s != last:
            self.start(s + 1)


class Reduce:
    def __init__(self, places, dims, path, source, own, met, results, send, recv, local, row):
        self.places, self.path, self.own, self.met = places, path, own, met
        self.results, self.flights, self.dims = results, [], []
        current = source
        for s, axis in enumerate(path):
            at = dims.index(axis)
            self.dims.append((current, dims, at))
            self.flights.append([])
            for r in range(1, places.count[axis]):
                to, (d, t) = places.peer(axis, r)
                self.flights[s].append(
                    remote(
                        current.at[(slice(None),) * at + (to,)], met[s].at[r - 1],
                        send.at[row + s, r - 1], recv.at[row + s, r - 1], d, t,
                    )
                )
            if s == 0:
                self.load = None
                if own is not None:
                    self.load = pltpu.make_async_copy(
                        current.at[(slice(None),) * at + (places.me[axis],)], own, local
                    )
            dims = dims.replace(axis, "")
            current = results[s]

    def start(self, s):
        for copy in self.flights[s]:
            copy.start()
        if s == 0 and self.load is not None:
            self.load.start()

    def advance(self, s):
        places, path = self.places, self.path
        for copy in self.flights[s]:
            copy.wait()
        current, dims, at = self.dims[s]
        rest = dims.replace(path[s], "")
        if s == 0 and self.load is not None:
            self.load.wait()
            current, at = self.own, None
        sizes = [places.count[a] for a in rest]

        def fold(n, carry):
            spot = []
            for size in reversed(sizes):
                spot.insert(0, lax.rem(n, size))
                n = n // size
            own = list(spot)
            if at is not None:
                own.insert(at, places.me[path[s]])
            value = current[tuple(own)].astype(F32)
            for r in range(places.count[path[s]] - 1):
                value += self.met[s][(r,) + tuple(spot)].astype(F32)
            if callable(self.results[s]):
                self.results[s](value)
            else:
                self.results[s][tuple(spot)] = value.astype(BF16)
            return carry

        if sizes:
            lax.fori_loop(0, int(np.prod(sizes)), fold, 0)
        else:
            fold(0, 0)
        if s + 1 < len(path):
            self.start(s + 1)


def reduce_scratch(count, dims, path, tail, own=True, last=True):
    shapes = []
    rest = dims.replace(path[0], "")
    if own:
        shapes.append(tuple(count[a] for a in rest) + tail)
    left = dims
    for axis in path:
        left = left.replace(axis, "")
        shapes.append((count[axis] - 1,) + tuple(count[a] for a in left) + tail)
    left = dims
    for axis in path if not last else path[:-1]:
        left = left.replace(axis, "")
        shapes.append(tuple(count[a] for a in left) + tail)
    return [pltpu.VMEM(shape, BF16) for shape in shapes]


BACK_SUMS = (("zy", "zy"), ("zx", "xz"), ("zyx", "xyz"), ("zyx", "yxz"), ("czyx", "czxy"))
CODE = {"z": 2, "y": 2, "x": 2, "c": 2}
EARLY = ((2, S_GATE_A), (3, S_SHIFT_M), (4, S_SCALE_M), (5, S_GATE_M))


def front_kernel(
    n_d, n_t, parts, heads, cond_at, bias_at, sizes,
    x_ref, qkv_ref, small_ref, ada_ref, up_ref, down_ref, outw_ref, cos_ref, sin_ref,
    in_all, proj_ref, mix_ref, lse_ref, mix_own, vec_ref, cond_ref, w_all, w_ul, w_dl, w_uh, w_dh, w_out,
    x_all, w_pack, wt_ref, out_pack, small_all, mod_all, mod_rows, key_ref,
    s_x, r_x, s_c, r_c, s_f, r_f, s_z, r_z, s_y, r_y, s_s, r_s, s_m, r_m, s_l,
    s_w, r_w, s_o, r_o,
):
    d, t, oi, ii, xi, ci = place(n_d, n_t)
    nx, no = n_t // CORES, n_d // INNER
    other = xi * CORES + (1 - ci)
    piece = x_ref.shape[0] // parts
    rows, features = x_ref.shape
    width = qkv_ref.shape[2]
    half = HEAD_DIM // 2
    cut = w_ul.shape[5]
    low_half, high_half = slice(0, cut), slice(cut, 2 * cut)
    for j in range(3):
        w_pack[:, j * width : (j + 1) * width] = qkv_ref[j]
    out_pack[:, :width] = outw_ref[...].T
    if out_pack.shape[1] > width:
        out_pack[:, width:] = jnp.zeros((out_pack.shape[0], out_pack.shape[1] - width), BF16)
    greet(n_d, n_t)
    places = Places(n_d, n_t)
    spread = lambda row, dims, path, array, source: Spread(
        places, dims, "", path, array, source, s_w, r_w, row
    )
    up_low = spread(0, "zyxc", "zyxc", w_ul, up_ref.at[:, low_half])
    down_low = spread(4, "zyxc", "xzyc", w_dl, down_ref.at[:, low_half])
    out_all = spread(8, "zyxc", "zxyc", w_out, out_pack)
    up_high = spread(12, "zy", "zy", w_uh, up_ref.at[:, high_half])
    down_high = spread(16, "zx", "zx", w_dh, down_ref.at[:, high_half])
    s_copies = []
    for r in range(1, n_d):
        copy = remote(
            small_ref, small_all.at[d], s_s.at[r - 1], r_s.at[r - 1], lax.rem(d + r, n_d), t
        )
        copy.start()
        s_copies.append(copy)
    down_low.start(0)
    x_copies = []
    for r in range(1, nx):
        peer = lax.rem(xi + r, nx) * CORES + ci
        for p in range(parts):
            at = pl.ds(p * piece, piece)
            copy = remote(
                x_ref.at[at], x_all.at[t, at], s_x.at[r - 1, p], r_x.at[r - 1, p], d, peer
            )
            copy.start()
            x_copies.append((r, p, copy))
    z_copies = []
    for r in range(1, no):
        copy = remote(
            w_pack, w_all.at[d], s_z.at[r - 1], r_z.at[r - 1], lax.rem(oi + r, no) * INNER + ii, t
        )
        copy.start()
        z_copies.append(copy)
    y_copies = []
    for q in range(1, INNER):
        copy = remote(
            w_pack, w_all.at[d], s_y.at[q - 1, 0], r_y.at[q - 1, 0],
            oi * INNER + lax.rem(ii + q, INNER), t,
        )
        copy.start()
        y_copies.append(copy)
    core_copy = remote(x_ref, x_all.at[t], s_c, r_c, d, other)
    core_copy.start()
    local = []
    for n, (src, dst) in enumerate(
        (
            (small_ref, small_all.at[d]),
            (x_ref, x_all.at[t]),
            (w_pack, w_all.at[d]),
            (up_ref.at[:, low_half], w_ul.at[oi, ii, xi, ci]),
            (down_ref.at[:, low_half], w_dl.at[oi, ii, xi, ci]),
            (up_ref.at[:, high_half], w_uh.at[oi, ii]),
            (down_ref.at[:, high_half], w_dh.at[oi, xi]),
            (out_pack, w_out.at[oi, ii, xi, ci]),
        )
    ):
        copy = pltpu.make_async_copy(src, dst, s_l.at[n])
        copy.start()
        local.append(copy)

    up_low.start(0)

    local[0].wait()
    for copy in s_copies:
        copy.wait()
    cond = small_all[:, 0, cond_at : cond_at + ada_ref.shape[1]]
    for s in range(n_d):
        cond_ref[:, s : s + 1] = cond[s : s + 1].T
    bias = small_ref[:, bias_at : bias_at + ada_ref.shape[0]]
    mod_rows[:, 0, :] = dot(cond.astype(BF16), ada_ref[...], 1, 1) + bias
    own_mod = pltpu.make_async_copy(mod_rows.at[d], mod_all.at[d], s_l.at[8])
    own_mod.start()
    m_copies = []
    for r in range(1, n_d):
        peer = lax.rem(d + r, n_d)
        copy = remote(mod_rows.at[peer], mod_all.at[d], s_m.at[r - 1], r_m.at[r - 1], peer, t)
        copy.start()
        m_copies.append(copy)
    for r in range(1, no):
        z_copies[r - 1].wait()
        origin = lax.rem(oi + no - r, no) * INNER + ii
        for q in range(1, INNER):
            copy = remote(
                w_all.at[origin], w_all.at[origin], s_y.at[q - 1, r], r_y.at[q - 1, r],
                oi * INNER + lax.rem(ii + q, INNER), t,
            )
            copy.start()
            y_copies.append(copy)
    for n in (3, 4, 7):
        local[n].wait()
    down_low.advance(0)
    up_low.advance(0)
    out_all.start(0)
    f_copies = []
    for r, p, copy in x_copies:
        copy.wait()
        origin = lax.rem(xi + nx - r, nx) * CORES + ci
        at = pl.ds(p * piece, piece)
        copy = remote(
            x_all.at[origin, at], x_all.at[origin, at],
            s_f.at[r - 1, p], r_f.at[r - 1, p], d, other,
        )
        copy.start()
        f_copies.append(copy)

    for copy in m_copies + [own_mod]:
        copy.wait()
    def put(first, piece_of, count):
        for s in range(n_d):
            value = piece_of(s)
            start = s * count
            done = 0
            while done < count:
                row, column = divmod(start + done, features)
                take = min(count - done, features - column)
                vec_ref[first + row : first + row + 1, column : column + take] = value[
                    :, done : done + take
                ]
                done += take

    vec_ref[...] = jnp.zeros_like(vec_ref)
    at = 0
    for first, count in sizes:
        put(first, lambda s: small_all[s, :, at : at + count], count)
        at += count
    columns = ada_ref.shape[0]
    for s in range(n_d):
        done = 0
        while done < columns:
            row, column = divmod(s * columns + done, features)
            take = min(columns - done, features - column)
            row = MOD_ROWS[row]
            vec_ref[row : row + 1, column : column + take] = mod_all[s, :, done : done + take]
            done += take

    for copy in f_copies + [local[1], core_copy]:
        copy.wait()

    def norm(b, carry):
        x = x_all[b].astype(F32)
        centred = x - mean_rows(x)
        normed = centred * lax.rsqrt(mean_rows(centred * centred) + EPSILON)
        normed = normed * vec_ref[GAIN1 : GAIN1 + 1]
        low = (normed * (1.0 + vec_ref[SCALE_A : SCALE_A + 1]) + vec_ref[SHIFT_A : SHIFT_A + 1])
        in_all[b] = low.astype(BF16)
        return carry

    lax.fori_loop(0, n_t, norm, 0)
    for copy in y_copies + [local[2]]:
        copy.wait()
    wt_ref[...] = w_all[...].reshape(features, 3 * width).T

    for n in (5, 6):
        local[n].wait()
    out_all.advance(0)
    down_high.start(0)
    up_high.start(0)

    def project(b, carry):
        proj = dot(wt_ref[...], in_all[b], 1, 1)
        lanes = pl.ds(pl.multiple_of(b * rows, rows), rows)
        cos, sin = cos_ref[:, lanes], sin_ref[:, lanes]
        for j in range(2):
            factor = HEAD_DIM**-0.5 if j == 0 else 1.0
            for h in range(heads):
                at = j * width + h * HEAD_DIM
                first, last = proj[at : at + half], proj[at + half : at + HEAD_DIM]
                top = ((first * cos - last * sin) * factor).astype(BF16)
                bottom = ((last * cos + first * sin) * factor).astype(BF16)
                proj_ref[b, at : at + half] = top
                proj_ref[b, at + half : at + HEAD_DIM] = bottom
                if j == 1:
                    key_ref[h, lanes, :] = jnp.concatenate([top, bottom], axis=0).T
        proj_ref[b, 2 * width :] = proj[2 * width :].astype(BF16)

        @pl.when(b == n_t - 2)
        def _():
            up_low.advance(1)

        return carry

    lax.fori_loop(0, n_t, project, 0)

    def attend(u, carry):
        plane = lax.rem(xi + nx - 1 - u // heads, nx)
        h = lax.rem(u, heads)
        at = pl.ds(pl.multiple_of(h * HEAD_DIM, HEAD_DIM), HEAD_DIM)
        value_at = pl.ds(pl.multiple_of(2 * width + h * HEAD_DIM, HEAD_DIM), HEAD_DIM)
        first = plane * CORES
        query = jnp.concatenate([proj_ref[first + c, at] for c in range(CORES)], axis=1)
        scores = dot(key_ref[h], query, 1, 0)
        top = jnp.max(scores, axis=0, keepdims=True)
        grown = jnp.exp(scores - top)
        total = jnp.sum(grown, axis=0, keepdims=True)
        value = jnp.concatenate([proj_ref[v, value_at] for v in range(n_t)], axis=1)
        mixed = (dot(value, grown.astype(BF16), 1, 0) / total).astype(BF16)
        log_total = top + jnp.log(total)
        for c in range(CORES):
            part = slice(c * rows, (c + 1) * rows)
            mix_ref[first + c, at] = mixed[:, part]
            lse_ref[first + c, pl.ds(h, 1)] = log_total[:, part]
        for r in range(nx):
            @pl.when(u == (nx - r) * heads - 1)
            def _(r=r):
                for c in range(CORES):
                    if r * CORES + c > 0:
                        o_copies[r * CORES + c].start()

        @pl.when(u == 0)
        def _():
            down_low.advance(1)
            out_all.advance(1)

        @pl.when(u == 4)
        def _():
            up_low.advance(2)

        @pl.when(u == 5)
        def _():
            down_high.advance(0)
            up_high.advance(0)
            out_all.advance(2)

        return carry

    o_copies = {}
    for m in range(1, n_t):
        b = order(m, xi, ci, nx)
        o_copies[m] = remote(
            mix_ref.at[b], mix_own.at[t], s_o.at[m - 1], r_o.at[mirror(m, nx) - 1], d, b
        )
    lax.fori_loop(0, nx * heads, attend, 0)
    mine = pltpu.make_async_copy(mix_ref.at[t], mix_own.at[t], s_l.at[9])
    mine.start()
    down_low.advance(2)
    down_high.wait(1)
    up_high.wait(1)
    for one in (out_all, up_low, down_low):
        one.wait(3)
    mine.wait()
    for copy in list(o_copies.values()):
        copy.wait()


def front_call(x, qkv, small, ada_t, up, down_t, outw, cos, sin, cond_at, bias_at, sizes, n_d, n_t):
    parts = 4
    nx, no = n_t // CORES, n_d // INNER
    rows, features = x.shape
    part, width = qkv.shape[1:]
    heads = width // HEAD_DIM
    length = rows * n_t
    wide = -(-width // 128) * 128
    units = up.shape[1]
    steps = max(no, INNER, nx) - 1
    cut = units // 2
    grid_of = (no, INNER, nx, CORES, part)
    columns = ada_t.shape[0]
    return pl.pallas_call(
        partial(front_kernel, n_d, n_t, parts, heads, cond_at, bias_at, sizes),
        name="front",
        out_shape=[
            struct((n_t, rows, features), BF16),
            struct((n_t, 3 * width, rows), BF16),
            struct((n_t, width, rows), BF16),
            struct((n_t, heads, rows), F32),
            struct((n_t, width, rows), BF16),
            struct((16, features), F32),
            struct((ada_t.shape[1], n_d), F32),
            struct((n_d, part, 3 * width), BF16),
            struct(grid_of + (cut,), BF16),
            struct(grid_of + (cut,), BF16),
            struct((no, INNER, part, cut), BF16),
            struct((no, nx, part, cut), BF16),
            struct(grid_of + (wide,), BF16),
        ],
        in_specs=[VMEM, VMEM, VMEM, VMEM, ANY, ANY, VMEM, VMEM, VMEM],
        out_specs=[VMEM] * 8 + [ANY] * 5,
        scratch_shapes=[
            pltpu.VMEM((n_t, rows, features), BF16),
            pltpu.VMEM((part, 3 * width), BF16),
            pltpu.VMEM((3 * width, features), BF16),
            pltpu.VMEM((part, wide), BF16),
            pltpu.VMEM((n_d,) + small.shape, F32),
            pltpu.VMEM((n_d, 1, columns), F32),
            pltpu.VMEM((n_d, 1, columns), F32),
            pltpu.VMEM((heads, length, HEAD_DIM), BF16),
            DMA((nx - 1, parts)), DMA((nx - 1, parts)), DMA, DMA,
            DMA((nx - 1, parts)), DMA((nx - 1, parts)),
            DMA((no - 1,)), DMA((no - 1,)),
            DMA((INNER - 1, no)), DMA((INNER - 1, no)),
            DMA((n_d - 1,)), DMA((n_d - 1,)), DMA((n_d - 1,)), DMA((n_d - 1,)),
            DMA((10,)),
            DMA((20, steps)), DMA((20, steps)),
            DMA((n_t - 1,)), DMA((n_t - 1,)),
        ],
        compiler_params=params(0),
        cost_estimate=cost(20 * heads * length * length * HEAD_DIM, 40e6, heads * length * length),
    )(x, qkv, small, ada_t, up, down_t, outw, cos, sin)


def middle_kernel(
    n_d, n_t,
    mix_ref, x_ref, g_ref, vec_ref, ul_ref, dl_ref, uh_ref, dh_ref, wout_ref,
    out_ref, dmid_ref, dmix_ref, stat_ref, hul_ref, hdl_ref, huh_ref, hdh_ref, gout_ref,
    up_buf, down_buf, o_buf, go_buf,
    attn_ref, low_ref, lowt_ref, dl_t_ref, dlt_ref, acc_out, acc_in,
    mul_c, rul, mul_x, mdl_c, mdl_y, rdl, muh, mdh,
    s_u, s_d, s_o, s_w, r_w, s_r, r_r,
):
    places = Places(n_d, n_t)
    count, me = places.count, places.me
    rows, features = x_ref.shape
    width = mix_ref.shape[1]
    cut = up_buf.shape[-1]
    wide = wout_ref.shape[-1]
    loads = [
        pltpu.make_async_copy(wout_ref, o_buf, s_o.at[0]),
        pltpu.make_async_copy(ul_ref, up_buf.at[0], s_u.at[0]),
        pltpu.make_async_copy(dl_ref, down_buf.at[0], s_d.at[0]),
        pltpu.make_async_copy(uh_ref, up_buf.at[1, :, :, me["x"], me["c"]], s_u.at[1]),
        pltpu.make_async_copy(dh_ref, down_buf.at[1, :, me["y"], :, me["c"]], s_d.at[1]),
    ]
    for copy in loads:
        copy.start()
    greet(n_d, n_t)
    up_high = Spread(places, "zyxc", "zy", "xc", up_buf.at[1], uh_ref, s_w, r_w, 0)
    down_high = Spread(places, "zyxc", "zx", "yc", down_buf.at[1], dh_ref, s_w, r_w, 2)
    up_high.start(0)
    down_high.start(0)
    nx = count["x"]
    planes = [lax.rem(me["x"] + nx - 1 - n, nx) for n in range(nx)]
    ul = [
        Reduce(
            places, "zyc", "c", up_buf.at[2, :, :, planes[n]], None, [mul_c.at[n]], [rul.at[n]],
            s_r, r_r, None, n,
        )
        for n in range(nx)
    ]
    ul_x = [
        remote(
            rul.at[nx - 1 - r], mul_x.at[r - 1], s_r.at[4 * nx + 2, r - 1], r_r.at[4 * nx + 2, r - 1],
            *places.peer("x", r)[1],
        )
        for r in range(1, nx)
    ]
    dl = [
        Reduce(
            places, "zyc", "c", down_buf.at[2, :, :, planes[n]], None, [mdl_c.at[n]],
            [rdl.at[:, :, planes[n]]], s_r, r_r, None, nx + n,
        )
        for n in range(nx)
    ]
    dl_y = Reduce(
        places, "zyx", "y", rdl, None, [mdl_y], [rdl.at[:, me["y"]]], s_r, r_r, None, 2 * nx
    )
    high_up, high_down = up_buf.at[0, :, :, :, me["c"]], down_buf.at[0, :, :, :, me["c"]]
    uh = Reduce(places, "zyxc", "c", up_buf.at[0], None, [muh], [high_up], s_r, r_r, None, 2 * nx + 1)
    dh = Reduce(
        places, "zyxc", "c", down_buf.at[0], None, [mdh], [high_down], s_r, r_r, None, 2 * nx + 2
    )
    keeps = [
        pltpu.make_async_copy(go_buf, gout_ref, s_o.at[1]),
        pltpu.make_async_copy(high_up, huh_ref, s_o.at[2]),
        pltpu.make_async_copy(high_down, hdh_ref, s_o.at[3]),
        pltpu.make_async_copy(rul.at[nx - 1], hul_ref, s_o.at[4]),
        pltpu.make_async_copy(rdl.at[:, me["y"]], hdl_ref, s_o.at[5]),
    ]
    vec = lambda row: vec_ref[row : row + 1]
    cot = g_ref[...].astype(F32)
    d_mlp = (vec(GATE_M) * cot).astype(BF16)
    dl_t_ref[...] = d_mlp
    dlt_ref[...] = d_mlp.T
    stat_ref[...] = jnp.zeros_like(stat_ref)
    stat_ref[S_B_DOWN : S_B_DOWN + 1] = sum_tokens(d_mlp.astype(F32))
    if wide > width:
        go_buf[...] = jnp.zeros_like(go_buf)
    loads[0].wait()
    w_out = lambda b: o_buf[:, :, b // CORES, b % CORES].reshape(features, wide)[:, :width]
    attn_out = jnp.zeros((rows, features), F32)
    for b in range(n_t):
        attn_out += dot(mix_ref[b].T, w_out(b), 1, 1)
    attn_ref[...] = attn_out
    branch = vec(GATE_A) * attn_out
    stat_ref[S_SQ_A : S_SQ_A + 1] = sum_tokens(branch * branch)
    middle = x_ref[...].astype(F32) + branch
    dmid_ref[...] = middle
    centred = middle - mean_rows(middle)
    inv = lax.rsqrt(mean_rows(centred * centred) + EPSILON)
    low = (centred * inv * vec(GAIN2) * (1.0 + vec(SCALE_M)) + vec(SHIFT_M)).astype(BF16)
    low_ref[...] = low
    lowt_ref[...] = low.T
    acc_out[...] = jnp.zeros_like(acc_out)
    acc_in[...] = jnp.zeros_like(acc_in)
    loads[1].wait()
    loads[2].wait()

    def block(n, carry):
        j, p = n // nx, lax.rem(me["x"] + nx - 1 - lax.rem(n, nx), nx)
        slot = 2 - 2 * j
        lanes = pl.ds(pl.multiple_of(j * cut, cut), cut)

        @pl.when(n == nx)
        def _():
            for one in (up_high, down_high):
                one.wait(1)

        both = lambda buf: jnp.concatenate(
            [buf[j, :, :, p, c].reshape(features, cut) for c in range(CORES)], axis=1
        )
        up, down = both(up_buf), both(down_buf)
        bias = jnp.concatenate(
            [vec_ref[pl.ds(B_UP + p * CORES + c, 1), lanes] for c in range(CORES)], axis=1
        )
        hidden = dot(low_ref[...], up, 1, 0) + bias
        square = hidden * hidden
        bent = jnp.tanh(GELU_C * hidden * (1.0 + GELU_A * square))
        half = 0.5 * (1.0 + bent)
        active = (hidden * half).astype(BF16)
        slope = half + (0.5 * GELU_C) * hidden * (1.0 - bent * bent) * (
            1.0 + (3.0 * GELU_A) * square
        )
        acc_out[...] += dot(active, down, 1, 1)
        grad_down = dot(dlt_ref[...], active, 1, 0).astype(BF16)
        d_hidden = (dot(dl_t_ref[...], down, 1, 0) * slope).astype(BF16)
        sums = sum_tokens(d_hidden.astype(F32))
        for c in range(CORES):
            stat_ref[pl.ds(S_B_UP + p * CORES + c, 1), lanes] = sums[:, c * cut : (c + 1) * cut]
        grad_up = dot(lowt_ref[...], d_hidden, 1, 0).astype(BF16)
        acc_in[...] += dot(d_hidden, up, 1, 1)
        for c in range(CORES):
            lanes_of = slice(c * cut, (c + 1) * cut)
            shape = up_buf.shape[1:3] + (-1, cut)
            down_buf[slot, :, :, p, c] = grad_down[:, lanes_of].reshape(shape)
            up_buf[slot, :, :, p, c] = grad_up[:, lanes_of].reshape(shape)

        for m in range(nx):
            @pl.when(n == m)
            def _(m=m):
                if m == nx - 1:
                    for copy in loads[3:]:
                        copy.wait()
                    for one in (up_high, down_high):
                        one.advance(0)
                ul[m].start(0)
                dl[m].start(0)
                if m > 0:
                    ul[m - 1].advance(0)
                    ul_x[nx - 1 - m].start()
                    dl[m - 1].advance(0)

        @pl.when(n == nx)
        def _():
            dl[nx - 1].advance(0)
            dl_y.start(0)
            ul[nx - 1].advance(0)

        return carry

    lax.fori_loop(0, 2 * nx, block, 0)
    uh.start(0)
    dh.start(0)
    middle = dmid_ref[...]
    mlp_out = acc_out[...] + vec(B_DOWN)
    mlp_branch = vec(GATE_M) * mlp_out
    result = middle + mlp_branch
    out_ref[...] = result.astype(BF16)
    cot = g_ref[...].astype(F32)
    stat_ref[S_SQ_M : S_SQ_M + 1] = sum_tokens(mlp_branch * mlp_branch)
    stat_ref[S_SQ_R : S_SQ_R + 1] = sum_tokens(result * result)
    stat_ref[S_GATE_M : S_GATE_M + 1] = sum_tokens(cot * mlp_out)
    e = acc_in[...]
    centred = middle - mean_rows(middle)
    inv = lax.rsqrt(mean_rows(centred * centred) + EPSILON)
    nhat = centred * inv
    gain, scale = vec(GAIN2), 1.0 + vec(SCALE_M)
    by_nhat = sum_tokens(e * nhat)
    stat_ref[S_SHIFT_M : S_SHIFT_M + 1] = sum_tokens(e)
    stat_ref[S_SCALE_M : S_SCALE_M + 1] = by_nhat * gain
    stat_ref[S_GAIN2 : S_GAIN2 + 1] = by_nhat * scale
    dn = e * (scale * gain)
    d_middle = cot + inv * (dn - mean_rows(dn) - nhat * mean_rows(dn * nhat))
    dmid_ref[...] = d_middle
    stat_ref[S_GATE_A : S_GATE_A + 1] = sum_tokens(d_middle * attn_ref[...])
    d_attn = (vec(GATE_A) * d_middle).astype(BF16)
    d_attn_t = d_attn.T
    for b in range(n_t):
        dmix_ref[b] = dot(d_attn, w_out(b), 1, 0).astype(BF16).T
        go_buf[b % CORES, :, :, b // CORES, :, :width] = (
            dot(d_attn_t, mix_ref[b], 1, 1).astype(BF16).reshape(go_buf.shape[1:3] + (-1, width))
        )
    keeps[0].start()
    uh.advance(0)
    keeps[1].start()
    dh.advance(0)
    keeps[2].start()
    for one in ul_x:
        one.wait()
    no = count["z"]

    def fold(n, carry):
        at = (n // INNER, lax.rem(n, INNER))
        value = rul[(nx - 1,) + at].astype(F32)
        for r in range(nx - 1):
            value += mul_x[(r,) + at].astype(F32)
        rul[(nx - 1,) + at] = value.astype(BF16)
        return carry

    lax.fori_loop(0, no * INNER, fold, 0)
    keeps[3].start()
    dl_y.advance(0)
    keeps[4].start()
    for copy in keeps:
        copy.wait()


def middle_call(mix, x, g, vecs, w_ul, w_dl, w_uh, w_dh, w_out, stat_rows, n_d, n_t):
    rows, features = x.shape
    cut = w_ul.shape[-1]
    part, wide = w_out.shape[-2:]
    width = mix.shape[1]
    count = counts(n_d, n_t)
    no, nx = count["z"], count["x"]
    per = (3,) + w_ul.shape
    plane = (no, INNER, part, cut)
    tail = (part, cut)
    g_out = (CORES, no, INNER, nx, part, wide)
    return pl.pallas_call(
        partial(middle_kernel, n_d, n_t),
        name="middle",
        out_shape=[
            struct((rows, features), BF16),
            struct((rows, features), F32),
            struct((n_t, width, rows), BF16),
            struct((stat_rows, features), F32),
            struct((no, INNER) + tail, BF16),
            struct((no, nx) + tail, BF16),
            struct((no, INNER, nx) + tail, BF16),
            struct((no, INNER, nx) + tail, BF16),
            struct(g_out, BF16),
        ],
        in_specs=[VMEM] * 4 + [ANY] * 5,
        out_specs=[VMEM] * 4 + [ANY] * 5,
        scratch_shapes=[
            pltpu.VMEM(per, BF16), pltpu.VMEM(per, BF16), pltpu.VMEM(w_out.shape, BF16),
            pltpu.VMEM(g_out, BF16),
            pltpu.VMEM((rows, features), F32),
            pltpu.VMEM((rows, features), BF16),
            pltpu.VMEM((features, rows), BF16),
            pltpu.VMEM((rows, features), BF16),
            pltpu.VMEM((features, rows), BF16),
            pltpu.VMEM((rows, features), F32),
            pltpu.VMEM((rows, features), F32),
        ]
        + [
            pltpu.VMEM((nx, 1) + plane, BF16), pltpu.VMEM((nx,) + plane, BF16),
            pltpu.VMEM((nx - 1,) + plane, BF16),
            pltpu.VMEM((nx, 1) + plane, BF16), pltpu.VMEM((INNER - 1, no, nx) + tail, BF16),
            pltpu.VMEM((no, INNER, nx) + tail, BF16),
            pltpu.VMEM((1, no, INNER, nx) + tail, BF16),
            pltpu.VMEM((1, no, INNER, nx) + tail, BF16),
        ]
        + [
            DMA((2,)), DMA((2,)), DMA((6,)),
            DMA((4, max(nx, INNER, CORES) - 1)), DMA((4, max(nx, INNER, CORES) - 1)),
            DMA((4 * nx + 3, max(nx, INNER, CORES) - 1)), DMA((4 * nx + 3, max(nx, INNER, CORES) - 1)),
        ],
        compiler_params=params(1),
        cost_estimate=cost(2 * rows * features * features * (6 * n_t + 4), 30e6),
    )(mix, x, g, vecs, w_ul, w_dl, w_uh, w_dh, w_out)


def back_kernel(
    n_d, n_t, parts, heads,
    dmix_ref, proj_ref, mix_ref, lse_ref, cos_ref, sin_ref, in_hbm, wq_hbm, stat_ref,
    x_hbm, dmid_hbm, vec_ref, ada_ref,
    hul_ref, hdl_ref, huh_ref, hdh_ref, gout_ref,
    grad_in_ref, gq_ref, up_ref, down_ref, out_ref, table_ref, flat_ref, gain_ref, gcond_ref,
    dmix_all, key_ref, keyt_ref, val_ref, dkey_ref, dval_ref, dquery_ref, dproj_ref, in_ref, wq_ref,
    acc_ref, grad_ref, rc, rx, ry, sz, rz, got_ref, mine_ref,
    x_ref, dmid_ref, late_ref, late_got, late_mine, late_all, rows_out, rows_in, *more,
):
    buffers, at = [], 0
    for size in (len(reduce_scratch(CODE, dims, path, (1, 1))) for dims, path in BACK_SUMS):
        buffers.append(more[at : at + size])
        at += size
    (
        s_a, r_a, s_l, s_g, r_g, s_t, r_t, s_d, r_d, s_c, r_c, s_x, r_x, s_y, r_y, s_z, r_z,
        s_v, r_v, s_e, r_e, s_p, r_p,
    ) = more[at:]
    places = Places(n_d, n_t)
    d, t, oi, ii, xi, ci = place(n_d, n_t)
    nx, no = n_t // CORES, n_d // INNER
    other = xi * CORES + (1 - ci)
    blocks, total, rows = proj_ref.shape
    width = total // 3
    half = HEAD_DIM // 2
    features = x_ref.shape[1]
    assert nx == 2 and CORES == 2

    cut = hul_ref.shape[-1]

    def put(target, lanes):
        def store(value):
            target[:, lanes] = value
        return store

    def put_out(value):
        out_ref[...] = value.T[:width]

    sinks = (
        put(up_ref, slice(0, cut)), put(down_ref, slice(0, cut)),
        put(up_ref, slice(cut, 2 * cut)), put(down_ref, slice(cut, 2 * cut)), put_out,
    )
    sums = []
    row = 0
    for n, ((dims, path), source) in enumerate(
        zip(BACK_SUMS, (hul_ref, hdl_ref, huh_ref, hdh_ref, gout_ref))
    ):
        steps = len(path)
        sums.append(
            Reduce(
                places, dims, path, source, buffers[n][0], buffers[n][1 : 1 + steps],
                list(buffers[n][1 + steps :]) + [sinks[n]], s_g, r_g, s_l.at[6 + n], row,
            )
        )
        row += steps
    ul, dl, uh, dh, go = sums

    greet(n_d, n_t)
    a_copies = {}
    for m in range(1, n_t):
        b = order(m, xi, ci, nx)
        a_copies[mirror(m, nx)] = remote(
            dmix_ref.at[b], dmix_all.at[t], s_a.at[m - 1], r_a.at[mirror(m, nx) - 1], d, b
        )
    for m in range(n_t - 1, 0, -1):
        a_copies[mirror(m, nx)].start()
    for one in (dh, go):
        one.start(0)
    loads = [
        pltpu.make_async_copy(dmix_ref.at[t], dmix_all.at[t], s_l.at[0]),
        pltpu.make_async_copy(in_hbm, in_ref, s_l.at[1]),
        pltpu.make_async_copy(wq_hbm, wq_ref, s_l.at[2]),
        pltpu.make_async_copy(x_hbm, x_ref, s_l.at[3]),
        pltpu.make_async_copy(dmid_hbm, dmid_ref, s_l.at[4]),
    ]
    for copy in loads:
        copy.start()
    t_copies = []
    for r in range(1, n_t):
        copy = remote(
            stat_ref, got_ref.at[r - 1], s_t.at[r - 1], r_t.at[r - 1], d, lax.rem(t + r, n_t)
        )
        copy.start()
        t_copies.append(copy)
    d_copies = [pltpu.make_async_copy(mine_ref, table_ref.at[d], s_l.at[5])]
    for r in range(1, n_d):
        d_copies.append(
            remote(mine_ref, table_ref.at[d], s_d.at[r - 1], r_d.at[r - 1], lax.rem(d + r, n_d), t)
        )

    def share_statistics():
        for copy in t_copies:
            copy.wait()
        value = stat_ref[...]
        for r in range(1, n_t):
            value += got_ref[r - 1]
        mine_ref[...] = value
        for copy in d_copies:
            copy.start()

    dkey_ref[...] = jnp.zeros_like(dkey_ref)
    dval_ref[...] = jnp.zeros_like(dval_ref)

    def turn(b, carry):
        lanes = pl.ds(pl.multiple_of(b * rows, rows), rows)
        keyt_ref[:, lanes] = proj_ref[b, width : 2 * width]
        for h in range(heads):
            at = h * HEAD_DIM
            key_ref[h, lanes] = proj_ref[b, width + at : width + at + HEAD_DIM].T
            val_ref[h, lanes] = proj_ref[b, 2 * width + at : 2 * width + at + HEAD_DIM].T
        return carry

    lax.fori_loop(0, blocks, turn, 0)
    loads[0].wait()

    loads[1].wait()
    loads[2].wait()
    dquery_ref[...] = jnp.zeros_like(dquery_ref)
    acc_ref[...] = jnp.zeros_like(acc_ref)
    part_ref = in_ref
    piece = rows // parts
    c_copies = {}
    for r in range(nx):
        block = lax.rem(xi + r, nx) * CORES + 1 - ci
        for p in range(parts):
            at = pl.ds(p * piece, piece)
            c_copies[r, p] = remote(
                part_ref.at[block, at], rc.at[r, at], s_c.at[r, p], r_c.at[r, p], d, other
            )
    x_copies = {}
    for p in range(parts):
        at = pl.ds(p * piece, piece)
        x_copies[p] = remote(
            part_ref.at[lax.rem(xi + 1, nx) * CORES + ci, at], rx.at[0, at],
            s_x.at[0, p], r_x.at[0, p], d, lax.rem(xi + 1, nx) * CORES + ci,
        )

    def unrotate(b, at, factor, first, last):
        lanes = pl.ds(pl.multiple_of(b * rows, rows), rows)
        cos, sin = cos_ref[:, lanes], sin_ref[:, lanes]
        dproj_ref[b, at : at + half] = ((first * cos + last * sin) * factor).astype(BF16)
        dproj_ref[b, at + half : at + HEAD_DIM] = ((last * cos - first * sin) * factor).astype(BF16)

    def close(b):
        lanes = pl.ds(pl.multiple_of(b * rows, rows), rows)
        for h in range(heads):
            at = h * HEAD_DIM
            d_query = dquery_ref[b, at : at + HEAD_DIM]
            unrotate(b, at, HEAD_DIM**-0.5, d_query[:half], d_query[half:])
            d_key = dkey_ref[h, lanes].T
            unrotate(b, width + at, 1.0, d_key[:half], d_key[half:])
            dproj_ref[b, 2 * width + at : 2 * width + at + HEAD_DIM] = (
                dval_ref[h, lanes].T.astype(BF16)
            )
        d_proj = dproj_ref[b]
        acc_ref[...] += dot(d_proj, in_ref[b], 1, 0)
        part_ref[b] = dot(d_proj.T, wq_ref[...], 1, 1).astype(BF16)

    def attend(n, carry):
        for m, at_step in ((1, 1), (2, 2), (3, 4)):
            @pl.when(n == at_step)
            def _(m=m):
                a_copies[m].wait()
        late_part, last_part = (n + 6) // 8, (n + 2) // 8
        q_other = late_part - last_part
        k_other = (1 - late_part) + q_other * lax.rem(n + 1, 2)
        offset = (1 - late_part) * n + q_other * (n // 2 - 1) + last_part * (n - 6)
        i = lax.rem(xi + q_other, nx) * CORES + lax.rem(ci + offset, CORES)
        span = CORES * rows
        keys = pl.ds(pl.multiple_of(lax.rem(xi + k_other, nx) * span, span), span)
        for h in range(heads):
            at = h * HEAD_DIM
            query_t = proj_ref[i, at : at + HEAD_DIM]
            dmix_t = dmix_all[i, at : at + HEAD_DIM]
            mix_t = mix_ref[i, at : at + HEAD_DIM]
            inner = jnp.sum(dmix_t.astype(F32) * mix_t.astype(F32), axis=0, keepdims=True)
            probs = jnp.exp(dot(key_ref[h, keys], query_t, 1, 0) - lse_ref[i, h : h + 1])
            d_probs = dot(val_ref[h, keys], dmix_t, 1, 0)
            d_scores = (probs * (d_probs - inner)).astype(BF16)
            dval_ref[h, keys] += dot(probs.astype(BF16), dmix_t.T, 1, 0)
            dkey_ref[h, keys] += dot(d_scores, query_t.T, 1, 0)
            dquery_ref[i, at : at + HEAD_DIM] += dot(keyt_ref[at : at + HEAD_DIM, keys], d_scores, 1, 0)

        @pl.when(n == 0)
        def _():
            go.advance(0)

        @pl.when(n == 1)
        def _():
            for one in (uh, dl, ul):
                one.start(0)
            share_statistics()

        @pl.when(n == 2)
        def _():
            dh.advance(0)

        @pl.when(n == 5)
        def _():
            dl.advance(0)

        @pl.when((n == 5) | (n == 7))
        def _():
            plane = lax.rem(xi + 1 - last_part, nx)

            def one(c, carry):
                close(plane * CORES + c)
                return carry

            lax.fori_loop(0, CORES, one, 0)

        @pl.when(n == 5)
        def _():
            for p in range(parts):
                c_copies[1, p].start()

        @pl.when(n == 6)
        def _():
            to = lax.rem(xi + 1, nx) * CORES + ci
            for p in range(parts):
                at = pl.ds(p * piece, piece)
                c_copies[1, p].wait()
                part_ref[to, at] = (part_ref[to, at].astype(F32) + rc[1, at].astype(F32)).astype(BF16)
                x_copies[p].start()
            dh.advance(1)
            go.advance(1)
            ul.advance(0)
            uh.advance(0)

        return carry

    lax.fori_loop(0, 2 * n_t, attend, 0)
    for p in range(parts):
        c_copies[0, p].start()
    grad_ref[...] = acc_ref[...].T.astype(BF16).reshape(grad_ref.shape)
    y_copies = []
    for q in range(1, INNER):
        to = lax.rem(ii + q, INNER)
        copy = remote(
            grad_ref.at[:, to], ry.at[q - 1], s_y.at[q - 1], r_y.at[q - 1], oi * INNER + to, t
        )
        copy.start()
        y_copies.append(copy)
    ul.advance(1)
    dl.advance(1)
    dh.advance(2)
    uh.advance(1)
    for copy in d_copies:
        copy.wait()
    loads[3].wait()
    loads[4].wait()
    for copy in y_copies:
        copy.wait()
    z_copies = []
    for r in range(1, no):
        to = lax.rem(oi + r, no)
        value = grad_ref[to, ii].astype(F32)
        for q in range(1, INNER):
            value += ry[q - 1, to].astype(F32)
        sz[r - 1] = value.astype(BF16)
        copy = remote(sz.at[r - 1], rz.at[r - 1], s_z.at[r - 1], r_z.at[r - 1], to * INNER + ii, t)
        copy.start()
        z_copies.append(copy)
    go.advance(2)

    gain, scale = vec_ref[GAIN1 : GAIN1 + 1], 1.0 + vec_ref[SCALE_A : SCALE_A + 1]
    shift_sum = jnp.zeros((1, features), F32)
    nhat_sum = jnp.zeros((1, features), F32)
    for p in range(parts):
        c_copies[0, p].wait()
        x_copies[p].wait()
        at = pl.ds(p * (rows // parts), rows // parts)
        e = part_ref[t, at].astype(F32) + rc[0, at].astype(F32)
        for r in range(1, nx):
            e += rx[r - 1, at].astype(F32)
        x = x_ref[at].astype(F32)
        centred = x - mean_rows(x)
        inv = lax.rsqrt(mean_rows(centred * centred) + EPSILON)
        nhat = centred * inv
        shift_sum += sum_tokens(e)
        nhat_sum += sum_tokens(e * nhat)
        dn = e * (scale * gain)
        grad_in_ref[at, 0, :] = dmid_ref[at] + inv * (
            dn - mean_rows(dn) - nhat * mean_rows(dn * nhat)
        )
    late_ref[:, :features] = shift_sum
    late_ref[:, features : 2 * features] = nhat_sum * gain
    late_ref[:, 2 * features :] = nhat_sum * scale

    copies = []
    for r in range(1, n_t):
        copy = remote(
            late_ref, late_got.at[r - 1], s_v.at[r - 1], r_v.at[r - 1], d, lax.rem(t + r, n_t)
        )
        copy.start()
        copies.append(copy)
    value = late_ref[...]
    for r in range(1, n_t):
        copies[r - 1].wait()
        value += late_got[r - 1]
    late_mine[...] = value
    copies = [pltpu.make_async_copy(late_mine, late_all.at[d], s_l.at[0])]
    for r in range(1, n_d):
        copies.append(
            remote(
                late_mine, late_all.at[d], s_e.at[r - 1], r_e.at[r - 1], lax.rem(d + r, n_d), t
            )
        )
    for copy in copies:
        copy.start()
    go.advance(3)
    for s in range(n_d):
        for block, row in EARLY:
            flat_ref[s : s + 1, block * features : (block + 1) * features] = table_ref[
                s, row : row + 1
            ]
    for copy in copies:
        copy.wait()
    value = late_all[0, :, 2 * features :]
    for s in range(1, n_d):
        value += late_all[s, :, 2 * features :]
    gain_ref[...] = value
    for s in range(n_d):
        flat_ref[s : s + 1, : 2 * features] = late_all[s, :, : 2 * features]
    columns = ada_ref.shape[0]
    moved = pltpu.roll(flat_ref[...], lax.rem(n_d - d, n_d) * columns, 1)[:, :columns]
    rows_out[:, 0, :] = lax.dot_general(
        moved, ada_ref[...].astype(F32), (((1,), (0,)), ((), ())),
        precision=lax.Precision.HIGHEST, preferred_element_type=F32,
    )
    copies = [pltpu.make_async_copy(rows_out.at[d], rows_in.at[d], s_l.at[1])]
    for r in range(1, n_d):
        peer = lax.rem(d + r, n_d)
        copies.append(remote(rows_out.at[peer], rows_in.at[d], s_p.at[r - 1], r_p.at[r - 1], peer, t))
    for copy in copies:
        copy.start()
    uh.advance(2)
    value = grad_ref[oi, ii].astype(F32)
    for q in range(1, INNER):
        value += ry[q - 1, oi].astype(F32)
    for copy in z_copies:
        copy.wait()
    for r in range(1, no):
        value += rz[r - 1].astype(F32)
    for j in range(3):
        gq_ref[j] = value[:, j * width : (j + 1) * width]
    for copy in copies:
        copy.wait()
    gcond_ref[...] = jnp.sum(rows_in[:, 0, :], axis=0, keepdims=True)


def back_call(
    dmix, proj, mix, lse, cos, sin, attn_in, w_qkv, stat, x, dmid, vecs, ada_t, partial_sums, n_d, n_t
):
    parts = 4
    count = counts(n_d, n_t)
    nx, no = count["x"], count["z"]
    blocks, total, rows = proj.shape
    width = total // 3
    heads = width // HEAD_DIM
    length = blocks * rows
    features = attn_in.shape[2]
    part = features // n_d
    cond_width = ada_t.shape[1]
    cut = partial_sums[0].shape[-1]
    buffers = []
    for (dims, path), source in zip(BACK_SUMS, partial_sums):
        buffers += reduce_scratch(count, dims, path, source.shape[-2:])
    stages = sum(len(path) for _, path in BACK_SUMS)
    widest = max(count.values()) - 1
    late = (1, 3 * features)
    return pl.pallas_call(
        partial(back_kernel, n_d, n_t, parts, heads),
        name="back",
        out_shape=[
            struct((rows, 1, features), F32),
            struct((3, part, width), F32),
            struct((part, 2 * cut), F32),
            struct((part, 2 * cut), F32),
            struct((width, part), F32),
            struct((n_d,) + stat.shape, F32),
            struct((n_d, 6 * features), F32),
            struct((1, features), F32),
            struct((1, cond_width), F32),
        ],
        in_specs=[VMEM] * 6 + [ANY] * 2 + [VMEM] + [ANY] * 2 + [VMEM] * 2 + [ANY] * 5,
        out_specs=[VMEM] * 9,
        scratch_shapes=[
            pltpu.VMEM(dmix.shape, BF16),
            pltpu.VMEM((heads, length, HEAD_DIM), BF16),
            pltpu.VMEM((width, length), BF16),
            pltpu.VMEM((heads, length, HEAD_DIM), BF16),
            pltpu.VMEM((heads, length, HEAD_DIM), F32),
            pltpu.VMEM((heads, length, HEAD_DIM), F32),
            pltpu.VMEM((n_t, width, rows), F32),
            pltpu.VMEM(proj.shape, BF16),
            pltpu.VMEM(attn_in.shape, BF16),
            pltpu.VMEM(w_qkv.shape, BF16),
            pltpu.VMEM((total, features), F32),
            pltpu.VMEM((no, INNER, part, total), BF16),
            pltpu.VMEM((nx, rows, features), BF16),
            pltpu.VMEM((nx - 1, rows, features), BF16),
            pltpu.VMEM((INNER - 1, no, part, total), BF16),
            pltpu.VMEM((no - 1, part, total), BF16),
            pltpu.VMEM((no - 1, part, total), BF16),
            pltpu.VMEM((n_t - 1,) + stat.shape, F32),
            pltpu.VMEM(stat.shape, F32),
            pltpu.VMEM(x.shape, BF16),
            pltpu.VMEM(x.shape, F32),
            pltpu.VMEM(late, F32),
            pltpu.VMEM((n_t - 1,) + late, F32),
            pltpu.VMEM(late, F32),
            pltpu.VMEM((n_d,) + late, F32),
            pltpu.VMEM((n_d, 1, cond_width), F32),
            pltpu.VMEM((n_d, 1, cond_width), F32),
        ]
        + buffers
        + [
            DMA((n_t - 1,)), DMA((n_t - 1,)), DMA((6 + len(BACK_SUMS),)),
            DMA((stages, widest)), DMA((stages, widest)),
            DMA((n_t - 1,)), DMA((n_t - 1,)), DMA((n_d - 1,)), DMA((n_d - 1,)),
            DMA((nx, parts)), DMA((nx, parts)), DMA((nx - 1, parts)), DMA((nx - 1, parts)),
            DMA((INNER - 1,)), DMA((INNER - 1,)), DMA((no - 1,)), DMA((no - 1,)),
            DMA((n_t - 1,)), DMA((n_t - 1,)), DMA((n_d - 1,)), DMA((n_d - 1,)),
            DMA((n_d - 1,)), DMA((n_d - 1,)),
        ],
        compiler_params=params(2),
        cost_estimate=cost(45 * heads * length * length * HEAD_DIM, 40e6, heads * length * length),
    )(dmix, proj, mix, lse, cos, sin, attn_in, w_qkv, stat, x, dmid, vecs, ada_t, *partial_sums)


def finish_kernel(
    count, n_units, table_ref, flat_ref, cond_ref, gain_in, gcond_in,
    ada_ref, bias_ref, gain1_ref, gain2_ref, bdown_ref, bup_ref, root_ref, gcond_ref,
):
    n_d = table_ref.shape[0]
    features = table_ref.shape[2]
    total = table_ref[0]
    for s in range(1, n_d):
        total += table_ref[s]
    for k, row in enumerate((S_SQ_A, S_SQ_M, S_SQ_R)):
        root_ref[k : k + 1] = jnp.broadcast_to(
            jnp.sqrt(jnp.sum(total[row : row + 1], axis=1, keepdims=True) / count),
            (1, root_ref.shape[1]),
        )
    gain2_ref[...] = total[S_GAIN2]
    bdown_ref[...] = total[S_B_DOWN]
    for u in range(n_units):
        bup_ref[u * features : (u + 1) * features] = total[S_B_UP + u]
    gain1_ref[...] = gain_in[0]
    gcond_ref[...] = gcond_in[...]
    for block in range(6):
        at = slice(block * features, (block + 1) * features)
        value = jnp.zeros((cond_ref.shape[0], features), F32)
        for s in range(n_d):
            value += cond_ref[:, s : s + 1] * flat_ref[s : s + 1, at]
        ada_ref[:, at] = value
        bias_ref[at] = jnp.sum(flat_ref[:, at], axis=0)


def finish_call(table, flat, cond_t, gain, gcond, count, n_units):
    features = table.shape[2]
    width = cond_t.shape[0]
    return pl.pallas_call(
        partial(finish_kernel, count, n_units),
        name="finish",
        out_shape=[
            struct((width, 6 * features), F32),
            struct((6 * features,), F32),
            struct((features,), F32),
            struct((features,), F32),
            struct((features,), F32),
            struct((n_units * features,), F32),
            struct((3, 128), F32),
            struct((1, width), F32),
        ],
        in_specs=[VMEM] * 5,
        out_specs=[VMEM] * 8,
        compiler_params=params(),
        cost_estimate=cost(1e7, 4e6),
    )(table, flat, cond_t, gain, gcond)


def shards(
    block_input, condition, modulation_weight, modulation_bias, first_gain, qkv_weight, out_weight,
    second_gain, up_weight, up_bias, down_weight, down_bias, grad_output,
):
    n_t, n_d = lax.axis_size("tensor"), lax.axis_size("dp")
    rows, sequences, features = block_input.shape
    assert sequences == 1
    length = rows * n_t
    part, width = qkv_weight.shape[1:]
    units = up_weight.shape[1]
    assert units == features and n_t % CORES == 0 and n_d % INNER == 0
    x = block_input.reshape(rows, features)
    g = grad_output.reshape(rows, features)
    ada_t = modulation_weight.T

    small = jnp.concatenate([first_gain, second_gain, down_bias, up_bias]).astype(F32)
    cond_at = -(-small.shape[0] // 128) * 128
    bias_at = cond_at + condition.shape[1]
    small = jnp.concatenate(
        [
            small, jnp.zeros((cond_at - small.shape[0],), F32),
            condition[0].astype(F32), modulation_bias.astype(F32),
        ]
    )[None]
    own = first_gain.shape[0]
    sizes = ((GAIN1, own), (GAIN2, own), (B_DOWN, own), (B_UP, up_bias.shape[0]))
    inverse = 10000.0 ** (-np.arange(HEAD_DIM // 2) * 2.0 / HEAD_DIM)
    angles = inverse[:, None] * np.arange(length)[None, :]
    cos, sin = jnp.asarray(np.cos(angles), F32), jnp.asarray(np.sin(angles), F32)

    attn_in, proj, mix, lse, mix_own, vecs, cond_t, w_qkv, w_ul, w_dl, w_uh, w_dh, w_out = front_call(
        x, qkv_weight, small, ada_t, up_weight, down_weight.T, out_weight, cos, sin,
        cond_at, bias_at, sizes, n_d, n_t,
    )
    stat_rows = -(-(S_B_UP + n_t) // 8) * 8
    out, d_middle, d_mix, stat, *partial_sums = middle_call(
        mix_own, x, g, vecs, w_ul, w_dl, w_uh, w_dh, w_out, stat_rows, n_d, n_t
    )
    grad_input, g_qkv, g_up, g_down, g_out, table, flat, gain1, grad_cond = back_call(
        d_mix, proj, mix, lse, cos, sin, attn_in, w_qkv.reshape(features, 3 * width), stat,
        x, d_middle, vecs, ada_t, partial_sums, n_d, n_t,
    )
    grad_ada, grad_ada_b, gain1, gain2, b_down, b_up, roots, grad_cond = finish_call(
        table, flat, cond_t, gain1, grad_cond, float(length * n_d * features), n_t
    )
    return (
        out.reshape(block_input.shape), grad_input, grad_cond, grad_ada, grad_ada_b, gain1, g_qkv,
        g_out, gain2, g_up, b_up, g_down.T, b_down, roots[:, 0],
    )


def solution(mesh):
    in_specs = (
        P("tensor", "dp", None),
        P("dp", None),
        P(None, "dp"),
        P("dp"),
        P("dp"),
        P(None, "dp", "tensor"),
        P("tensor", "dp"),
        P("dp"),
        P("dp", "tensor"),
        P("dp"),
        P("tensor", "dp"),
        P("dp"),
        P("tensor", "dp", None),
    )
    out_specs = (
        P("tensor", "dp", None),
        P("tensor", "dp", None),
        P("dp", None),
        P(),
        P(),
        P(),
        P(None, "dp", "tensor"),
        P("tensor", "dp"),
        P(),
        P("dp", "tensor"),
        P(),
        P("tensor", "dp"),
        P(),
        P(),
    )
    return jax.shard_map(shards, mesh=mesh, in_specs=in_specs, out_specs=out_specs, check_vma=False)
```

time: 269 us -> 236 us (0.88)
  Pallas kernels: 250 us -> 226 us
  local copies, waits for them, and re-layouts: 14.8 us -> 7.5 us
    pallas_call x1, Pallas kernels: 97.7 us -> 82.8 us  [front_call(): pl.pallas_call(partial(front_kernel, n_d, n_t, parts, heads, cond_at, bia...]
    pallas_call x3, Pallas kernels: 153 us -> 143 us  [the longest x1 92.4 us: back_call(): pl.pallas_call(partial(back_kernel, n_d, n_t, parts, heads), name='back',...]
    unnamed x23 -> x18, local copies, waits for them, and re-layouts: 9.15 us -> 4.83 us
where the time goes in v3:
time: 236 us; the launch traced here: 235 us
  Pallas kernels  226 us (96%)
  local copies, waits for them, and re-layouts  7.5 us (3%)
    pallas_call x1, Pallas kernels, back_call(): pl.pallas_call(partial(back_kernel, n_d, n_t, parts, heads), name='back',...  92.4 us
    pallas_call x1, Pallas kernels, front_call(): pl.pallas_call(partial(front_kernel, n_d, n_t, parts, heads, cond_at, bia...  82.8 us
    pallas_call x1, Pallas kernels, middle_call(): pl.pallas_call(partial(middle_kernel, n_d, n_t), name='middle', out_shape...  46.3 us
    unnamed x18, local copies, waits for them, and re-layouts  4.83 us

profile of v3, /device:TPU:0, one launch (start us, length us, event | category | flops | bytes accessed | tf_op | source)
XLA Modules:
  0.0 235.5 jit_solution(16034310918058458558)
XLA Ops:
  0.6 0.7 bitcast_convert_fusion
  1.3 0.8 maximum_convert_fusion
  2.1 0.8 concatenate.7
  2.8 0.6 broadcast_in_dim.7.small_ref
  3.4 82.8 %front.1 = (bf16[4,512,768]{2,1,0:T(8,128)(2,1)}, bf16[4,576,512]{2,1,0:T(8,128)(2,1)}, bf16[4,192,512]{2,1,0:T(8,128)(2,1)}, f32[4,3,512]{2,1,0:T(4,128)}, bf16...) custom-call(bf16[512,768]{1,0:T(8,128)(2,1)} %bitcast.13, ...), custom_call_target="tpu_custom_call" | custom-call | flops 16106127360 | bytes 40000000 | tf_op jit(solution)/shard_map/front/pallas_call | solution.py:511
  86.3 46.3 %middle.1 = (bf16[512,768]{1,0:T(8,128)(2,1)}, f32[512,768]{1,0:T(8,128)}, bf16[4,192,512]{2,1,0:T(8,128)(2,1)}, f32[16,768]{1,0:T(8,128)}, bf16[4,2,96,384]{3,2...) custom-call(bf16[4,192,512]{2,1,0:T(8,128)(2,1)} %get-tuple-element., ...), custom_call_target="tpu_custom_call" | custom-call | flops 16911433728 | bytes 30000000 | tf_op jit(solution)/shard_map/middle/pallas_call | solution.py:780
  132.6 0.0 copy-start.1
  132.6 92.4 %back.1 = (f32[512,1,768]{2,1,0:T(1,128)}, f32[3,96,192]{2,1,0:T(8,128)}, f32[96,768]{1,0:T(8,128)}, f32[96,768]{1,0:T(8,128)}, f32[192,96]{1,0:T(8,128)}, /*ind...) custom-call(bf16[4,192,512]{2,1,0:T(8,128)(2,1)} %get-tuple-element.61.dmix_ref, ...), custom_call_target="tpu_custom_call" | custom-call | flops 36238786560 | bytes 40000000 | tf_op jit(solution)/shard_map/back/pallas_call | solution.py:1196
  225.0 0.0 copy-start
  225.0 4.3 %finish.1 = (f32[128,4608]{1,0:T(8,128)}, f32[4608]{0:T(1024)}, f32[768]{0:T(1024)}, f32[768]{0:T(1024)}, f32[768]{0:T(1024)}, /*index=5*/f32[3072]{0:T(1024)}, f32[3,128]{1,0:T(4,128)}, f32[1,128]{1,0:T(1,128)}) custom-call(f32[8,16,768]{2,1,0:T(8,128)} %get-tuple-element.75.table_ref, f32[8,4608]{1,0:T(8,128)} %get-tuple-element.76.flat_ref, ...), custom_call_target="tpu_custom_call" | custom-call | flops 10000000 | bytes 4000000 | tf_op jit(solution)/shard_map/finish/pallas_call | solution.py:1288
  229.3 1.3 slice_reduce_fusion
  230.6 0.0 copy-done.1
  230.6 0.9 copy.35
  231.5 0.0 copy-done
  231.5 0.0 copy-start.4
  231.5 0.0 copy-start.5
  231.5 0.0 copy-start.3
  231.5 0.0 copy-start.2
  231.5 1.1 copy.36
  232.7 0.0 copy-done.4
  232.7 0.7 copy.37
  233.4 0.0 copy-done.5
  233.4 0.6 copy.38
  234.0 0.0 copy-done.3
  234.0 0.7 copy.39
  234.7 0.0 copy-done.2
  234.8 0.7 copy.40
  (1 shorter events, 0.0 us)
Async XLA Ops:
  132.6 98.0 %copy-start.1 = (bf16[512,768]{1,0:T(8,128)(2,1)S(1)}, bf16[512,768]{1,0:T(8,128)(2,1)}, u32[]{:S(2)}) copy-start(bf16[512,768]{1,0:T(8,128)(2,1)} %get-tuple-element.60) | copy-start | bytes 2359300
  225.0 6.5 %copy-start = (f32[512,1,768]{2,1,0:T(1,128)S(1)}, f32[512,1,768]{2,1,0:T(1,128)}, u32[]{:S(2)}) copy-start(f32[512,1,768]{2,1,0:T(1,128)} %get-tuple-element.107) | copy-start | bytes 4718596
  231.5 1.2 copy-start.4
  231.5 1.9 copy-start.5
  231.5 2.5 %copy-start.3 = (f32[96,768]{1,0:T(8,128)S(1)}, f32[96,768]{1,0:T(8,128)}, u32[]{:S(2)}) copy-start(f32[96,768]{1,0:T(8,128)} %get-tuple-element.115) | copy-start | bytes 884740
  231.5 3.2 %copy-start.2 = (f32[96,768]{1,0:T(8,128)S(1)}, f32[96,768]{1,0:T(8,128)}, u32[]{:S(2)}) copy-start(f32[96,768]{1,0:T(8,128)} %get-tuple-element.89) | copy-start | bytes 884740

commit v4 on v3

--- a/solution.py
+++ b/solution.py
@@ -222,6 +222,19 @@
     return [pltpu.VMEM(shape, BF16) for shape in shapes]
 
 
+FRONT_PATHS = {"ul": "zyxc", "dl": "xzyc", "o": "xzyc", "uh": "zy", "dh": "zx"}
+FRONT_PLAN = {
+    "pre": ("s dl",),
+    "0": ("s ul",),
+    "qz": ("a dl", "a ul",),
+    "n": ("s o",),
+    "g": ("a o",),
+    "p3": ("a dl", "a ul",),
+    "a0": ("s uh", "s dh",),
+    "a2": ("a o",),
+    "a5": ("a dl", "a ul", "a uh", "a dh",),
+    "end": ("a o", "a dl", "a ul", "a o", "a uh", "a dh",),
+}
 BACK_SUMS = (("zy", "zy"), ("zx", "xz"), ("zyx", "xyz"), ("zyx", "yxz"), ("czyx", "czxy"))
 CODE = {"z": 2, "y": 2, "x": 2, "c": 2}
 EARLY = ((2, S_GATE_A), (3, S_SHIFT_M), (4, S_SCALE_M), (5, S_GATE_M))
@@ -229,9 +242,10 @@
 
 def front_kernel(
     n_d, n_t, parts, heads, cond_at, bias_at, sizes,
-    x_ref, qkv_ref, small_ref, ada_ref, up_ref, down_ref, outw_ref, cos_ref, sin_ref,
+    x_ref, qkv_ref, gain1_ref, gain2_ref, bdown_ref, bup_ref, cond_in, ada_b_ref,
+    ada_ref, up_ref, down_ref, outw_ref, cos_ref, sin_ref,
     in_all, proj_ref, mix_ref, lse_ref, mix_own, vec_ref, cond_ref, w_all, w_ul, w_dl, w_uh, w_dh, w_out,
-    x_all, w_pack, wt_ref, out_pack, small_all, mod_all, mod_rows, key_ref,
+    x_all, w_pack, wt_ref, out_pack, small_ref, small_all, mod_all, mod_rows, key_ref,
     s_x, r_x, s_c, r_c, s_f, r_f, s_z, r_z, s_y, r_y, s_s, r_s, s_m, r_m, s_l,
     s_w, r_w, s_o, r_o,
 ):
@@ -247,18 +261,41 @@
     for j in range(3):
         w_pack[:, j * width : (j + 1) * width] = qkv_ref[j]
     out_pack[:, :width] = outw_ref[...].T
+    small_ref[...] = jnp.zeros_like(small_ref)
+    at = 0
+    for ref in (gain1_ref, gain2_ref, bdown_ref, bup_ref):
+        small_ref[:, at : at + ref.shape[0]] = ref[...].astype(F32).reshape(1, -1)
+        at += ref.shape[0]
+    small_ref[:, cond_at : cond_at + cond_in.shape[1]] = cond_in[...].astype(F32)
+    small_ref[:, bias_at : bias_at + ada_b_ref.shape[0]] = ada_b_ref[...].astype(F32).reshape(1, -1)
     if out_pack.shape[1] > width:
         out_pack[:, width:] = jnp.zeros((out_pack.shape[0], out_pack.shape[1] - width), BF16)
     greet(n_d, n_t)
     places = Places(n_d, n_t)
-    spread = lambda row, dims, path, array, source: Spread(
-        places, dims, "", path, array, source, s_w, r_w, row
-    )
-    up_low = spread(0, "zyxc", "zyxc", w_ul, up_ref.at[:, low_half])
-    down_low = spread(4, "zyxc", "xzyc", w_dl, down_ref.at[:, low_half])
-    out_all = spread(8, "zyxc", "zxyc", w_out, out_pack)
-    up_high = spread(12, "zy", "zy", w_uh, up_ref.at[:, high_half])
-    down_high = spread(16, "zx", "zx", w_dh, down_ref.at[:, high_half])
+    flows = {}
+    for row, (name, dims, array, source) in enumerate(
+        (
+            ("ul", "zyxc", w_ul, up_ref.at[:, low_half]),
+            ("dl", "zyxc", w_dl, down_ref.at[:, low_half]),
+            ("o", "zyxc", w_out, out_pack),
+            ("uh", "zy", w_uh, up_ref.at[:, high_half]),
+            ("dh", "zx", w_dh, down_ref.at[:, high_half]),
+        )
+    ):
+        flows[name] = Spread(
+            places, dims, "", FRONT_PATHS[name], array, source, s_w, r_w, 4 * row
+        )
+    stage = dict.fromkeys(flows, 0)
+
+    def at_point(point):
+        for step in FRONT_PLAN.get(point, ()):
+            what, name = step.split()
+            if what == "s":
+                flows[name].start(0)
+            else:
+                flows[name].advance(stage[name])
+                stage[name] += 1
+
     s_copies = []
     for r in range(1, n_d):
         copy = remote(
@@ -266,7 +303,7 @@
         )
         copy.start()
         s_copies.append(copy)
-    down_low.start(0)
+    at_point("pre")
     x_copies = []
     for r in range(1, nx):
         peer = lax.rem(xi + r, nx) * CORES + ci
@@ -311,7 +348,7 @@
         copy.start()
         local.append(copy)
 
-    up_low.start(0)
+    at_point("0")
 
     local[0].wait()
     for copy in s_copies:
@@ -339,11 +376,9 @@
             )
             copy.start()
             y_copies.append(copy)
-    for n in (3, 4, 7):
+    for n in range(3, 8):
         local[n].wait()
-    down_low.advance(0)
-    up_low.advance(0)
-    out_all.start(0)
+    at_point("qz")
     f_copies = []
     for r, p, copy in x_copies:
         copy.wait()
@@ -356,6 +391,7 @@
         copy.start()
         f_copies.append(copy)
 
+    at_point("X")
     for copy in m_copies + [own_mod]:
         copy.wait()
     def put(first, piece_of, count):
@@ -399,15 +435,12 @@
         return carry
 
     lax.fori_loop(0, n_t, norm, 0)
+    at_point("n")
     for copy in y_copies + [local[2]]:
         copy.wait()
     wt_ref[...] = w_all[...].reshape(features, 3 * width).T
 
-    for n in (5, 6):
-        local[n].wait()
-    out_all.advance(0)
-    down_high.start(0)
-    up_high.start(0)
+    at_point("g")
 
     def project(b, carry):
         proj = dot(wt_ref[...], in_all[b], 1, 1)
@@ -426,9 +459,11 @@
                     key_ref[h, lanes, :] = jnp.concatenate([top, bottom], axis=0).T
         proj_ref[b, 2 * width :] = proj[2 * width :].astype(BF16)
 
-        @pl.when(b == n_t - 2)
-        def _():
-            up_low.advance(1)
+        for m in range(n_t):
+            if f"p{m}" in FRONT_PLAN:
+                @pl.when(b == m)
+                def _(m=m):
+                    at_point(f"p{m}")
 
         return carry
 
@@ -459,20 +494,11 @@
                     if r * CORES + c > 0:
                         o_copies[r * CORES + c].start()
 
-        @pl.when(u == 0)
-        def _():
-            down_low.advance(1)
-            out_all.advance(1)
-
-        @pl.when(u == 4)
-        def _():
-            up_low.advance(2)
-
-        @pl.when(u == 5)
-        def _():
-            down_high.advance(0)
-            up_high.advance(0)
-            out_all.advance(2)
+        for m in range(nx * heads):
+            if f"a{m}" in FRONT_PLAN:
+                @pl.when(u == m)
+                def _(m=m):
+                    at_point(f"a{m}")
 
         return carry
 
@@ -485,17 +511,20 @@
     lax.fori_loop(0, nx * heads, attend, 0)
     mine = pltpu.make_async_copy(mix_ref.at[t], mix_own.at[t], s_l.at[9])
     mine.start()
-    down_low.advance(2)
-    down_high.wait(1)
-    up_high.wait(1)
-    for one in (out_all, up_low, down_low):
-        one.wait(3)
+    at_point("end")
+    for name, flow in flows.items():
+        assert stage[name] == len(flow.path), name
     mine.wait()
     for copy in list(o_copies.values()):
         copy.wait()
 
 
-def front_call(x, qkv, small, ada_t, up, down_t, outw, cos, sin, cond_at, bias_at, sizes, n_d, n_t):
+def front_call(x, qkv, smalls, ada_t, up, down_t, outw, cos, sin, n_d, n_t):
+    cond, ada_b = smalls[4:]
+    sizes = tuple(zip((GAIN1, GAIN2, B_DOWN, B_UP), (a.shape[0] for a in smalls[:4])))
+    cond_at = -(-sum(size for _, size in sizes) // 128) * 128
+    bias_at = cond_at + cond.shape[1]
+    small = bias_at + ada_b.shape[0]
     parts = 4
     nx, no = n_t // CORES, n_d // INNER
     rows, features = x.shape
@@ -526,14 +555,15 @@
             struct((no, nx, part, cut), BF16),
             struct(grid_of + (wide,), BF16),
         ],
-        in_specs=[VMEM, VMEM, VMEM, VMEM, ANY, ANY, VMEM, VMEM, VMEM],
+        in_specs=[VMEM] * 9 + [ANY] * 2 + [VMEM] * 3,
         out_specs=[VMEM] * 8 + [ANY] * 5,
         scratch_shapes=[
             pltpu.VMEM((n_t, rows, features), BF16),
             pltpu.VMEM((part, 3 * width), BF16),
             pltpu.VMEM((3 * width, features), BF16),
             pltpu.VMEM((part, wide), BF16),
-            pltpu.VMEM((n_d,) + small.shape, F32),
+            pltpu.VMEM((1, small), F32),
+            pltpu.VMEM((n_d, 1, small), F32),
             pltpu.VMEM((n_d, 1, columns), F32),
             pltpu.VMEM((n_d, 1, columns), F32),
             pltpu.VMEM((heads, length, HEAD_DIM), BF16),
@@ -548,7 +578,7 @@
         ],
         compiler_params=params(0),
         cost_estimate=cost(20 * heads * length * length * HEAD_DIM, 40e6, heads * length * length),
-    )(x, qkv, small, ada_t, up, down_t, outw, cos, sin)
+    )(x, qkv, *smalls, ada_t, up, down_t, outw, cos, sin)
 
 
 def middle_kernel(
@@ -576,11 +606,36 @@
     for copy in loads:
         copy.start()
     greet(n_d, n_t)
-    up_high = Spread(places, "zyxc", "zy", "xc", up_buf.at[1], uh_ref, s_w, r_w, 0)
-    down_high = Spread(places, "zyxc", "zx", "yc", down_buf.at[1], dh_ref, s_w, r_w, 2)
-    up_high.start(0)
-    down_high.start(0)
     nx = count["x"]
+    every, mx, my, mc = slice(None), me["x"], me["y"], me["c"]
+    taken = [0]
+
+    def send(target, region, axis, r, source=None):
+        at = target.at[(1,) + region]
+        n = taken[0]
+        taken[0] += 1
+        return remote(
+            at if source is None else source, at, s_w.at[n], r_w.at[n], *places.peer(axis, r)[1]
+        )
+
+    own_up = [send(up_buf, (every, every, mx, mc), "c", 1, uh_ref)]
+    own_down = [send(down_buf, (every, my, every, mc), "c", 1, dh_ref)]
+    near_down, far_down, near_on, far_on, far_up = [], [], [], [], []
+    for r in range(1, INNER):
+        near_down.append(send(down_buf, (every, my, mx, mc), "y", r, dh_ref.at[:, mx]))
+        near_on.append(send(down_buf, (every, places.peer("y", r)[0], mx, mc), "c", 1))
+    for r in range(1, nx):
+        far_up.append(send(up_buf, (every, every, mx, mc), "x", r, uh_ref))
+        far_on.append(send(up_buf, (every, every, places.peer("x", r)[0], mc), "c", 1))
+    for r in range(1, INNER):
+        for q in range(1, nx):
+            x_at = places.peer("x", q)[0]
+            far_down.append(send(down_buf, (every, my, x_at, mc), "y", r, dh_ref.at[:, x_at]))
+            far_on.append(
+                send(down_buf, (every, places.peer("y", r)[0], x_at, mc), "c", 1)
+            )
+    for copy in near_down + far_up + own_up + own_down + far_down:
+        copy.start()
     planes = [lax.rem(me["x"] + nx - 1 - n, nx) for n in range(nx)]
     ul = [
         Reduce(
@@ -591,7 +646,7 @@
     ]
     ul_x = [
         remote(
-            rul.at[nx - 1 - r], mul_x.at[r - 1], s_r.at[4 * nx + 2, r - 1], r_r.at[4 * nx + 2, r - 1],
+            rul.at[nx - 1 - r], mul_x.at[r - 1], s_r.at[4 * nx + 3, r - 1], r_r.at[4 * nx + 3, r - 1],
             *places.peer("x", r)[1],
         )
         for r in range(1, nx)
@@ -603,9 +658,13 @@
         )
         for n in range(nx)
     ]
-    dl_y = Reduce(
-        places, "zyx", "y", rdl, None, [mdl_y], [rdl.at[:, me["y"]]], s_r, r_r, None, 2 * nx
-    )
+    dl_y = [
+        Reduce(
+            places, "zy", "y", rdl.at[:, :, planes[n]], None, [mdl_y.at[n]],
+            [rdl.at[:, my, planes[n]]], s_r, r_r, None, 3 * nx + 3 + n,
+        )
+        for n in range(nx)
+    ]
     high_up, high_down = up_buf.at[0, :, :, :, me["c"]], down_buf.at[0, :, :, :, me["c"]]
     uh = Reduce(places, "zyxc", "c", up_buf.at[0], None, [muh], [high_up], s_r, r_r, None, 2 * nx + 1)
     dh = Reduce(
@@ -648,14 +707,21 @@
     loads[2].wait()
 
     def block(n, carry):
-        j, p = n // nx, lax.rem(me["x"] + nx - 1 - lax.rem(n, nx), nx)
+        j = n // nx
+        step = lax.rem(n, nx)
+        p = lax.rem(mx + (1 - j) * (nx - 1 - step) + j * step, nx)
         slot = 2 - 2 * j
         lanes = pl.ds(pl.multiple_of(j * cut, cut), cut)
 
         @pl.when(n == nx)
         def _():
-            for one in (up_high, down_high):
-                one.wait(1)
+            for copy in loads[3:] + own_up + own_down + near_on:
+                copy.wait()
+
+        @pl.when(n == nx + 1)
+        def _():
+            for copy in far_on:
+                copy.wait()
 
         both = lambda buf: jnp.concatenate(
             [buf[j, :, :, p, c].reshape(features, cut) for c in range(CORES)], axis=1
@@ -673,6 +739,24 @@
             1.0 + (3.0 * GELU_A) * square
         )
         acc_out[...] += dot(active, down, 1, 1)
+        for m in range(1, nx):
+            @pl.when(n == m)
+            def _(m=m):
+                ul[m - 1].advance(0)
+                ul_x[nx - 1 - m].start()
+                dl[m - 1].advance(0)
+                dl_y[m - 1].start(0)
+
+        @pl.when(n == nx)
+        def _():
+            ul[nx - 1].advance(0)
+            dl[nx - 1].advance(0)
+            dl_y[nx - 1].start(0)
+            for copy in far_up + far_down:
+                copy.wait()
+            for copy in far_on:
+                copy.start()
+
         grad_down = dot(dlt_ref[...], active, 1, 0).astype(BF16)
         d_hidden = (dot(dl_t_ref[...], down, 1, 0) * slope).astype(BF16)
         sums = sum_tokens(d_hidden.astype(F32))
@@ -689,23 +773,13 @@
         for m in range(nx):
             @pl.when(n == m)
             def _(m=m):
-                if m == nx - 1:
-                    for copy in loads[3:]:
-                        copy.wait()
-                    for one in (up_high, down_high):
-                        one.advance(0)
                 ul[m].start(0)
                 dl[m].start(0)
-                if m > 0:
-                    ul[m - 1].advance(0)
-                    ul_x[nx - 1 - m].start()
-                    dl[m - 1].advance(0)
-
-        @pl.when(n == nx)
-        def _():
-            dl[nx - 1].advance(0)
-            dl_y.start(0)
-            ul[nx - 1].advance(0)
+                if m == 0:
+                    for copy in near_down:
+                        copy.wait()
+                    for copy in near_on:
+                        copy.start()
 
         return carry
 
@@ -760,7 +834,8 @@
 
     lax.fori_loop(0, no * INNER, fold, 0)
     keeps[3].start()
-    dl_y.advance(0)
+    for one in dl_y:
+        one.advance(0)
     keeps[4].start()
     for copy in keeps:
         copy.wait()
@@ -807,15 +882,16 @@
         + [
             pltpu.VMEM((nx, 1) + plane, BF16), pltpu.VMEM((nx,) + plane, BF16),
             pltpu.VMEM((nx - 1,) + plane, BF16),
-            pltpu.VMEM((nx, 1) + plane, BF16), pltpu.VMEM((INNER - 1, no, nx) + tail, BF16),
+            pltpu.VMEM((nx, 1) + plane, BF16), pltpu.VMEM((nx, INNER - 1, no) + tail, BF16),
             pltpu.VMEM((no, INNER, nx) + tail, BF16),
             pltpu.VMEM((1, no, INNER, nx) + tail, BF16),
             pltpu.VMEM((1, no, INNER, nx) + tail, BF16),
         ]
         + [
             DMA((2,)), DMA((2,)), DMA((6,)),
-            DMA((4, max(nx, INNER, CORES) - 1)), DMA((4, max(nx, INNER, CORES) - 1)),
-            DMA((4 * nx + 3, max(nx, INNER, CORES) - 1)), DMA((4 * nx + 3, max(nx, INNER, CORES) - 1)),
+            DMA((2 + 2 * (INNER - 1 + nx - 1 + (INNER - 1) * (nx - 1)),)),
+            DMA((2 + 2 * (INNER - 1 + nx - 1 + (INNER - 1) * (nx - 1)),)),
+            DMA((4 * nx + 4, max(nx, INNER, CORES) - 1)), DMA((4 * nx + 4, max(nx, INNER, CORES) - 1)),
         ],
         compiler_params=params(1),
         cost_estimate=cost(2 * rows * features * features * (6 * n_t + 4), 30e6),
@@ -1104,7 +1180,7 @@
         shift_sum += sum_tokens(e)
         nhat_sum += sum_tokens(e * nhat)
         dn = e * (scale * gain)
-        grad_in_ref[at, 0, :] = dmid_ref[at] + inv * (
+        grad_in_ref[at] = dmid_ref[at] + inv * (
             dn - mean_rows(dn) - nhat * mean_rows(dn * nhat)
         )
     late_ref[:, :features] = shift_sum
@@ -1197,7 +1273,7 @@
         partial(back_kernel, n_d, n_t, parts, heads),
         name="back",
         out_shape=[
-            struct((rows, 1, features), F32),
+            struct((rows, features), F32),
             struct((3, part, width), F32),
             struct((part, 2 * cut), F32),
             struct((part, 2 * cut), F32),
@@ -1254,19 +1330,21 @@
 
 
 def finish_kernel(
-    count, n_units, table_ref, flat_ref, cond_ref, gain_in, gcond_in,
-    ada_ref, bias_ref, gain1_ref, gain2_ref, bdown_ref, bup_ref, root_ref, gcond_ref,
+    count, n_units, n_moved, table_ref, flat_ref, cond_ref, gain_in, gcond_in, *more
 ):
+    sources, more = more[:n_moved], more[n_moved:]
+    ada_ref, bias_ref, gain1_ref, gain2_ref, bdown_ref, bup_ref, root_ref, gcond_ref = more[:8]
+    for src, dst in zip(sources, more[8:]):
+        if len(dst.shape) > len(src.shape):
+            dst[:, 0, :] = src[...]
+        else:
+            dst[...] = src[...]
     n_d = table_ref.shape[0]
     features = table_ref.shape[2]
     total = table_ref[0]
     for s in range(1, n_d):
         total += table_ref[s]
-    for k, row in enumerate((S_SQ_A, S_SQ_M, S_SQ_R)):
-        root_ref[k : k + 1] = jnp.broadcast_to(
-            jnp.sqrt(jnp.sum(total[row : row + 1], axis=1, keepdims=True) / count),
-            (1, root_ref.shape[1]),
-        )
+    root_ref[...] = jnp.sqrt(jnp.sum(total[S_SQ_A : S_SQ_R + 1], axis=1) / count)
     gain2_ref[...] = total[S_GAIN2]
     bdown_ref[...] = total[S_B_DOWN]
     for u in range(n_units):
@@ -1282,11 +1360,14 @@
         bias_ref[at] = jnp.sum(flat_ref[:, at], axis=0)
 
 
-def finish_call(table, flat, cond_t, gain, gcond, count, n_units):
+def finish_call(table, flat, cond_t, gain, gcond, moved, count, n_units):
+    rows, wide = moved[1].shape
+    shapes = [a.shape for a in moved]
+    shapes[1] = (rows, 1, wide)
     features = table.shape[2]
     width = cond_t.shape[0]
     return pl.pallas_call(
-        partial(finish_kernel, count, n_units),
+        partial(finish_kernel, count, n_units, len(moved)),
         name="finish",
         out_shape=[
             struct((width, 6 * features), F32),
@@ -1295,14 +1376,15 @@
             struct((features,), F32),
             struct((features,), F32),
             struct((n_units * features,), F32),
-            struct((3, 128), F32),
+            struct((3,), F32),
             struct((1, width), F32),
-        ],
-        in_specs=[VMEM] * 5,
-        out_specs=[VMEM] * 8,
+        ]
+        + [struct(shape, a.dtype) for a, shape in zip(moved, shapes)],
+        in_specs=[VMEM] * (5 + len(moved)),
+        out_specs=[VMEM] * (8 + len(moved)),
         compiler_params=params(),
         cost_estimate=cost(1e7, 4e6),
-    )(table, flat, cond_t, gain, gcond)
+    )(table, flat, cond_t, gain, gcond, *moved)
 
 
 def shards(
@@ -1320,24 +1402,13 @@
     g = grad_output.reshape(rows, features)
     ada_t = modulation_weight.T
 
-    small = jnp.concatenate([first_gain, second_gain, down_bias, up_bias]).astype(F32)
-    cond_at = -(-small.shape[0] // 128) * 128
-    bias_at = cond_at + condition.shape[1]
-    small = jnp.concatenate(
-        [
-            small, jnp.zeros((cond_at - small.shape[0],), F32),
-            condition[0].astype(F32), modulation_bias.astype(F32),
-        ]
-    )[None]
-    own = first_gain.shape[0]
-    sizes = ((GAIN1, own), (GAIN2, own), (B_DOWN, own), (B_UP, up_bias.shape[0]))
+    smalls = (first_gain, second_gain, down_bias, up_bias, condition, modulation_bias)
     inverse = 10000.0 ** (-np.arange(HEAD_DIM // 2) * 2.0 / HEAD_DIM)
     angles = inverse[:, None] * np.arange(length)[None, :]
     cos, sin = jnp.asarray(np.cos(angles), F32), jnp.asarray(np.sin(angles), F32)
 
     attn_in, proj, mix, lse, mix_own, vecs, cond_t, w_qkv, w_ul, w_dl, w_uh, w_dh, w_out = front_call(
-        x, qkv_weight, small, ada_t, up_weight, down_weight.T, out_weight, cos, sin,
-        cond_at, bias_at, sizes, n_d, n_t,
+        x, qkv_weight, smalls, ada_t, up_weight, down_weight.T, out_weight, cos, sin, n_d, n_t
     )
     stat_rows = -(-(S_B_UP + n_t) // 8) * 8
     out, d_middle, d_mix, stat, *partial_sums = middle_call(
@@ -1347,12 +1418,14 @@
         d_mix, proj, mix, lse, cos, sin, attn_in, w_qkv.reshape(features, 3 * width), stat,
         x, d_middle, vecs, ada_t, partial_sums, n_d, n_t,
     )
-    grad_ada, grad_ada_b, gain1, gain2, b_down, b_up, roots, grad_cond = finish_call(
-        table, flat, cond_t, gain1, grad_cond, float(length * n_d * features), n_t
+    moved = (out, grad_input, g_qkv, g_up, g_down, g_out)
+    grad_ada, grad_ada_b, gain1, gain2, b_down, b_up, roots, grad_cond, *moved = finish_call(
+        table, flat, cond_t, gain1, grad_cond, moved, float(length * n_d * features), n_t
     )
+    out, grad_input, g_qkv, g_up, g_down, g_out = moved
     return (
         out.reshape(block_input.shape), grad_input, grad_cond, grad_ada, grad_ada_b, gain1, g_qkv,
-        g_out, gain2, g_up, b_up, g_down.T, b_down, roots[:, 0],
+        g_out, gain2, g_up, b_up, g_down.T, b_down, roots,
     )
 
 

time: 236 us -> 217 us (0.919)
  Pallas kernels: 226 us -> 216 us
  local copies, waits for them, and re-layouts: 7.5 us -> 0 us
    pallas_call x1, Pallas kernels: 46.3 us -> 39.6 us  [middle_call(): pl.pallas_call(partial(middle_kernel, n_d, n_t), name='middle', out_shape...]
    pallas_call x1, Pallas kernels: 82.8 us -> 77.3 us  [front_call(): pl.pallas_call(partial(front_kernel, n_d, n_t, parts, heads, cond_at, bia...]
    unnamed x18 -> x0, local copies, waits for them, and re-layouts: 4.83 us -> none
where the time goes in v4:
time: 217 us
  Pallas kernels  216 us (100%)
    pallas_call x1, Pallas kernels, back_call(): pl.pallas_call(partial(back_kernel, n_d, n_t, parts, heads), name='back',...  93.1 us
    pallas_call x1, Pallas kernels, front_call(): pl.pallas_call(partial(front_kernel, n_d, n_t, parts, heads, cond_at, bia...  77.3 us
    pallas_call x1, Pallas kernels, middle_call(): pl.pallas_call(partial(middle_kernel, n_d, n_t), name='middle', out_shape...  39.6 us
    pallas_call x1, Pallas kernels, finish_call(): pl.pallas_call(partial(finish_kernel, count, n_units, len(moved)), name='...  6.34 us

profile of v4, /device:TPU:0, one launch (start us, length us, event | category | flops | bytes accessed | tf_op | source)
XLA Modules:
  0.0 217.2 jit_solution(17066022419410829918)
XLA Ops:
  0.6 77.3 %front.1 = (bf16[4,512,768]{2,1,0:T(8,128)(2,1)}, bf16[4,576,512]{2,1,0:T(8,128)(2,1)}, bf16[4,192,512]{2,1,0:T(8,128)(2,1)}, f32[4,3,512]{2,1,0:T(4,128)}, bf16...) custom-call(bf16[512,768]{1,0:T(8,128)(2,1)} %bitcast.8, ...), custom_call_target="tpu_custom_call" | custom-call | flops 16106127360 | bytes 40000000 | tf_op jit(solution)/shard_map/front/pallas_call | solution.py:540
  78.0 39.6 %middle.1 = (bf16[512,768]{1,0:T(8,128)(2,1)}, f32[512,768]{1,0:T(8,128)}, bf16[4,192,512]{2,1,0:T(8,128)(2,1)}, f32[16,768]{1,0:T(8,128)}, bf16[4,2,96,384]{3,2...) custom-call(bf16[4,192,512]{2,1,0:T(8,128)(2,1)} %get-tuple-element., ...), custom_call_target="tpu_custom_call" | custom-call | flops 16911433728 | bytes 30000000 | tf_op jit(solution)/shard_map/middle/pallas_call | solution.py:855
  117.6 93.1 %back.1 = (f32[512,768]{1,0:T(8,128)}, f32[3,96,192]{2,1,0:T(8,128)}, f32[96,768]{1,0:T(8,128)}, f32[96,768]{1,0:T(8,128)}, f32[192,96]{1,0:T(8,128)}, /*index=5...) custom-call(bf16[4,192,512]{2,1,0:T(8,128)(2,1)} %get-tuple-element.66.dmix_ref, ...), custom_call_target="tpu_custom_call" | custom-call | flops 36238786560 | bytes 40000000 | tf_op jit(solution)/shard_map/back/pallas_call | solution.py:1272
  210.7 6.3 %finish.1 = (f32[128,4608]{1,0:T(8,128)}, f32[4608]{0:T(1024)}, f32[768]{0:T(1024)}, f32[768]{0:T(1024)}, f32[768]{0:T(1024)}, /*index=5*/f32[3072]{0:T(1024)}, ...) custom-call(f32[8,16,768]{2,1,0:T(8,128)} %get-tuple-element.79.tabl, ...), custom_call_target="tpu_custom_call" | custom-call | flops 10000000 | bytes 4000000 | tf_op jit(solution)/shard_map/finish/pallas_call | solution.py:1369

commit v5 on v4

--- a/solution.py
+++ b/solution.py
@@ -235,7 +235,22 @@
     "a5": ("a dl", "a ul", "a uh", "a dh",),
     "end": ("a o", "a dl", "a ul", "a o", "a uh", "a dh",),
 }
-BACK_SUMS = (("zy", "zy"), ("zx", "xz"), ("zyx", "xyz"), ("zyx", "yxz"), ("czyx", "czxy"))
+BACK_DIMS = {"ul": "zy", "dl": "zx", "uh": "zyx", "dh": "zyx", "o": "czyx"}
+BACK_PATHS = {"ul": "yz", "dl": "xz", "uh": "xyz", "dh": "yxz", "o": "czxy"}
+BACK_PLAN = {
+    "0": ("s dh", "s o",),
+    "n0": ("a o",),
+    "n1": ("s uh", "s dl", "s ul",),
+    "n2": ("a dh",),
+    "n5": ("a dl", "a ul",),
+    "n6": ("a dh", "a o", "a uh",),
+    "n7": ("a ul", "a dl",),
+    "t4": ("a dh",),
+    "t5": ("a uh", "a o",),
+    "t0": ("a uh",),
+    "t2": ("a o",),
+}
+BACK_SUMS = tuple((BACK_DIMS[name], BACK_PATHS[name]) for name in BACK_DIMS)
 CODE = {"z": 2, "y": 2, "x": 2, "c": 2}
 EARLY = ((2, S_GATE_A), (3, S_SHIFT_M), (4, S_SCALE_M), (5, S_GATE_M))
 
@@ -905,7 +920,8 @@
     hul_ref, hdl_ref, huh_ref, hdh_ref, gout_ref,
     grad_in_ref, gq_ref, up_ref, down_ref, out_ref, table_ref, flat_ref, gain_ref, gcond_ref,
     dmix_all, key_ref, keyt_ref, val_ref, dkey_ref, dval_ref, dquery_ref, dproj_ref, in_ref, wq_ref,
-    acc_ref, grad_ref, rc, rx, ry, sz, rz, got_ref, mine_ref,
+    acc_ref, pair_ref, value_ref, rc, rx, pair_y, pair_z, pair_sum, value_z, value_y, value_mid,
+    got_ref, mine_ref,
     x_ref, dmid_ref, late_ref, late_got, late_mine, late_all, rows_out, rows_in, *more,
 ):
     buffers, at = [], 0
@@ -913,7 +929,7 @@
         buffers.append(more[at : at + size])
         at += size
     (
-        s_a, r_a, s_l, s_g, r_g, s_t, r_t, s_d, r_d, s_c, r_c, s_x, r_x, s_y, r_y, s_z, r_z,
+        s_a, r_a, s_l, s_g, r_g, s_t, r_t, s_d, r_d, s_c, r_c, s_x, r_x,
         s_v, r_v, s_e, r_e, s_p, r_p,
     ) = more[at:]
     places = Places(n_d, n_t)
@@ -953,7 +969,32 @@
             )
         )
         row += steps
-    ul, dl, uh, dh, go = sums
+    flows = dict(zip(BACK_DIMS, sums))
+    stage = dict.fromkeys(flows, 0)
+
+    def at_point(point):
+        for step in BACK_PLAN.get(point, ()):
+            what, name = step.split()
+            if what == "s":
+                flows[name].start(0)
+            else:
+                flows[name].advance(stage[name])
+                stage[name] += 1
+
+    def put_low(value):
+        gq_ref[0] = value[:, :width]
+        gq_ref[1] = value[:, width:]
+
+    def put_high(value):
+        gq_ref[2] = value
+
+    pair = Reduce(
+        places, "zy", "yz", pair_ref, None, [pair_y, pair_z], [pair_sum, put_low], s_g, r_g, None, row
+    )
+    value_sum = Reduce(
+        places, "zy", "zy", value_ref, None, [value_z, value_y], [value_mid, put_high],
+        s_g, r_g, None, row + 2,
+    )
 
     greet(n_d, n_t)
     a_copies = {}
@@ -964,8 +1005,7 @@
         )
     for m in range(n_t - 1, 0, -1):
         a_copies[mirror(m, nx)].start()
-    for one in (dh, go):
-        one.start(0)
+    at_point("0")
     loads = [
         pltpu.make_async_copy(dmix_ref.at[t], dmix_all.at[t], s_l.at[0]),
         pltpu.make_async_copy(in_hbm, in_ref, s_l.at[1]),
@@ -1081,23 +1121,9 @@
             dkey_ref[h, keys] += dot(d_scores, query_t.T, 1, 0)
             dquery_ref[i, at : at + HEAD_DIM] += dot(keyt_ref[at : at + HEAD_DIM, keys], d_scores, 1, 0)
 
-        @pl.when(n == 0)
-        def _():
-            go.advance(0)
-
         @pl.when(n == 1)
         def _():
-            for one in (uh, dl, ul):
-                one.start(0)
             share_statistics()
-
-        @pl.when(n == 2)
-        def _():
-            dh.advance(0)
-
-        @pl.when(n == 5)
-        def _():
-            dl.advance(0)
 
         @pl.when((n == 5) | (n == 7))
         def _():
@@ -1122,46 +1148,32 @@
                 c_copies[1, p].wait()
                 part_ref[to, at] = (part_ref[to, at].astype(F32) + rc[1, at].astype(F32)).astype(BF16)
                 x_copies[p].start()
-            dh.advance(1)
-            go.advance(1)
-            ul.advance(0)
-            uh.advance(0)
+
+        for m in range(2 * n_t):
+            if f"n{m}" in BACK_PLAN:
+                @pl.when(n == m)
+                def _(m=m):
+                    at_point(f"n{m}")
 
         return carry
 
     lax.fori_loop(0, 2 * n_t, attend, 0)
     for p in range(parts):
         c_copies[0, p].start()
-    grad_ref[...] = acc_ref[...].T.astype(BF16).reshape(grad_ref.shape)
-    y_copies = []
-    for q in range(1, INNER):
-        to = lax.rem(ii + q, INNER)
-        copy = remote(
-            grad_ref.at[:, to], ry.at[q - 1], s_y.at[q - 1], r_y.at[q - 1], oi * INNER + to, t
-        )
-        copy.start()
-        y_copies.append(copy)
-    ul.advance(1)
-    dl.advance(1)
-    dh.advance(2)
-    uh.advance(1)
+    grads = acc_ref[...].T.astype(BF16)
+    pair_ref[...] = grads[:, : 2 * width].reshape(pair_ref.shape)
+    value_ref[...] = grads[:, 2 * width :].reshape(value_ref.shape)
+    pair.start(0)
+    value_sum.start(0)
+    at_point("t0")
     for copy in d_copies:
         copy.wait()
     loads[3].wait()
     loads[4].wait()
-    for copy in y_copies:
-        copy.wait()
-    z_copies = []
-    for r in range(1, no):
-        to = lax.rem(oi + r, no)
-        value = grad_ref[to, ii].astype(F32)
-        for q in range(1, INNER):
-            value += ry[q - 1, to].astype(F32)
-        sz[r - 1] = value.astype(BF16)
-        copy = remote(sz.at[r - 1], rz.at[r - 1], s_z.at[r - 1], r_z.at[r - 1], to * INNER + ii, t)
-        copy.start()
-        z_copies.append(copy)
-    go.advance(2)
+    pair.advance(0)
+    at_point("t1")
+    value_sum.advance(0)
+    at_point("t2")
 
     gain, scale = vec_ref[GAIN1 : GAIN1 + 1], 1.0 + vec_ref[SCALE_A : SCALE_A + 1]
     shift_sum = jnp.zeros((1, features), F32)
@@ -1183,6 +1195,7 @@
         grad_in_ref[at] = dmid_ref[at] + inv * (
             dn - mean_rows(dn) - nhat * mean_rows(dn * nhat)
         )
+    at_point("t3")
     late_ref[:, :features] = shift_sum
     late_ref[:, features : 2 * features] = nhat_sum * gain
     late_ref[:, 2 * features :] = nhat_sum * scale
@@ -1208,7 +1221,7 @@
         )
     for copy in copies:
         copy.start()
-    go.advance(3)
+    at_point("t4")
     for s in range(n_d):
         for block, row in EARLY:
             flat_ref[s : s + 1, block * features : (block + 1) * features] = table_ref[
@@ -1234,16 +1247,13 @@
         copies.append(remote(rows_out.at[peer], rows_in.at[d], s_p.at[r - 1], r_p.at[r - 1], peer, t))
     for copy in copies:
         copy.start()
-    uh.advance(2)
-    value = grad_ref[oi, ii].astype(F32)
-    for q in range(1, INNER):
-        value += ry[q - 1, oi].astype(F32)
-    for copy in z_copies:
-        copy.wait()
-    for r in range(1, no):
-        value += rz[r - 1].astype(F32)
-    for j in range(3):
-        gq_ref[j] = value[:, j * width : (j + 1) * width]
+    at_point("t5")
+    pair.advance(1)
+    value_sum.advance(1)
+    at_point("t6")
+    at_point("end")
+    for name, flow in flows.items():
+        assert stage[name] == len(flow.path), name
     for copy in copies:
         copy.wait()
     gcond_ref[...] = jnp.sum(rows_in[:, 0, :], axis=0, keepdims=True)
@@ -1297,12 +1307,12 @@
             pltpu.VMEM(attn_in.shape, BF16),
             pltpu.VMEM(w_qkv.shape, BF16),
             pltpu.VMEM((total, features), F32),
-            pltpu.VMEM((no, INNER, part, total), BF16),
+            pltpu.VMEM((no, INNER, part, 2 * width), BF16),
+            pltpu.VMEM((no, INNER, part, width), BF16),
             pltpu.VMEM((nx, rows, features), BF16),
             pltpu.VMEM((nx - 1, rows, features), BF16),
-            pltpu.VMEM((INNER - 1, no, part, total), BF16),
-            pltpu.VMEM((no - 1, part, total), BF16),
-            pltpu.VMEM((no - 1, part, total), BF16),
+            *reduce_scratch(count, "zy", "yz", (part, 2 * width), own=False),
+            *reduce_scratch(count, "zy", "zy", (part, width), own=False),
             pltpu.VMEM((n_t - 1,) + stat.shape, F32),
             pltpu.VMEM(stat.shape, F32),
             pltpu.VMEM(x.shape, BF16),
@@ -1317,10 +1327,9 @@
         + buffers
         + [
             DMA((n_t - 1,)), DMA((n_t - 1,)), DMA((6 + len(BACK_SUMS),)),
-            DMA((stages, widest)), DMA((stages, widest)),
+            DMA((stages + 4, widest)), DMA((stages + 4, widest)),
             DMA((n_t - 1,)), DMA((n_t - 1,)), DMA((n_d - 1,)), DMA((n_d - 1,)),
             DMA((nx, parts)), DMA((nx, parts)), DMA((nx - 1, parts)), DMA((nx - 1, parts)),
-            DMA((INNER - 1,)), DMA((INNER - 1,)), DMA((no - 1,)), DMA((no - 1,)),
             DMA((n_t - 1,)), DMA((n_t - 1,)), DMA((n_d - 1,)), DMA((n_d - 1,)),
             DMA((n_d - 1,)), DMA((n_d - 1,)),
         ],

time: 217 us -> 215 us (level)
    pallas_call x1, Pallas kernels: 93.1 us -> 90.5 us  [back_call(): pl.pallas_call(partial(back_kernel, n_d, n_t, parts, heads), name='back',...]
where the time goes in v5:
time: 215 us
  Pallas kernels  214 us (100%)
    pallas_call x1, Pallas kernels, back_call(): pl.pallas_call(partial(back_kernel, n_d, n_t, parts, heads), name='back',...  90.5 us
    pallas_call x1, Pallas kernels, front_call(): pl.pallas_call(partial(front_kernel, n_d, n_t, parts, heads, cond_at, bia...  77.3 us
    pallas_call x1, Pallas kernels, middle_call(): pl.pallas_call(partial(middle_kernel, n_d, n_t), name='middle', out_shape...  39.6 us
    pallas_call x1, Pallas kernels, finish_call(): pl.pallas_call(partial(finish_kernel, count, n_units, len(moved)), name='...  6.34 us

profile of v5, /device:TPU:0, one launch (start us, length us, event | category | flops | bytes accessed | tf_op | source)
XLA Modules:
  0.0 214.6 jit_solution(16466854042539865652)
XLA Ops:
  0.6 77.3 %front.1 = (bf16[4,512,768]{2,1,0:T(8,128)(2,1)}, bf16[4,576,512]{2,1,0:T(8,128)(2,1)}, bf16[4,192,512]{2,1,0:T(8,128)(2,1)}, f32[4,3,512]{2,1,0:T(4,128)}, bf16...) custom-call(bf16[512,768]{1,0:T(8,128)(2,1)} %bitcast.8, ...), custom_call_target="tpu_custom_call" | custom-call | flops 16106127360 | bytes 40000000 | tf_op jit(solution)/shard_map/front/pallas_call | solution.py:555
  78.0 39.6 %middle.1 = (bf16[512,768]{1,0:T(8,128)(2,1)}, f32[512,768]{1,0:T(8,128)}, bf16[4,192,512]{2,1,0:T(8,128)(2,1)}, f32[16,768]{1,0:T(8,128)}, bf16[4,2,96,384]{3,2...) custom-call(bf16[4,192,512]{2,1,0:T(8,128)(2,1)} %get-tuple-element., ...), custom_call_target="tpu_custom_call" | custom-call | flops 16911433728 | bytes 30000000 | tf_op jit(solution)/shard_map/middle/pallas_call | solution.py:870
  117.6 90.5 %back.1 = (f32[512,768]{1,0:T(8,128)}, f32[3,96,192]{2,1,0:T(8,128)}, f32[96,768]{1,0:T(8,128)}, f32[96,768]{1,0:T(8,128)}, f32[192,96]{1,0:T(8,128)}, /*index=5...) custom-call(bf16[4,192,512]{2,1,0:T(8,128)(2,1)} %get-tuple-element.66.dmix_ref, ...), custom_call_target="tpu_custom_call" | custom-call | flops 36238786560 | bytes 40000000 | tf_op jit(solution)/shard_map/back/pallas_call | solution.py:1282
  208.1 6.3 %finish.1 = (f32[128,4608]{1,0:T(8,128)}, f32[4608]{0:T(1024)}, f32[768]{0:T(1024)}, f32[768]{0:T(1024)}, f32[768]{0:T(1024)}, /*index=5*/f32[3072]{0:T(1024)}, ...) custom-call(f32[8,16,768]{2,1,0:T(8,128)} %get-tuple-element.79.tabl, ...), custom_call_target="tpu_custom_call" | custom-call | flops 10000000 | bytes 4000000 | tf_op jit(solution)/shard_map/finish/pallas_call | solution.py:1378

commit v6 on v5

--- a/solution.py
+++ b/solution.py
@@ -222,18 +222,21 @@
     return [pltpu.VMEM(shape, BF16) for shape in shapes]
 
 
-FRONT_PATHS = {"ul": "zyxc", "dl": "xzyc", "o": "xzyc", "uh": "zy", "dh": "zx"}
+FRONT_PATHS = {"ula": "zyxc", "ulb": "zxyc", "dla": "zxyc", "dlb": "zxyc", "o": "xyzc", "uh": "zy", "dh": "zx"}
 FRONT_PLAN = {
-    "pre": ("s dl",),
-    "0": ("s ul",),
-    "qz": ("a dl", "a ul",),
-    "n": ("s o",),
-    "g": ("a o",),
-    "p3": ("a dl", "a ul",),
-    "a0": ("s uh", "s dh",),
-    "a2": ("a o",),
-    "a5": ("a dl", "a ul", "a uh", "a dh",),
-    "end": ("a o", "a dl", "a ul", "a o", "a uh", "a dh",),
+    "pre": ("s ula",),
+    "qz": ("a ula", "s ulb", "s dlb", "s o",),
+    "X": ("s dla",),
+    "n": ("a ulb", "a dlb", "a o", "s uh",),
+    "g": ("a dla",),
+    "p1": ("s dh",),
+    "p3": ("a ula", "a ulb", "a dlb", "a o",),
+    "a0": ("a uh",),
+    "a1": ("a dla",),
+    "a3": ("a ula", "a dh",),
+    "a4": ("a ula", "a ulb", "a dlb",),
+    "a5": ("a ulb", "a dlb",),
+    "end": ("a uh", "a o", "a dla", "a o", "a dh", "a dla",),
 }
 BACK_DIMS = {"ul": "zy", "dl": "zx", "uh": "zyx", "dh": "zyx", "o": "czyx"}
 BACK_PATHS = {"ul": "yz", "dl": "xz", "uh": "xyz", "dh": "yxz", "o": "czxy"}
@@ -288,17 +291,21 @@
     greet(n_d, n_t)
     places = Places(n_d, n_t)
     flows = {}
-    for row, (name, dims, array, source) in enumerate(
+    split = 2 * cut // 3 // 128 * 128
+    whole, first_lanes, last_lanes = slice(None), slice(0, split), slice(split, cut)
+    for row, (name, dims, array, source, lanes) in enumerate(
         (
-            ("ul", "zyxc", w_ul, up_ref.at[:, low_half]),
-            ("dl", "zyxc", w_dl, down_ref.at[:, low_half]),
-            ("o", "zyxc", w_out, out_pack),
-            ("uh", "zy", w_uh, up_ref.at[:, high_half]),
-            ("dh", "zx", w_dh, down_ref.at[:, high_half]),
+            ("ula", "zyxc", w_ul, up_ref.at[:, first_lanes], first_lanes),
+            ("ulb", "zyxc", w_ul, up_ref.at[:, last_lanes], last_lanes),
+            ("dla", "zyxc", w_dl, down_ref.at[:, first_lanes], first_lanes),
+            ("dlb", "zyxc", w_dl, down_ref.at[:, last_lanes], last_lanes),
+            ("o", "zyxc", w_out, out_pack, whole),
+            ("uh", "zy", w_uh, up_ref.at[:, high_half], whole),
+            ("dh", "zx", w_dh, down_ref.at[:, high_half], whole),
         )
     ):
         flows[name] = Spread(
-            places, dims, "", FRONT_PATHS[name], array, source, s_w, r_w, 4 * row
+            places, dims, "", FRONT_PATHS[name], array, source, s_w, r_w, 4 * row, lanes
         )
     stage = dict.fromkeys(flows, 0)
 
@@ -588,7 +595,7 @@
             DMA((INNER - 1, no)), DMA((INNER - 1, no)),
             DMA((n_d - 1,)), DMA((n_d - 1,)), DMA((n_d - 1,)), DMA((n_d - 1,)),
             DMA((10,)),
-            DMA((20, steps)), DMA((20, steps)),
+            DMA((28, steps)), DMA((28, steps)),
             DMA((n_t - 1,)), DMA((n_t - 1,)),
         ],
         compiler_params=params(0),

time: 215 us -> 210 us (0.977)
  Pallas kernels: 214 us -> 209 us
    pallas_call x1, Pallas kernels: 77.3 us -> 69.4 us  [front_call(): pl.pallas_call(partial(front_kernel, n_d, n_t, parts, heads, cond_at, bia...]
    pallas_call x1, Pallas kernels: 39.6 us -> 42.9 us  [middle_call(): pl.pallas_call(partial(middle_kernel, n_d, n_t), name='middle', out_shape...]
where the time goes in v6:
time: 210 us
  Pallas kernels  209 us (100%)
    pallas_call x1, Pallas kernels, back_call(): pl.pallas_call(partial(back_kernel, n_d, n_t, parts, heads), name='back',...  90.3 us
    pallas_call x1, Pallas kernels, front_call(): pl.pallas_call(partial(front_kernel, n_d, n_t, parts, heads, cond_at, bia...  69.4 us
    pallas_call x1, Pallas kernels, middle_call(): pl.pallas_call(partial(middle_kernel, n_d, n_t), name='middle', out_shape...  42.9 us
    pallas_call x1, Pallas kernels, finish_call(): pl.pallas_call(partial(finish_kernel, count, n_units, len(moved)), name='...  6.34 us

profile of v6, /device:TPU:0, one launch (start us, length us, event | category | flops | bytes accessed | tf_op | source)
XLA Modules:
  0.0 209.7 jit_solution(9388620481810684941)
XLA Ops:
  0.6 69.4 %front.1 = (bf16[4,512,768]{2,1,0:T(8,128)(2,1)}, bf16[4,576,512]{2,1,0:T(8,128)(2,1)}, bf16[4,192,512]{2,1,0:T(8,128)(2,1)}, f32[4,3,512]{2,1,0:T(4,128)}, bf16...) custom-call(bf16[512,768]{1,0:T(8,128)(2,1)} %bitcast.8, ...), custom_call_target="tpu_custom_call" | custom-call | flops 16106127360 | bytes 40000000 | tf_op jit(solution)/shard_map/front/pallas_call | solution.py:562
  70.0 42.9 %middle.1 = (bf16[512,768]{1,0:T(8,128)(2,1)}, f32[512,768]{1,0:T(8,128)}, bf16[4,192,512]{2,1,0:T(8,128)(2,1)}, f32[16,768]{1,0:T(8,128)}, bf16[4,2,96,384]{3,2...) custom-call(bf16[4,192,512]{2,1,0:T(8,128)(2,1)} %get-tuple-element., ...), custom_call_target="tpu_custom_call" | custom-call | flops 16911433728 | bytes 30000000 | tf_op jit(solution)/shard_map/middle/pallas_call | solution.py:877
  112.9 90.3 %back.1 = (f32[512,768]{1,0:T(8,128)}, f32[3,96,192]{2,1,0:T(8,128)}, f32[96,768]{1,0:T(8,128)}, f32[96,768]{1,0:T(8,128)}, f32[192,96]{1,0:T(8,128)}, /*index=5...) custom-call(bf16[4,192,512]{2,1,0:T(8,128)(2,1)} %get-tuple-element.66.dmix_ref, ...), custom_call_target="tpu_custom_call" | custom-call | flops 36238786560 | bytes 40000000 | tf_op jit(solution)/shard_map/back/pallas_call | solution.py:1289
  203.2 6.3 %finish.1 = (f32[128,4608]{1,0:T(8,128)}, f32[4608]{0:T(1024)}, f32[768]{0:T(1024)}, f32[768]{0:T(1024)}, f32[768]{0:T(1024)}, /*index=5*/f32[3072]{0:T(1024)}, ...) custom-call(f32[8,16,768]{2,1,0:T(8,128)} %get-tuple-element.79.tabl, ...), custom_call_target="tpu_custom_call" | custom-call | flops 10000000 | bytes 4000000 | tf_op jit(solution)/shard_map/finish/pallas_call | solution.py:1385

commit v7 on v6

--- a/solution.py
+++ b/solution.py
@@ -70,7 +70,7 @@
     return d, t, d // INNER, lax.rem(d, INNER), t // CORES, lax.rem(t, CORES)
 
 
-def greet(n_d, n_t):
+def greet(n_d, n_t, between=None):
     d, t = lax.axis_index("dp"), lax.axis_index("tensor")
     barrier = pltpu.get_barrier_semaphore()
     for r in range(1, n_t):
@@ -81,6 +81,8 @@
         pl.semaphore_signal(
             barrier, 1, device_id=(lax.rem(d + r, n_d), t), device_id_type=MESH
         )
+    if between is not None:
+        between()
     pl.semaphore_wait(barrier, n_t - 1 + n_d - 1)
 
 
@@ -276,19 +278,21 @@
     half = HEAD_DIM // 2
     cut = w_ul.shape[5]
     low_half, high_half = slice(0, cut), slice(cut, 2 * cut)
-    for j in range(3):
-        w_pack[:, j * width : (j + 1) * width] = qkv_ref[j]
-    out_pack[:, :width] = outw_ref[...].T
-    small_ref[...] = jnp.zeros_like(small_ref)
-    at = 0
-    for ref in (gain1_ref, gain2_ref, bdown_ref, bup_ref):
-        small_ref[:, at : at + ref.shape[0]] = ref[...].astype(F32).reshape(1, -1)
-        at += ref.shape[0]
-    small_ref[:, cond_at : cond_at + cond_in.shape[1]] = cond_in[...].astype(F32)
-    small_ref[:, bias_at : bias_at + ada_b_ref.shape[0]] = ada_b_ref[...].astype(F32).reshape(1, -1)
-    if out_pack.shape[1] > width:
-        out_pack[:, width:] = jnp.zeros((out_pack.shape[0], out_pack.shape[1] - width), BF16)
-    greet(n_d, n_t)
+    def pack():
+        for j in range(3):
+            w_pack[:, j * width : (j + 1) * width] = qkv_ref[j]
+        out_pack[:, :width] = outw_ref[...].T
+        small_ref[...] = jnp.zeros_like(small_ref)
+        at = 0
+        for ref in (gain1_ref, gain2_ref, bdown_ref, bup_ref):
+            small_ref[:, at : at + ref.shape[0]] = ref[...].astype(F32).reshape(1, -1)
+            at += ref.shape[0]
+        small_ref[:, cond_at : cond_at + cond_in.shape[1]] = cond_in[...].astype(F32)
+        small_ref[:, bias_at : bias_at + ada_b_ref.shape[0]] = ada_b_ref[...].astype(F32).reshape(1, -1)
+        if out_pack.shape[1] > width:
+            out_pack[:, width:] = jnp.zeros((out_pack.shape[0], out_pack.shape[1] - width), BF16)
+
+    greet(n_d, n_t, pack)
     places = Places(n_d, n_t)
     flows = {}
     split = 2 * cut // 3 // 128 * 128

time: 210 us -> 210 us (level)
  no operation moved by 1% of the time
where the time goes in v7:
time: 210 us
  Pallas kernels  209 us (100%)
    pallas_call x1, Pallas kernels, back_call(): pl.pallas_call(partial(back_kernel, n_d, n_t, parts, heads), name='back',...  90.3 us
    pallas_call x1, Pallas kernels, front_call(): pl.pallas_call(partial(front_kernel, n_d, n_t, parts, heads, cond_at, bia...  69.2 us
    pallas_call x1, Pallas kernels, middle_call(): pl.pallas_call(partial(middle_kernel, n_d, n_t), name='middle', out_shape...  42.9 us
    pallas_call x1, Pallas kernels, finish_call(): pl.pallas_call(partial(finish_kernel, count, n_units, len(moved)), name='...  6.34 us

profile of v7, /device:TPU:0, one launch (start us, length us, event | category | flops | bytes accessed | tf_op | source)
XLA Modules:
  0.0 209.6 jit_solution(243894208408098229)
XLA Ops:
  0.6 69.2 %front.1 = (bf16[4,512,768]{2,1,0:T(8,128)(2,1)}, bf16[4,576,512]{2,1,0:T(8,128)(2,1)}, bf16[4,192,512]{2,1,0:T(8,128)(2,1)}, f32[4,3,512]{2,1,0:T(4,128)}, bf16...) custom-call(bf16[512,768]{1,0:T(8,128)(2,1)} %bitcast.8, ...), custom_call_target="tpu_custom_call" | custom-call | flops 16106127360 | bytes 40000000 | tf_op jit(solution)/shard_map/front/pallas_call | solution.py:566
  69.9 42.9 %middle.1 = (bf16[512,768]{1,0:T(8,128)(2,1)}, f32[512,768]{1,0:T(8,128)}, bf16[4,192,512]{2,1,0:T(8,128)(2,1)}, f32[16,768]{1,0:T(8,128)}, bf16[4,2,96,384]{3,2...) custom-call(bf16[4,192,512]{2,1,0:T(8,128)(2,1)} %get-tuple-element., ...), custom_call_target="tpu_custom_call" | custom-call | flops 16911433728 | bytes 30000000 | tf_op jit(solution)/shard_map/middle/pallas_call | solution.py:881
  112.8 90.3 %back.1 = (f32[512,768]{1,0:T(8,128)}, f32[3,96,192]{2,1,0:T(8,128)}, f32[96,768]{1,0:T(8,128)}, f32[96,768]{1,0:T(8,128)}, f32[192,96]{1,0:T(8,128)}, /*index=5...) custom-call(bf16[4,192,512]{2,1,0:T(8,128)(2,1)} %get-tuple-element.66.dmix_ref, ...), custom_call_target="tpu_custom_call" | custom-call | flops 36238786560 | bytes 40000000 | tf_op jit(solution)/shard_map/back/pallas_call | solution.py:1293
  203.1 6.3 %finish.1 = (f32[128,4608]{1,0:T(8,128)}, f32[4608]{0:T(1024)}, f32[768]{0:T(1024)}, f32[768]{0:T(1024)}, f32[768]{0:T(1024)}, /*index=5*/f32[3072]{0:T(1024)}, ...) custom-call(f32[8,16,768]{2,1,0:T(8,128)} %get-tuple-element.79.tabl, ...), custom_call_target="tpu_custom_call" | custom-call | flops 10000000 | bytes 4000000 | tf_op jit(solution)/shard_map/finish/pallas_call | solution.py:1389
